TPU v7x, 32 devices: a whole 2x2x4 slice. The times are simulated.
32 devices in a mesh: dp: 4 (over x, core), fsdp: 8 (over z, y).
Axes of the slice: x: 2, y: 2, z: 4, core: 2. Of those that a mesh axis runs over, the one named last changes fastest.
Arguments:
- inputs: bfloat16 [32768, 1024], P(('dp', 'fsdp')), may hold values from -6 to 6
- lengths: int32 [32], P(('dp', 'fsdp')), may hold values from 256 to 1024, as said below
- query_weight: bfloat16 [1024, 1024], P(None, ('dp', 'fsdp')), may hold values from -0.1875 to 0.1875
- key_weight: bfloat16 [1024, 1024], P(None, ('dp', 'fsdp')), may hold values from -0.1875 to 0.1875
- value_weight: bfloat16 [1024, 1024], P(None, ('dp', 'fsdp')), may hold values from -0.1875 to 0.1875
- gate_weight: bfloat16 [1024, 1024], P(None, ('dp', 'fsdp')), may hold values from -0.1875 to 0.1875
- out_weight: bfloat16 [1024, 1024], P(None, ('dp', 'fsdp')), may hold values from -0.1875 to 0.1875
- first_weight: bfloat16 [1024, 2816], P(None, ('dp', 'fsdp')), may hold values from -0.1875 to 0.1875
- second_weight: bfloat16 [1024, 2816], P(None, ('dp', 'fsdp')), may hold values from -0.1875 to 0.1875
- down_weight: bfloat16 [2816, 1024], P(None, ('dp', 'fsdp')), may hold values from -0.109375 to 0.109375
- cotangent: bfloat16 [32768, 1024], P(('dp', 'fsdp')), may hold values from -6 to 6
Outputs:
- outputs: bfloat16 [32768, 1024], P(('dp', 'fsdp'))
- input_grad: float32 [32768, 1024], P(('dp', 'fsdp'))
- query_grad: float32 [1024, 1024], P(None, ('dp', 'fsdp'))
- key_grad: float32 [1024, 1024], P(None, ('dp', 'fsdp'))
- value_grad: float32 [1024, 1024], P(None, ('dp', 'fsdp'))
- gate_grad: float32 [1024, 1024], P(None, ('dp', 'fsdp'))
- out_grad: float32 [1024, 1024], P(None, ('dp', 'fsdp'))
- first_grad: float32 [1024, 2816], P(None, ('dp', 'fsdp'))
- second_grad: float32 [1024, 2816], P(None, ('dp', 'fsdp'))
- down_grad: float32 [2816, 1024], P(None, ('dp', 'fsdp'))
Inputs may be any that keep to these rules, and one draw needn't show every extreme that they name: `lengths`: one length for each sequence; at least one sequence fills all 1024 slots.
All inputs are finite; a program needn't handle non-finite values.
Results may differ from a plain program's by a relative error of at most 0.014.
Values may be sent and summed in bfloat16 or wider, within the bound.
No kernel may reach another device: no remote copies, remote signals or barrier semaphores. Data moves between devices by JAX's collectives and lax.ppermute only.
A program may use at most 320 MiB of HBM per device.

v0:
```python
import math

import jax
import jax.numpy as jnp
from jax import lax
from jax.sharding import PartitionSpec as P

D = 1024
HEADS = 8
HEAD = 128
SPAN = 256
LAYER = 12
LAYERS = 24


NORM_EPS = 1e-06


def simple_norm(values):
    return values * lax.rsqrt(jnp.mean(values * values, axis=-1, keepdims=True) + NORM_EPS)


def norm_back(values, upstream):
    return jax.vjp(simple_norm, values)[1](upstream)[0]


def silu_back(values, upstream):
    return jax.vjp(jax.nn.silu, values)[1](upstream)[0]


def forward_dot(left, right):
    return jnp.dot(left, right, preferred_element_type=jnp.float32)


def back_dot(left, right):
    return lax.dot_general(
        left, right, (((1,), (1,)), ((), ())), preferred_element_type=jnp.float32
    )


def weight_dot(left, right):
    return lax.dot_general(
        left, right, (((0,), (0,)), ((), ())), preferred_element_type=jnp.float32
    )


def group_columns(lows, shards):
    tokens = lows[0].shape[0]
    width = lows[0].shape[1] // shards
    stacked = jnp.stack([matrix.reshape(tokens, shards, width) for matrix in lows], axis=2)
    return stacked.reshape(tokens, shards * len(lows) * width)


def split_rows(summed, count):
    width = summed.shape[0] // count
    pieces = summed.reshape(count, width, summed.shape[1])
    return tuple((jnp.transpose(pieces[index]) for index in range(count)))


def make_tables(length):
    head_index = jnp.arange(HEADS, dtype=jnp.float32)
    slopes = jnp.exp2(-8.0 * (head_index + 1.0) / HEADS) * (1.0 - LAYER / LAYERS)
    offsets = jnp.arange(SPAN, dtype=jnp.float32)
    distance = offsets[:, None] - offsets[None, :]
    within = jnp.where(
        distance[None] >= 0.0,
        jnp.exp(-slopes[:, None, None] * jnp.maximum(distance, 0.0)[None]),
        0.0,
    )
    query_decay = jnp.exp(-(offsets[:, None] + 1.0) * slopes[None, :])
    key_decay = jnp.exp(-(SPAN - 1.0 - offsets[:, None]) * slopes[None, :])
    block_decay = jnp.exp(-SPAN * slopes)
    places = jnp.arange(length, dtype=jnp.float32)
    frequency = jnp.exp(-jnp.arange(HEAD, dtype=jnp.float32) * (math.log(10000.0) / HEAD))
    angles = places[:, None] * frequency[None, :]
    return (jnp.cos(angles), jnp.sin(angles), within, query_decay, key_decay, block_decay)


def rotate(values, cosine_table, sine_table):
    split_heads = values.reshape(values.shape[0], HEADS, HEAD)
    return jnp.concatenate(
        [split_heads * cosine_table[:, None, :], split_heads * sine_table[:, None, :]], axis=-1
    )


def unrotate(grads, cosine_table, sine_table):
    joined = (
        grads[..., :HEAD] * cosine_table[:, None, :] + grads[..., HEAD:] * sine_table[:, None, :]
    )
    return joined.reshape(grads.shape[0], D)


def lightning_forward(query_rot, key_rot, values, tables):
    cosine_table, sine_table, within, query_decay, key_decay, block_decay = tables
    blocks = query_rot.shape[0] // SPAN
    query_blocks = query_rot.reshape(blocks, SPAN, HEADS, 2 * HEAD)
    key_blocks = key_rot.reshape(blocks, SPAN, HEADS, 2 * HEAD)
    value_blocks = values.reshape(blocks, SPAN, HEADS, HEAD)
    scores = jnp.einsum(
        "cthf,cshf->chts", query_blocks, key_blocks, preferred_element_type=jnp.float32
    )
    weights_low = (scores * within[None]).astype(jnp.bfloat16)
    local_part = jnp.einsum(
        "chts,cshe->cthe", weights_low, value_blocks, preferred_element_type=jnp.float32
    )
    query_scaled = (query_blocks * query_decay[None, :, :, None]).astype(jnp.bfloat16)
    key_scaled = (key_blocks * key_decay[None, :, :, None]).astype(jnp.bfloat16)
    updates = jnp.einsum(
        "cshf,cshe->chfe", key_scaled, value_blocks, preferred_element_type=jnp.float32
    )

    def advance(state, update):
        return (block_decay[:, None, None] * state + update, state)

    unused, states = lax.scan(advance, jnp.zeros(updates.shape[1:], jnp.float32), updates)
    states_low = states.astype(jnp.bfloat16)
    carried = jnp.einsum(
        "cthf,chfe->cthe", query_scaled, states_low, preferred_element_type=jnp.float32
    )
    attended = (local_part + carried).reshape(query_rot.shape[0], D)
    return (attended, (weights_low, query_scaled, key_scaled, states_low))


def lightning_backward(upstream, query_rot, key_rot, values, saved, tables):
    cosine_table, sine_table, within, query_decay, key_decay, block_decay = tables
    weights_low, query_scaled, key_scaled, states_low = saved
    length = query_rot.shape[0]
    blocks = length // SPAN
    query_blocks = query_rot.reshape(blocks, SPAN, HEADS, 2 * HEAD)
    key_blocks = key_rot.reshape(blocks, SPAN, HEADS, 2 * HEAD)
    value_blocks = values.reshape(blocks, SPAN, HEADS, HEAD)
    upstream_blocks = upstream.reshape(blocks, SPAN, HEADS, HEAD)
    weight_grad = jnp.einsum(
        "cthe,cshe->chts", upstream_blocks, value_blocks, preferred_element_type=jnp.float32
    )
    score_low = (weight_grad * within[None]).astype(jnp.bfloat16)
    query_part = jnp.einsum(
        "chts,cshf->cthf", score_low, key_blocks, preferred_element_type=jnp.float32
    )
    key_part = jnp.einsum(
        "chts,cthf->cshf", score_low, query_blocks, preferred_element_type=jnp.float32
    )
    value_part = jnp.einsum(
        "chts,cthe->cshe", weights_low, upstream_blocks, preferred_element_type=jnp.float32
    )
    scaled_grad = jnp.einsum(
        "cthe,chfe->cthf", upstream_blocks, states_low, preferred_element_type=jnp.float32
    )
    query_part = query_part + scaled_grad * query_decay[None, :, :, None]
    state_terms = jnp.einsum(
        "cthf,cthe->chfe", query_scaled, upstream_blocks, preferred_element_type=jnp.float32
    )

    def retreat(later, term):
        return (
            (block_decay[:, None, None] * later.astype(jnp.float32) + term).astype(jnp.bfloat16),
            later,
        )

    unused, update_grads = lax.scan(
        retreat, jnp.zeros(state_terms.shape[1:], jnp.bfloat16), state_terms, reverse=True
    )
    key_scaled_grad = jnp.einsum(
        "cshe,chfe->cshf", value_blocks, update_grads, preferred_element_type=jnp.float32
    )
    key_part = key_part + key_scaled_grad * key_decay[None, :, :, None]
    value_part = value_part + jnp.einsum(
        "cshf,chfe->cshe", key_scaled, update_grads, preferred_element_type=jnp.float32
    )
    return (
        query_part.reshape(length, HEADS, 2 * HEAD),
        key_part.reshape(length, HEADS, 2 * HEAD),
        value_part.reshape(length, D),
    )


def attention_forward(inputs_f, mask, weights, tables):
    query_weight, key_weight, value_weight, gate_weight, out_weight = weights
    normed = simple_norm(inputs_f).astype(jnp.bfloat16)
    query_pre = forward_dot(normed, query_weight)
    key_pre = forward_dot(normed, key_weight)
    value_pre = forward_dot(normed, value_weight)
    gate_pre = forward_dot(normed, gate_weight)
    query_rot = rotate(jax.nn.silu(query_pre) * mask, tables[0], tables[1]).astype(jnp.bfloat16)
    key_rot = rotate(jax.nn.silu(key_pre) * mask, tables[0], tables[1]).astype(jnp.bfloat16)
    values = (value_pre * mask).astype(jnp.bfloat16)
    attended, saved = lightning_forward(query_rot, key_rot, values, tables)
    attended_norm = simple_norm(attended)
    gated = (attended_norm * gate_pre * mask).astype(jnp.bfloat16)
    mixed = inputs_f + forward_dot(gated, out_weight)
    kept = (
        normed,
        query_pre,
        key_pre,
        gate_pre,
        values,
        query_rot,
        key_rot,
        attended,
        attended_norm,
        gated,
        saved,
    )
    return (mixed, kept)


def glu_forward(mixed, mask, weights):
    first_weight, second_weight, down_weight = weights
    normed_two = simple_norm(mixed).astype(jnp.bfloat16)
    first = forward_dot(normed_two, first_weight)
    second = forward_dot(normed_two, second_weight)
    product_low = (first * second * mask).astype(jnp.bfloat16)
    result = mixed + forward_dot(product_low, down_weight)
    return (result, (normed_two, first, second, product_low))


def per_device(
    inputs,
    lengths,
    query_weight,
    key_weight,
    value_weight,
    gate_weight,
    out_weight,
    first_weight,
    second_weight,
    down_weight,
    cotangent,
):
    shards = lax.axis_size(("dp", "fsdp"))
    attn_full = (
        lax.all_gather(query_weight, ("dp", "fsdp"), axis=1, tiled=True),
        lax.all_gather(key_weight, ("dp", "fsdp"), axis=1, tiled=True),
        lax.all_gather(value_weight, ("dp", "fsdp"), axis=1, tiled=True),
        lax.all_gather(gate_weight, ("dp", "fsdp"), axis=1, tiled=True),
        lax.all_gather(out_weight, ("dp", "fsdp"), axis=1, tiled=True),
    )
    inputs_f = inputs.astype(jnp.float32)
    length = inputs.shape[0]
    mask = (lax.iota(jnp.int32, length) < lengths[0]).astype(jnp.float32)[:, None]
    tables = make_tables(length)
    mixed, attn_kept = attention_forward(inputs_f, mask, attn_full, tables)
    glu_full = (
        lax.all_gather(first_weight, ("dp", "fsdp"), axis=1, tiled=True),
        lax.all_gather(second_weight, ("dp", "fsdp"), axis=1, tiled=True),
        lax.all_gather(down_weight, ("dp", "fsdp"), axis=1, tiled=True),
    )
    result, glu_kept = glu_forward(mixed, mask, glu_full)
    glu_back = (
        lax.all_gather(first_weight, ("dp", "fsdp"), axis=1, tiled=True),
        lax.all_gather(second_weight, ("dp", "fsdp"), axis=1, tiled=True),
        lax.all_gather(down_weight, ("dp", "fsdp"), axis=1, tiled=True),
    )
    first_back, second_back, down_back = glu_back
    normed_two, first, second, product_low = glu_kept
    product_grad = back_dot(cotangent, down_back)
    first_low = (product_grad * second * mask).astype(jnp.bfloat16)
    second_low = (product_grad * first * mask).astype(jnp.bfloat16)
    normed_two_grad = back_dot(first_low, first_back) + back_dot(second_low, second_back)
    pair_left = group_columns((first_low, second_low), shards)
    pair_sums = lax.psum_scatter(
        weight_dot(pair_left, normed_two), ("dp", "fsdp"), scatter_dimension=0, tiled=True
    )
    first_sum, second_sum = split_rows(pair_sums, 2)
    down_sums = lax.psum_scatter(
        weight_dot(cotangent, product_low), ("dp", "fsdp"), scatter_dimension=0, tiled=True
    )
    down_sum = jnp.transpose(down_sums)
    mixed_grad = cotangent.astype(jnp.float32) + norm_back(mixed, normed_two_grad)
    attn_back = (
        lax.all_gather(query_weight, ("dp", "fsdp"), axis=1, tiled=True),
        lax.all_gather(key_weight, ("dp", "fsdp"), axis=1, tiled=True),
        lax.all_gather(value_weight, ("dp", "fsdp"), axis=1, tiled=True),
        lax.all_gather(gate_weight, ("dp", "fsdp"), axis=1, tiled=True),
        lax.all_gather(out_weight, ("dp", "fsdp"), axis=1, tiled=True),
    )
    query_back, key_back, value_back, gate_back, out_back = attn_back
    (
        normed,
        query_pre,
        key_pre,
        gate_pre,
        values,
        query_rot,
        key_rot,
        attended,
        attended_norm,
        gated,
        saved,
    ) = attn_kept
    mixed_low = mixed_grad.astype(jnp.bfloat16)
    gated_grad = back_dot(mixed_low, out_back)
    gate_low = (gated_grad * attended_norm * mask).astype(jnp.bfloat16)
    attended_low = norm_back(attended, gated_grad * gate_pre * mask).astype(jnp.bfloat16)
    query_rot_grad, key_rot_grad, values_grad = lightning_backward(
        attended_low, query_rot, key_rot, values, saved, tables
    )
    query_low = silu_back(query_pre, unrotate(query_rot_grad, tables[0], tables[1]) * mask).astype(
        jnp.bfloat16
    )
    key_low = silu_back(key_pre, unrotate(key_rot_grad, tables[0], tables[1]) * mask).astype(
        jnp.bfloat16
    )
    value_low = (values_grad * mask).astype(jnp.bfloat16)
    normed_grad = (
        back_dot(query_low, query_back)
        + back_dot(key_low, key_back)
        + back_dot(value_low, value_back)
        + back_dot(gate_low, gate_back)
    )
    attn_left = group_columns((query_low, key_low, value_low, gate_low, mixed_low), shards)
    width = query_weight.shape[1]
    piece = attn_left
    owners = 5 * width * lax.axis_size(("dp", "fsdp")) // (5 * width)
    piece = piece.reshape(length, owners, 5, width)
    front = weight_dot(piece[:, :, :4].reshape(length, owners * 4 * width), normed).reshape(
        owners, 4, width, D
    )
    rear = weight_dot(piece[:, :, 4].reshape(length, owners * width), gated).reshape(
        owners, 1, width, D
    )
    attn_sums = lax.psum_scatter(
        jnp.concatenate([front, rear], axis=1).reshape(
            5 * width * lax.axis_size(("dp", "fsdp")), D
        ),
        ("dp", "fsdp"),
        scatter_dimension=0,
        tiled=True,
    )
    query_sum, key_sum, value_sum, gate_sum, out_sum = split_rows(attn_sums, 5)
    input_grad = mixed_grad + norm_back(inputs_f, normed_grad)
    return (
        result.astype(jnp.bfloat16),
        input_grad,
        query_sum,
        key_sum,
        value_sum,
        gate_sum,
        out_sum,
        first_sum,
        second_sum,
        down_sum,
    )


def solution(mesh):
    return jax.shard_map(
        per_device,
        mesh=mesh,
        in_specs=(
            P(("dp", "fsdp"), None),
            P(("dp", "fsdp")),
            P(None, ("dp", "fsdp")),
            P(None, ("dp", "fsdp")),
            P(None, ("dp", "fsdp")),
            P(None, ("dp", "fsdp")),
            P(None, ("dp", "fsdp")),
            P(None, ("dp", "fsdp")),
            P(None, ("dp", "fsdp")),
            P(None, ("dp", "fsdp")),
            P(("dp", "fsdp"), None),
        ),
        out_specs=(
            P(("dp", "fsdp"), None),
            P(("dp", "fsdp"), None),
            P(None, ("dp", "fsdp")),
            P(None, ("dp", "fsdp")),
            P(None, ("dp", "fsdp")),
            P(None, ("dp", "fsdp")),
            P(None, ("dp", "fsdp")),
            P(None, ("dp", "fsdp")),
            P(None, ("dp", "fsdp")),
            P(None, ("dp", "fsdp")),
        ),
        check_vma=False,
    )
```

profile of v0, /device:TPU:0, one launch (start us, length us, event | category | flops | bytes accessed | tf_op | source)
XLA Modules:
  0.0 1905.5 jit_solution(14923088616747733090)
XLA Ops:
  28.7 41.4 %all-gather.11.cloned.1.call-done = bf16[1024,1024]{0,1:T(8,128)(2,1)} async-done(((bf16[1024,32]{0,1:T(8,128)(2,1)}), bf16[1024,1024]{0,1:T(8,128)(2,1)}) %all-gather.11.cloned.1.call-update) | async-done | bytes 2097168 | tf_op jit(solution)/shard_map/all_gather | solution.py:232
  76.1 52.2 %all-gather.13.cloned.1.call-done = bf16[1024,1024]{0,1:T(8,128)(2,1)} async-done(((bf16[1024,32]{0,1:T(8,128)(2,1)}), bf16[1024,1024]{0,1:T(8,128)(2,1)}) %all-gather.13.cloned.1.call-update) | async-done | bytes 2097168 | tf_op jit(solution)/shard_map/all_gather | solution.py:233
  142.0 44.6 %all-gather.9.cloned.1.call-done = bf16[1024,1024]{0,1:T(8,128)(2,1)} async-done(((bf16[1024,32]{0,1:T(8,128)(2,1)}), bf16[1024,1024]{0,1:T(8,128)(2,1)}) %all-gather.9.cloned.1.call-update) | async-done | bytes 2097168 | tf_op jit(solution)/shard_map/all_gather | solution.py:234
  227.8 16.8 all-gather.15.cloned.1.call-done
  253.3 49.3 %all-gather.17.cloned.1.call-done = bf16[1024,1024]{0,1:T(8,128)(2,1)} async-done(((bf16[1024,32]{0,1:T(8,128)(2,1)}), bf16[1024,1024]{0,1:T(8,128)(2,1)}) %all-gather.17.cloned.1.call-update) | async-done | bytes 2097168 | tf_op jit(solution)/shard_map/all_gather | solution.py:236
  309.9 61.8 %all-gather.19.cloned.1.call-done = bf16[1024,2816]{0,1:T(8,128)(2,1)} async-done(((bf16[1024,88]{0,1:T(8,128)(2,1)}), bf16[1024,2816]{0,1:T(8,128)(2,1)}) %all-gather.19.cloned.1.call-update) | async-done | bytes 5767184 | tf_op jit(solution)/shard_map/all_gather | solution.py:244
  371.7 11.5 fusion.65
  383.2 57.4 %all-gather.21.cloned.1.call-done = bf16[1024,2816]{0,1:T(8,128)(2,1)} async-done(((bf16[1024,88]{0,1:T(8,128)(2,1)}), bf16[1024,2816]{0,1:T(8,128)(2,1)}) %all-gather.21.cloned.1.call-update) | async-done | bytes 5767184 | tf_op jit(solution)/shard_map/all_gather | solution.py:245
  440.6 11.9 fusion.66
  452.5 57.1 %all-gather.23.cloned.1.call-done = bf16[2816,1024]{0,1:T(8,128)(2,1)} async-done(((bf16[2816,32]{0,1:T(8,128)(2,1)}), bf16[2816,1024]{0,1:T(8,128)(2,1)}) %all-gather.23.cloned.1.call-update) | async-done | bytes 5767184 | tf_op jit(solution)/shard_map/all_gather | solution.py:246
  509.5 16.3 multiply_convert_fusion
  525.8 11.4 fusion.67
  537.3 11.4 multiply_reduce_fusion
  610.4 11.3 fusion.7
  621.6 11.7 copy.131
  637.9 11.7 copy.125
  691.1 12.2 fusion.5
  740.5 19.3 %fusion.71 = f32[5632,1024]{1,0:T(8,128)} fusion(bf16[1024,5632]{0,1:T(8,128)(2,1)} %bitcast.190, bf16[1024,1024]{0,1:T(8,128)(2,1)S(1)} %copy-done.44), kind=kOutput, calls=%fused_computation.153 | convolution fusion | flops 11811160064 | bytes 36700160 | tf_op jit(solution)/shard_map/dot_general | solution.py:42
  759.9 12.0 convolution_bitcast_fusion
  771.9 11.9 copy.161
  789.1 11.5 add_convert_fusion
  831.0 325.1 %reduce-scatter.6.cloned.1.call-done = f32[160,1024]{1,0:T(8,128)} async-done(((f32[5120,1024]{1,0:T(8,128)}), f32[160,1024]{1,0:T(8,128)}) %reduce-scatter.6.cloned.1.call-update) | async-done | bytes 655376 | tf_op jit(solution)/shard_map/reduce_scatter | solution.py:322
  1158.2 488.2 %reduce-scatter.8.cloned.1.call-done = f32[176,1024]{1,0:T(8,128)} async-done(((f32[5632,1024]{1,0:T(8,128)}), f32[176,1024]{1,0:T(8,128)}) %reduce-scatter.8.cloned.1.call-update) | async-done | bytes 720912 | tf_op jit(solution)/shard_map/reduce_scatter | solution.py:261
  1648.4 250.4 %reduce-scatter.10.cloned.1.call-done = f32[32,2816]{1,0:T(8,128)} async-done(((f32[1024,2816]{1,0:T(8,128)}), f32[32,2816]{1,0:T(8,128)}) %reduce-scatter.10.cloned.1.call-update) | async-done | bytes 360464
  (238 shorter events, 300.8 us)
Async XLA Ops:
  7.2 62.9 %all-gather.11.cloned.1.call-start = ((), (), s32[]{:S(2)}) async-start(), calls=%async_computation.4 | async-start | bytes 2162688 | tf_op jit(solution)/shard_map/all_gather | solution.py:232
  7.9 120.4 %all-gather.13.cloned.1.call-start = ((), (), s32[]{:S(2)}) async-start(), calls=%async_computation.5 | async-start | bytes 2162688 | tf_op jit(solution)/shard_map/all_gather | solution.py:233
  8.7 177.9 %all-gather.9.cloned.1.call-start = ((), (), s32[]{:S(2)}) async-start(), calls=%async_computation.3 | async-start | bytes 2162688 | tf_op jit(solution)/shard_map/all_gather | solution.py:234
  9.4 235.2 %all-gather.15.cloned.1.call-start = ((), (), s32[]{:S(2)}) async-start(), calls=%async_computation.6 | async-start | bytes 2162688 | tf_op jit(solution)/shard_map/all_gather | solution.py:235
  10.0 292.7 %all-gather.17.cloned.1.call-start = ((), (), s32[]{:S(2)}) async-start(), calls=%async_computation.7 | async-start | bytes 2162688 | tf_op jit(solution)/shard_map/all_gather | solution.py:236
  10.6 361.1 %all-gather.19.cloned.1.call-start = ((), (), s32[]{:S(2)}) async-start(), calls=%async_computation.8 | async-start | bytes 5947392 | tf_op jit(solution)/shard_map/all_gather | solution.py:244
  11.1 429.5 %all-gather.21.cloned.1.call-start = ((), (), s32[]{:S(2)}) async-start(), calls=%async_computation.9 | async-start | bytes 5947392 | tf_op jit(solution)/shard_map/all_gather | solution.py:245
  11.9 497.7 %all-gather.23.cloned.1.call-start = ((), (), s32[]{:S(2)}) async-start(), calls=%async_computation.10 | async-start | bytes 5947392 | tf_op jit(solution)/shard_map/all_gather | solution.py:246
  12.6 1143.5 %reduce-scatter.6.cloned.1.call-start = ((), (), s32[]{:S(2)}) async-start(), calls=%async_computation.11 | async-start | bytes 21626880 | tf_op jit(solution)/shard_map/reduce_scatter | solution.py:322
  15.8 286.9 %copy-start.7 = (bf16[1024,1024]{0,1:T(8,128)(2,1)}, bf16[1024,1024]{0,1:T(8,128)(2,1)S(1)}, u32[]{:S(2)}) copy-start(bf16[1024,1024]{0,1:T(8,128)(2,1)S(1)} %copy.103) | copy-start | bytes 6291460
  16.3 228.3 %copy-start.48 = (f32[1024]{0:T(1024)}, f32[1024]{0:T(1024)S(1)}, u32[]{:S(2)}) copy-start(f32[1024]{0:T(1024)S(1)} %fusion.62) | copy-start | bytes 12292
  309.9 61.8 %copy-start.43 = (bf16[1024,1024]{0,1:T(8,128)(2,1)}, bf16[1024,1024]{0,1:T(8,128)(2,1)S(1)}, u32[]{:S(2)}) copy-start(bf16[1024,1024]{0,1:T(8,128)(2,1)S(1)} %multiply_convert_fusion.9) | copy-start | bytes 6291460
  383.2 126.3 %copy-start.30 = (bf16[1024,1024]{1,0:T(8,128)(2,1)S(1)}, bf16[1024,1024]{1,0:T(8,128)(2,1)}, u32[]{:S(2)}) copy-start(bf16[1024,1024]{1,0:T(8,128)(2,1)} %param.25) | copy-start | bytes 6291460
  525.8 11.4 copy-start.6
  525.8 11.4 copy-start.24
  537.3 11.5 copy-start.34
  606.5 26.9 %slice-start = ((s8[8388608]{0:T(1024)(128)(4,1)}), s8[4194304]{0:T(1024)(128)(4,1)S(1)}, s32[]{:S(2)}) async-start(s8[8388608]{0:T(1024)(128)(4,1)} %bitcast.176), calls=%async_computation.14 | async-start | bytes 8388608
  610.4 23.0 %slice-start.1 = ((s8[8388608]{0:T(1024)(128)(4,1)}), s8[4194304]{0:T(1024)(128)(4,1)S(1)}, s32[]{:S(2)}) async-start(s8[8388608]{0:T(1024)(128)(4,1)} %bitcast.176), calls=%async_computation.15 | async-start | bytes 8388608
  621.6 11.7 copy-start.5
  621.6 11.7 copy-start.19
  621.6 11.8 copy-start.22
  637.9 11.7 copy-start.15
  712.8 933.6 %reduce-scatter.8.cloned.1.call-start = ((), (), s32[]{:S(2)}) async-start(), calls=%async_computation.12 | async-start | bytes 23789568 | tf_op jit(solution)/shard_map/reduce_scatter | solution.py:261
  759.8 1139.0 %reduce-scatter.10.cloned.1.call-start = ((), (), s32[]{:S(2)}) async-start(), calls=%async_computation.13 | async-start | bytes 11894784
  (42 other events, 205.4 us)
Sparse Core Ops, SparseCore 0:
  11.0 59.0 all-gather.10
  73.1 55.1 all-gather.12
  131.3 55.1 all-gather.8
  189.4 55.1 all-gather.14
  247.4 55.2 all-gather.16
  305.4 66.1 all-gather.18
  374.6 65.9 all-gather.20
  443.5 65.9 all-gather.22
  713.0 443.1 reduce-scatter.5
  1158.3 488.0 reduce-scatter.7
  1649.3 249.4 reduce-scatter.9
where the time goes:
time: 1920 us; the launch traced here: 1910 us
  waiting for transfers between devices  1450 us (76%)
  matrix products  232 us (12%)
  local copies, waits for them, and re-layouts  131 us (7%)
  other arithmetic  76.5 us (4%)
    reduce_scatter x1, waiting for transfers between devices, per_device(): lax.psum_scatter(weight_dot(pair_left, normed_two), ('dp', 'fsdp'), scatt...  488 us
    reduce_scatter x1, waiting for transfers between devices, per_device(): lax.psum_scatter(jnp.concatenate([front, rear], axis=1).reshape(5 * width...  325 us
    unnamed x12, waiting for transfers between devices  255 us
    dot_general x8, matrix products, forward_dot(): return jnp.dot(left, right, preferred_element_type=jnp.float32)  62.6 us
    all_gather x1, waiting for transfers between devices, per_device(): lax.all_gather(first_weight, ('dp', 'fsdp'), axis=1, tiled=True)  61.8 us
    dot_general x8, matrix products, back_dot(): lax.dot_general(left, right, (((1,), (1,)), ((), ())), preferred_element_...  59.8 us
    all_gather x1, waiting for transfers between devices, per_device(): lax.all_gather(second_weight, ('dp', 'fsdp'), axis=1, tiled=True)  57.4 us
    all_gather x1, waiting for transfers between devices, per_device(): lax.all_gather(down_weight, ('dp', 'fsdp'), axis=1, tiled=True)  57.1 us
  transfers between devices with their start and end apart: 11, of which 11 were waited for; matrix products, arithmetic and copies ran while one was open for 12% of the time, Pallas kernels for 0%

commit v1 on v0

--- a/solution.py
+++ b/solution.py
@@ -214,6 +214,37 @@
     return (result, (normed_two, first, second, product_low))
 
 
+AXES = ("dp", "fsdp")
+ROWS = 24
+
+
+def gather_rows(matrices, shards):
+    count = len(matrices)
+    local = jnp.stack([jnp.transpose(matrix).reshape(-1, D) for matrix in matrices])
+    width = local.shape[1]
+    full = lax.all_gather(local.reshape(count * width, D), AXES, axis=0, tiled=True)
+    full = full.reshape(shards, count, width, D)
+    return tuple(full[:, index].reshape(shards * width, D) for index in range(count))
+
+
+def scatter_rows(terms, shards):
+    count = len(terms)
+    width = terms[0].shape[0] // shards
+    extra = -count * width % ROWS
+    pieces = [term.reshape(shards, width, D) for term in terms]
+    if extra:
+        pieces.append(jnp.zeros((shards, extra, D), terms[0].dtype))
+    stacked = jnp.concatenate(pieces, axis=1)
+    summed = lax.psum_scatter(
+        stacked.reshape(shards * (count * width + extra), D), AXES, scatter_dimension=0, tiled=True
+    )
+    return summed[: count * width].reshape(count, width, D)
+
+
+def weight_term(left, right):
+    return weight_dot(left, right).astype(jnp.bfloat16)
+
+
 def per_device(
     inputs,
     lengths,
@@ -227,69 +258,48 @@
     down_weight,
     cotangent,
 ):
-    shards = lax.axis_size(("dp", "fsdp"))
-    attn_full = (
-        lax.all_gather(query_weight, ("dp", "fsdp"), axis=1, tiled=True),
-        lax.all_gather(key_weight, ("dp", "fsdp"), axis=1, tiled=True),
-        lax.all_gather(value_weight, ("dp", "fsdp"), axis=1, tiled=True),
-        lax.all_gather(gate_weight, ("dp", "fsdp"), axis=1, tiled=True),
-        lax.all_gather(out_weight, ("dp", "fsdp"), axis=1, tiled=True),
-    )
+    shards = lax.axis_size(AXES)
+    query_t, key_t, value_t, gate_t, out_t = gather_rows(
+        (query_weight, key_weight, value_weight, gate_weight, out_weight), shards
+    )
+    first_t, second_t, down_flat = gather_rows((first_weight, second_weight, down_weight), shards)
+    down_t = down_flat.reshape(D, -1)
     inputs_f = inputs.astype(jnp.float32)
     length = inputs.shape[0]
     mask = (lax.iota(jnp.int32, length) < lengths[0]).astype(jnp.float32)[:, None]
     tables = make_tables(length)
-    mixed, attn_kept = attention_forward(inputs_f, mask, attn_full, tables)
-    glu_full = (
-        lax.all_gather(first_weight, ("dp", "fsdp"), axis=1, tiled=True),
-        lax.all_gather(second_weight, ("dp", "fsdp"), axis=1, tiled=True),
-        lax.all_gather(down_weight, ("dp", "fsdp"), axis=1, tiled=True),
-    )
-    result, glu_kept = glu_forward(mixed, mask, glu_full)
-    glu_back = (
-        lax.all_gather(first_weight, ("dp", "fsdp"), axis=1, tiled=True),
-        lax.all_gather(second_weight, ("dp", "fsdp"), axis=1, tiled=True),
-        lax.all_gather(down_weight, ("dp", "fsdp"), axis=1, tiled=True),
-    )
-    first_back, second_back, down_back = glu_back
-    normed_two, first, second, product_low = glu_kept
-    product_grad = back_dot(cotangent, down_back)
+    normed = simple_norm(inputs_f).astype(jnp.bfloat16)
+    query_pre = back_dot(normed, query_t)
+    key_pre = back_dot(normed, key_t)
+    value_pre = back_dot(normed, value_t)
+    gate_pre = back_dot(normed, gate_t)
+    query_rot = rotate(jax.nn.silu(query_pre) * mask, tables[0], tables[1]).astype(jnp.bfloat16)
+    key_rot = rotate(jax.nn.silu(key_pre) * mask, tables[0], tables[1]).astype(jnp.bfloat16)
+    values = (value_pre * mask).astype(jnp.bfloat16)
+    attended, saved = lightning_forward(query_rot, key_rot, values, tables)
+    attended_norm = simple_norm(attended)
+    gated = (attended_norm * gate_pre * mask).astype(jnp.bfloat16)
+    mixed = inputs_f + back_dot(gated, out_t)
+    normed_two = simple_norm(mixed).astype(jnp.bfloat16)
+    first = back_dot(normed_two, first_t)
+    second = back_dot(normed_two, second_t)
+    product_low = (first * second * mask).astype(jnp.bfloat16)
+    result = mixed + back_dot(product_low, down_t)
+    product_grad = forward_dot(cotangent, down_t)
     first_low = (product_grad * second * mask).astype(jnp.bfloat16)
     second_low = (product_grad * first * mask).astype(jnp.bfloat16)
-    normed_two_grad = back_dot(first_low, first_back) + back_dot(second_low, second_back)
-    pair_left = group_columns((first_low, second_low), shards)
-    pair_sums = lax.psum_scatter(
-        weight_dot(pair_left, normed_two), ("dp", "fsdp"), scatter_dimension=0, tiled=True
-    )
-    first_sum, second_sum = split_rows(pair_sums, 2)
-    down_sums = lax.psum_scatter(
-        weight_dot(cotangent, product_low), ("dp", "fsdp"), scatter_dimension=0, tiled=True
-    )
-    down_sum = jnp.transpose(down_sums)
+    normed_two_grad = forward_dot(first_low, first_t) + forward_dot(second_low, second_t)
+    down_term = weight_term(cotangent, product_low).reshape(-1, D)
+    glu_sums = scatter_rows(
+        (weight_term(first_low, normed_two), weight_term(second_low, normed_two), down_term),
+        shards,
+    ).astype(jnp.float32)
+    first_sum = jnp.transpose(glu_sums[0])
+    second_sum = jnp.transpose(glu_sums[1])
+    down_sum = jnp.transpose(glu_sums[2].reshape(down_weight.shape[1], -1))
     mixed_grad = cotangent.astype(jnp.float32) + norm_back(mixed, normed_two_grad)
-    attn_back = (
-        lax.all_gather(query_weight, ("dp", "fsdp"), axis=1, tiled=True),
-        lax.all_gather(key_weight, ("dp", "fsdp"), axis=1, tiled=True),
-        lax.all_gather(value_weight, ("dp", "fsdp"), axis=1, tiled=True),
-        lax.all_gather(gate_weight, ("dp", "fsdp"), axis=1, tiled=True),
-        lax.all_gather(out_weight, ("dp", "fsdp"), axis=1, tiled=True),
-    )
-    query_back, key_back, value_back, gate_back, out_back = attn_back
-    (
-        normed,
-        query_pre,
-        key_pre,
-        gate_pre,
-        values,
-        query_rot,
-        key_rot,
-        attended,
-        attended_norm,
-        gated,
-        saved,
-    ) = attn_kept
     mixed_low = mixed_grad.astype(jnp.bfloat16)
-    gated_grad = back_dot(mixed_low, out_back)
+    gated_grad = forward_dot(mixed_low, out_t)
     gate_low = (gated_grad * attended_norm * mask).astype(jnp.bfloat16)
     attended_low = norm_back(attended, gated_grad * gate_pre * mask).astype(jnp.bfloat16)
     query_rot_grad, key_rot_grad, values_grad = lightning_backward(
@@ -302,33 +312,26 @@
         jnp.bfloat16
     )
     value_low = (values_grad * mask).astype(jnp.bfloat16)
+    attn_sums = scatter_rows(
+        (
+            weight_term(query_low, normed),
+            weight_term(key_low, normed),
+            weight_term(value_low, normed),
+            weight_term(gate_low, normed),
+            weight_term(mixed_low, gated),
+        ),
+        shards,
+    ).astype(jnp.float32)
     normed_grad = (
-        back_dot(query_low, query_back)
-        + back_dot(key_low, key_back)
-        + back_dot(value_low, value_back)
-        + back_dot(gate_low, gate_back)
-    )
-    attn_left = group_columns((query_low, key_low, value_low, gate_low, mixed_low), shards)
-    width = query_weight.shape[1]
-    piece = attn_left
-    owners = 5 * width * lax.axis_size(("dp", "fsdp")) // (5 * width)
-    piece = piece.reshape(length, owners, 5, width)
-    front = weight_dot(piece[:, :, :4].reshape(length, owners * 4 * width), normed).reshape(
-        owners, 4, width, D
-    )
-    rear = weight_dot(piece[:, :, 4].reshape(length, owners * width), gated).reshape(
-        owners, 1, width, D
-    )
-    attn_sums = lax.psum_scatter(
-        jnp.concatenate([front, rear], axis=1).reshape(
-            5 * width * lax.axis_size(("dp", "fsdp")), D
-        ),
-        ("dp", "fsdp"),
-        scatter_dimension=0,
-        tiled=True,
-    )
-    query_sum, key_sum, value_sum, gate_sum, out_sum = split_rows(attn_sums, 5)
+        forward_dot(query_low, query_t)
+        + forward_dot(key_low, key_t)
+        + forward_dot(value_low, value_t)
+        + forward_dot(gate_low, gate_t)
+    )
     input_grad = mixed_grad + norm_back(inputs_f, normed_grad)
+    query_sum, key_sum, value_sum, gate_sum, out_sum = (
+        jnp.transpose(attn_sums[index]) for index in range(5)
+    )
     return (
         result.astype(jnp.bfloat16),
         input_grad,

time: 1920 us -> 810 us (0.42)
  waiting for transfers between devices: 1450 us -> 351 us
    reduce_scatter x2, waiting for transfers between devices: 813 us -> 237 us  [scatter_rows(): lax.psum_scatter(stacked.reshape(shards * (count * width + extra), D), AX...]
    all_gather x8 -> x2, waiting for transfers between devices: 381 us -> 114 us  [gather_rows(): lax.all_gather(local.reshape(count * width, D), AXES, axis=0, tiled=True)]
    unnamed x12 -> x4, waiting for transfers between devices: 255 us -> 0.07 us
    another operation x1 -> x5, local copies, waits for them, and re-layouts: 5.03 us -> 26.5 us  [the longest x1 11.9 us: scatter_rows(): pieces = [term.reshape(shards, width, D) for term in terms]]
    slice x0 -> x3, local copies, waits for them, and re-layouts: none -> 20.1 us  [the longest x2 19.2 us: gather_rows(): full[:, index].reshape(shards * width, D)]
    unnamed x120 -> x156, local copies, waits for them, and re-layouts: 42.9 us -> 40.3 us
    dot_general x4 -> x8, matrix products: 47.8 us -> 48 us  [weight_dot(): lax.dot_general(left, right, (((0,), (0,)), ((), ())), preferred_element_...]
  transfers between devices with their start and end apart: 11 -> 4, of which waited for: 11 -> 4; matrix products, arithmetic and copies ran while one was open for 12% -> 24% of each run, Pallas kernels for 0% -> 0%
where the time goes in v1:
time: 810 us; the launch traced here: 800 us
  waiting for transfers between devices  351 us (43%)
  matrix products  226 us (28%)
  local copies, waits for them, and re-layouts  139 us (17%)
  other arithmetic  68.5 us (8%)
  between operations  15.6 us (2%)
    reduce_scatter x2, waiting for transfers between devices, scatter_rows(): lax.psum_scatter(stacked.reshape(shards * (count * width + extra), D), AX...  237 us
    all_gather x2, waiting for transfers between devices, gather_rows(): lax.all_gather(local.reshape(count * width, D), AXES, axis=0, tiled=True)  114 us
    dot_general x8, matrix products, back_dot(): lax.dot_general(left, right, (((1,), (1,)), ((), ())), preferred_element_...  58.8 us
    dot_general x8, matrix products, forward_dot(): return jnp.dot(left, right, preferred_element_type=jnp.float32)  55.1 us
    dot_general x8, matrix products, weight_dot(): lax.dot_general(left, right, (((0,), (0,)), ((), ())), preferred_element_...  48 us
    unnamed x156, local copies, waits for them, and re-layouts  40.3 us
    slice x2, local copies, waits for them, and re-layouts, gather_rows(): full[:, index].reshape(shards * width, D)  19.2 us
  transfers between devices with their start and end apart: 4, of which 4 were waited for; matrix products, arithmetic and copies ran while one was open for 24% of the time, Pallas kernels for 0%

profile of v1, /device:TPU:0, one launch (start us, length us, event | category | flops | bytes accessed | tf_op | source)
XLA Modules:
  0.0 800.1 jit_solution(1190515735452336546)
XLA Ops:
  32.4 68.9 %all-gather.3.cloned.1.call-done = bf16[5120,1024]{1,0:T(8,128)(2,1)} async-done(((bf16[160,1024]{1,0:T(8,128)(2,1)}), bf16[5120,1024]{1,0:T(8,128)(2,1)}) %all-gather.3.cloned.1.call-update) | async-done | bytes 10485776 | tf_op jit(solution)/shard_map/all_gather | solution.py:225
  137.7 9.6 %while.30 = (s32[]{:T(128)}, f32[8,256,128]{2,1,0:T(8,128)S(1)}, bf16[4,8,256,128]{3,2,1,0:T(8,128)(2,1)}, f32[4,8,256,128]{3,2,1,0:T(8,128)}, s32[]{:T(128)}, /*index=5*/s32[]{:T(128)}) while((s32[]{:T(128)}, f32[8,256,128]{2,1,0:T(8,128)S(1)}, bf16[4,8,256,128]{3,2,1,0:T(8,128)(2,1)}, f32[4,8,256,128]{3,2,1,0:T(8,128)}, ...), condition=%wide.region_2.3_spmd.clone, body=%wide.region_1.2_spmd.clone.sunk | while | flops 1048603 | bytes 4718752 | solution.py:115
  161.0 8.1 %multiply_convert_fusion.8 = (bf16[1024,1024]{1,0:T(8,128)(2,1)S(1)}, f32[1024,1024]{1,0:T(8,128)}) fusion(f32[128,8,8,128]{3,2,1,0:T(8,128)} %bitcast.224, f32[1024]{0:T(1024)S(1)} %rsqrt.34, f32[1024]{0:T(1024)S(1)} %fusion.70, bf16[1024,1024]{1,0:T(8,128)(2,1)} %bitcast.245, bf16[1024,1024]{0,1:T(8,128)(2,1)S(1)} %copy.50, f32[1024]{0:T(1024)S(1)} %fusion.71), kind=kOutput, calls=%fused_computation.76 | convolution fusion | flops 2154823680 | bytes 14692352 | tf_op jit(solution)/shard_map/dot_general | solution.py:36
  174.2 45.4 %all-gather.5.cloned.1.call-done = bf16[8448,1024]{1,0:T(8,128)(2,1)} async-done(((bf16[264,1024]{1,0:T(8,128)(2,1)}), bf16[8448,1024]{1,0:T(8,128)(2,1)}) %all-gather.5.cloned.1.call-update) | async-done | bytes 17301520 | tf_op jit(solution)/shard_map/all_gather | solution.py:225
  219.6 13.1 %fusion.74 = (bf16[32,1,88,1024]{3,2,1,0:T(8,128)(2,1)}, bf16[32,1,88,1024]{3,2,1,0:T(8,128)(2,1)}, bf16[32,1,88,1024]{3,2,1,0:T(8,128)(2,1)}) fusion(bf16[32,3,88,1024]{3,2,1,0:T(8,128)(2,1)} %bitcast.239), kind=kLoop, calls=%fused_computation.169 | loop fusion | bytes 34603008 | tf_op jit(solution)/shard_map/slice | solution.py:227
  232.7 11.7 %reshape_reshape_squeeze.3 = bf16[1024,2816]{1,0:T(8,128)(2,1)} reshape(bf16[32,1,88,1024]{3,2,1,0:T(8,128)(2,1)} %get-tuple-element.212) | data formatting | bytes 11534336 | tf_op jit(solution)/shard_map/reshape;reshape;squeeze | solution.py:266
  244.4 11.9 %fusion.81 = f32[2816,1024]{0,1:T(8,128)} fusion(bf16[1024,1024]{1,0:T(8,128)(2,1)} %param.25, bf16[1024,2816]{1,0:T(8,128)(2,1)} %reshape_reshape_squeeze.3), kind=kOutput, calls=%fused_computation.176 | convolution fusion | flops 5905580032 | bytes 19398656 | tf_op jit(solution)/shard_map/dot_general | solution.py:32
  256.3 9.1 %fusion.76 = f32[1024,2816]{1,0:T(8,128)} fusion(bf16[1024,1024]{0,1:T(8,128)(2,1)S(1)} %multiply_convert_fusion.7, bf16[2816,1024]{1,0:T(8,128)(2,1)S(1)} %bitcast.251), kind=kOutput, calls=%fused_computation.171 | convolution fusion | flops 5905580032 | bytes 19398656 | tf_op jit(solution)/shard_map/dot_general | solution.py:36
  265.4 20.1 %fusion.8 = (bf16[1024,2816]{1,0:T(8,128)(2,1)}, bf16[1024,2816]{1,0:T(8,128)(2,1)}, bf16[1024,2816]{1,0:T(8,128)(2,1)}) fusion(f32[2816,1024]{0,1:T(8,128)} %fusion.81, f32[1024]{0:T(1024)S(1)} %fusion.70, f32[1024,2816]{1,0:T(8,128)} %fusion.76, bf16[1024,1024]{0,1:T(8,128)(2,1)S(1)} %multiply_convert_fusion.7, bf16[2816,1024]{1,0:T(8,128)(2,1)} %bitcast.237), kind=kOutput, calls=%fused_computation.16 | convolution fusion | flops 5931532288 | bytes 48238592 | tf_op jit(solution)/shard_map/dot_general | solution.py:36
  285.5 11.4 %fusion.77 = f32[1024,1024]{0,1:T(8,128)} fusion(bf16[1024,2816]{1,0:T(8,128)(2,1)} %get-tuple-element.216, bf16[2816,1024]{1,0:T(8,128)(2,1)} %bitcast.238), kind=kOutput, calls=%fused_computation.172 | convolution fusion | flops 5905580032 | bytes 15728640 | tf_op jit(solution)/shard_map/dot_general | solution.py:32
  296.9 11.4 %multiply_reduce_fusion = (f32[1024]{0:T(1024)S(1)}, f32[1024,1024]{0,1:T(8,128)}) fusion(f32[1024,1024]{0,1:T(8,128)S(1)} %copy-done.21, f32[1024,1024]{0,1:T(8,128)} %fusion.77, bf16[1024,2816]{1,0:T(8,128)(2,1)S(1)} %copy-done.28, bf16[2816,1024]{1,0:T(8,128)(2,1)} %bitcast.250), kind=kOutput, calls=%fused_computation.72 | convolution fusion | flops 5908724736 | bytes 24121344 | tf_op jit(solution)/shard_map/dot_general | solution.py:32
  349.0 9.8 %while.31 = (s32[]{:T(128)}, bf16[8,256,128]{2,1,0:T(8,128)(2,1)S(1)}, bf16[4,8,256,128]{3,2,1,0:T(8,128)(2,1)}, f32[4,8,256,128]{3,2,1,0:T(8,128)}, s32[]{:T(128)}, /*index=5*/s32[]{:T(128)}, s32[]{:T(128)}) while((s32[]{:T(128)}, bf16[8,256,128]{2,1,0:T(8,128)(2,1)S(1)}, bf16[4,8,256,128]{3,2,1,0:T(8,128)(2,1)}, ...), condition=%wide.region_8.9_spmd.clone, body=%wide.region_7.8_spmd.clone.sunk | while | flops 1572892 | bytes 3145908 | solution.py:160
  365.2 11.3 %fusion.9 = f32[4,256,8,256]{3,1,2,0:T(8,128)} fusion(f32[4,8,256,256]{2,3,1,0:T(8,128)} %fusion.44, f32[256,8]{0,1:T(8,128)S(1)} %copy-done.57, bf16[4,8,256,256]{3,2,1,0:T(8,128)(2,1)} %multiply_convert_fusion.1, bf16[4,256,8,128]{3,1,2,0:T(8,128)(2,1)} %get-tuple-element.231, bf16[4,256,8,128]{3,1,2,0:T(8,128)(2,1)} %get-tuple-element.232), kind=kOutput, calls=%fused_computation.19 | convolution fusion | flops 1086324736 | bytes 25174016 | tf_op jit(solution)/shard_map/chts,cthf->cshf/dot_general | solution.py:140
  376.4 11.7 %copy.74 = f32[4,256,8,256]{3,2,1,0:T(8,128)} copy(f32[4,256,8,256]{3,1,2,0:T(8,128)} %fusion.9) | data formatting | bytes 16777216 | tf_op jit(solution)/shard_map/add | solution.py:166
  392.7 8.4 %copy.69 = f32[4,256,8,256]{3,2,1,0:T(8,128)S(1)} copy(f32[4,256,8,256]{3,1,2,0:T(8,128)} %fusion.10) | data formatting | bytes 16777216 | tf_op jit(solution)/shard_map/add | solution.py:149
  405.2 8.4 %fusion.18 = (bf16[1024,1024]{1,0:T(8,128)(2,1)S(1)}, bf16[1024,1024]{1,0:T(8,128)(2,1)S(1)}) fusion(f32[1024,1024]{1,0:T(8,128)} %copy-done.23, f32[128,8,8,128]{3,2,1,0:T(8,128)} %bitcast.242, f32[1024]{0:T(1024)S(1)} %fusion.70, f32[1024,1024]{1,0:T(8,128)} %copy-done.22, f32[128,8,8,128]{3,2,1,0:T(8,128)} %bitcast.243), kind=kLoop, calls=%fused_computation.46 | loop fusion | flops 23068672 | bytes 20975616 | tf_op jit(solution)/shard_map/convert_element_type | solution.py:311
  446.4 11.5 %convert_bitcast_fusion = bf16[1024,2816]{0,1:T(8,128)(2,1)} fusion(bf16[1024,2816]{1,0:T(8,128)(2,1)} %get-tuple-element.217, bf16[1024,1024]{1,0:T(8,128)(2,1)} %param.25), kind=kOutput, calls=%fused_computation.36 | convolution fusion | flops 5908463616 | bytes 13631488 | tf_op jit(solution)/shard_map/dot_general | solution.py:42
  458.0 8.6 %copy.80 = bf16[1024,2816]{1,0:T(8,128)(2,1)} copy(bf16[1024,2816]{0,1:T(8,128)(2,1)} %convert_bitcast_fusion) | data formatting | bytes 11534336 | tf_op jit(solution)/shard_map/convert_element_type | solution.py:245
  466.6 11.9 %reshape_reshape.3 = bf16[32,88,1024]{2,1,0:T(8,128)(2,1)} reshape(bf16[1024,2816]{1,0:T(8,128)(2,1)} %copy.80) | data formatting | bytes 11534336 | tf_op jit(solution)/shard_map/reshape;reshape | solution.py:234
  478.5 9.9 %convolution_convert_fusion = bf16[2816,1024]{1,0:T(8,128)(2,1)S(1)} fusion(bf16[1024,2816]{1,0:T(8,128)(2,1)} %get-tuple-element.215, bf16[1024,1024]{0,1:T(8,128)(2,1)} %copy-done.26), kind=kOutput, calls=%fused_computation.37 | convolution fusion | flops 5908463616 | bytes 13631488 | tf_op jit(solution)/shard_map/dot_general | solution.py:42
  488.4 9.2 %convolution_convert_fusion.1 = bf16[2816,1024]{1,0:T(8,128)(2,1)S(1)} fusion(bf16[1024,2816]{1,0:T(8,128)(2,1)} %get-tuple-element.216, bf16[1024,1024]{0,1:T(8,128)(2,1)S(1)} %copy-done.27), kind=kOutput, calls=%fused_computation.38 | convolution fusion | flops 5908463616 | bytes 13631488 | tf_op jit(solution)/shard_map/dot_general | solution.py:42
  504.8 11.6 %add_convert_fusion = bf16[1024,1024]{0,1:T(8,128)(2,1)} fusion(f32[1024,1024]{0,1:T(8,128)} %copy-done.20, bf16[1024,2816]{1,0:T(8,128)(2,1)} %get-tuple-element.217, bf16[1024,2816]{1,0:T(8,128)(2,1)} %reshape_reshape_squeeze.3), kind=kOutput, calls=%fused_computation.73 | convolution fusion | flops 5907677184 | bytes 17825792 | tf_op jit(solution)/shard_map/dot_general | solution.py:36
  550.4 38.3 %reduce-scatter.3.cloned.1.call-done = bf16[168,1024]{1,0:T(8,128)(2,1)} async-done(((bf16[5376,1024]{1,0:T(8,128)(2,1)}), bf16[168,1024]{1,0:T(8,128)(2,1)}) %reduce-scatter.3.cloned.1.call-update) | async-done | bytes 344080 | tf_op jit(solution)/shard_map/reduce_scatter | solution.py:238
  590.6 198.8 %reduce-scatter.5.cloned.1.call-done = bf16[264,1024]{1,0:T(8,128)(2,1)} async-done(((bf16[8448,1024]{1,0:T(8,128)(2,1)}), bf16[264,1024]{1,0:T(8,128)(2,1)}) %reduce-scatter.5.cloned.1.call-update) | async-done | bytes 540688 | tf_op jit(solution)/shard_map/reduce_scatter | solution.py:238
  (263 shorter events, 233.7 us)
Async XLA Ops:
  7.2 94.1 %all-gather.3.cloned.1.call-start = ((), (), s32[]{:S(2)}) async-start(), calls=%async_computation.2 | async-start | bytes 10813440 | tf_op jit(solution)/shard_map/all_gather | solution.py:225
  12.2 207.4 %all-gather.5.cloned.1.call-start = ((), (), s32[]{:S(2)}) async-start(), calls=%async_computation.3 | async-start | bytes 17842176 | tf_op jit(solution)/shard_map/all_gather | solution.py:225
  15.3 573.4 %reduce-scatter.3.cloned.1.call-start = ((), (), s32[]{:S(2)}) async-start(), calls=%async_computation.4 | async-start | bytes 11354112 | tf_op jit(solution)/shard_map/reduce_scatter | solution.py:238
  18.3 150.9 %copy-start.7 = (bf16[1024,1024]{0,1:T(8,128)(2,1)}, bf16[1024,1024]{0,1:T(8,128)(2,1)S(1)}, u32[]{:S(2)}) copy-start(bf16[1024,1024]{0,1:T(8,128)(2,1)S(1)} %copy.50) | copy-start | bytes 6291460
  24.2 136.8 %copy-start.60 = (f32[1024]{0:T(1024)}, f32[1024]{0:T(1024)S(1)}, u32[]{:S(2)}) copy-start(f32[1024]{0:T(1024)S(1)} %fusion.71) | copy-start | bytes 12292
  24.9 109.2 %copy-start.56 = (f32[256,8]{0,1:T(8,128)}, f32[256,8]{0,1:T(8,128)S(1)}, u32[]{:S(2)}) copy-start(f32[256,8]{0,1:T(8,128)S(1)} %get-tuple-element.248) | copy-start | bytes 24580
  107.3 9.8 %copy-start.40 = (bf16[32,1,32,1024]{3,2,1,0:T(8,128)(2,1)}, bf16[32,1,32,1024]{3,2,1,0:T(8,128)(2,1)S(1)}, u32[]{:S(2)}) copy-start(bf16[32,1,32,1024]{3,2,1,0:T(8,128)(2,1)S(1)} %get-tuple-element.222) | copy-start | bytes 6291460
  120.4 13.6 %copy-start.9 = (bf16[128,8,8,128]{3,2,1,0:T(8,128)(2,1)}, bf16[128,8,8,128]{3,2,1,0:T(8,128)(2,1)S(1)}, u32[]{:S(2)}) copy-start(bf16[128,8,8,128]{3,2,1,0:T(8,128)(2,1)S(1)} %copy.92) | copy-start | bytes 6291460
  124.8 9.3 %copy-start.16 = (bf16[4,256,8,128]{3,1,2,0:T(8,128)(2,1)}, bf16[4,256,8,128]{3,1,2,0:T(8,128)(2,1)S(1)}, u32[]{:S(2)}) copy-start(bf16[4,256,8,128]{3,1,2,0:T(8,128)(2,1)S(1)} %get-tuple-element.228) | copy-start | bytes 6291460
  174.2 91.2 %copy-start.26 = (bf16[1024,1024]{0,1:T(8,128)(2,1)}, bf16[1024,1024]{0,1:T(8,128)(2,1)S(1)}, u32[]{:S(2)}) copy-start(bf16[1024,1024]{0,1:T(8,128)(2,1)S(1)} %multiply_convert_fusion.7) | copy-start | bytes 6291460
  244.4 11.9 %copy-start.38 = (bf16[32,1,88,1024]{3,2,1,0:T(8,128)(2,1)S(1)}, bf16[32,1,88,1024]{3,2,1,0:T(8,128)(2,1)}, u32[]{:S(2)}) copy-start(bf16[32,1,88,1024]{3,2,1,0:T(8,128)(2,1)} %get-tuple-element.213) | copy-start | bytes 17301508
  285.5 11.4 %copy-start.21 = (f32[1024,1024]{0,1:T(8,128)S(1)}, f32[1024,1024]{0,1:T(8,128)}, u32[]{:S(2)}) copy-start(f32[1024,1024]{0,1:T(8,128)} %copy-done.20) | copy-start | bytes 12582916
  285.5 11.4 %copy-start.28 = (bf16[1024,2816]{1,0:T(8,128)(2,1)S(1)}, bf16[1024,2816]{1,0:T(8,128)(2,1)}, u32[]{:S(2)}) copy-start(bf16[1024,2816]{1,0:T(8,128)(2,1)} %get-tuple-element.215) | copy-start | bytes 17301508
  296.9 11.4 %copy-start.34 = (bf16[1024,1024]{0,1:T(8,128)(2,1)S(1)}, bf16[1024,1024]{0,1:T(8,128)(2,1)}, u32[]{:S(2)}) copy-start(bf16[1024,1024]{0,1:T(8,128)(2,1)} %copy.62) | copy-start | bytes 6291460
  349.0 9.8 %copy-start.11 = (bf16[128,8,8,128]{3,2,1,0:T(8,128)(2,1)S(1)}, bf16[128,8,8,128]{3,2,1,0:T(8,128)(2,1)}, u32[]{:S(2)}) copy-start(bf16[128,8,8,128]{3,2,1,0:T(8,128)(2,1)} %copy-done.9) | copy-start | bytes 6291460
  358.8 29.3 %slice-start = ((s8[8388608]{0:T(1024)(128)(4,1)}), s8[4194304]{0:T(1024)(128)(4,1)S(1)}, s32[]{:S(2)}) async-start(s8[8388608]{0:T(1024)(128)(4,1)} %bitcast.227), calls=%async_computation.6 | async-start | bytes 8388608
  365.2 23.0 %slice-start.1 = ((s8[8388608]{0:T(1024)(128)(4,1)}), s8[4194304]{0:T(1024)(128)(4,1)S(1)}, s32[]{:S(2)}) async-start(s8[8388608]{0:T(1024)(128)(4,1)} %bitcast.227), calls=%async_computation.7 | async-start | bytes 8388608
  376.4 11.7 %copy-start.5 = (bf16[4,8,256,256]{3,2,1,0:T(8,128)(2,1)S(1)}, bf16[4,8,256,256]{3,2,1,0:T(8,128)(2,1)}, u32[]{:S(2)}) copy-start(bf16[4,8,256,256]{3,2,1,0:T(8,128)(2,1)} %multiply_convert_fusion.1) | copy-start | bytes 12582916
  376.4 11.7 %copy-start.14 = (bf16[4,256,8,128]{3,1,2,0:T(8,128)(2,1)S(1)}, bf16[4,256,8,128]{3,1,2,0:T(8,128)(2,1)}, u32[]{:S(2)}) copy-start(bf16[4,256,8,128]{3,1,2,0:T(8,128)(2,1)} %copy-done.13) | copy-start | bytes 6291460
  376.4 11.7 %copy-start.17 = (bf16[4,256,8,128]{3,1,2,0:T(8,128)(2,1)S(1)}, bf16[4,256,8,128]{3,1,2,0:T(8,128)(2,1)}, u32[]{:S(2)}) copy-start(bf16[4,256,8,128]{3,1,2,0:T(8,128)(2,1)} %copy-done.16) | copy-start | bytes 6291460
  446.4 343.0 %reduce-scatter.5.cloned.1.call-start = ((), (), s32[]{:S(2)}) async-start(), calls=%async_computation.5 | async-start | bytes 17842176 | tf_op jit(solution)/shard_map/reduce_scatter | solution.py:238
  478.5 9.9 %copy-start.27 = (bf16[1024,1024]{0,1:T(8,128)(2,1)S(1)}, bf16[1024,1024]{0,1:T(8,128)(2,1)}, u32[]{:S(2)}) copy-start(bf16[1024,1024]{0,1:T(8,128)(2,1)} %copy-done.26) | copy-start | bytes 6291460
  478.5 19.2 %slice-start.2 = ((s8[5767168]{0:T(1024)(128)(4,1)}), s8[4194304]{0:T(1024)(128)(4,1)S(1)}, s32[]{:S(2)}) async-start(s8[5767168]{0:T(1024)(128)(4,1)} %bitcast.235), calls=%async_computation.8 | async-start | bytes 8388608
  488.4 9.3 %slice-start.3 = ((s8[5767168]{0:T(1024)(128)(4,1)}), s8[1572864]{0:T(1024)(128)(4,1)S(1)}, s32[]{:S(2)}) async-start(s8[5767168]{0:T(1024)(128)(4,1)} %bitcast.235), calls=%async_computation.9 | async-start | bytes 3145728
  (49 other events, 218.3 us)
Sparse Core Ops, SparseCore 0:
  12.3 88.8 all-gather.2
  104.1 115.3 all-gather.4
  446.5 142.1 reduce-scatter.2
  595.0 194.3 reduce-scatter.4

commit v2 on v1

--- a/solution.py
+++ b/solution.py
@@ -215,7 +215,6 @@
 
 
 AXES = ("dp", "fsdp")
-ROWS = 24
 
 
 def gather_rows(matrices, shards):
@@ -227,18 +226,83 @@
     return tuple(full[:, index].reshape(shards * width, D) for index in range(count))
 
 
+def pick(parts, axis, index):
+    return lax.dynamic_index_in_dim(parts, index, axis, keepdims=False)
+
+
+def add_low(*pieces):
+    total = pieces[0].astype(jnp.float32)
+    for piece in pieces[1:]:
+        total = total + piece.astype(jnp.float32)
+    return total.astype(jnp.bfloat16)
+
+
+class Line:
+    def __init__(self, name, size, inner):
+        self.name, self.size, self.inner = name, size, inner
+        self.place = lax.axis_index(name) // inner % size
+
+    def move(self, value, shift, allowed):
+        pairs = []
+        for source in range(lax.axis_size(self.name)):
+            place = source // self.inner % self.size
+            if place in allowed and 0 <= place + shift < self.size:
+                pairs.append((source, source + shift * self.inner))
+        return lax.ppermute(value, self.name, pairs)
+
+    def swap(self, value):
+        pairs = []
+        for source in range(lax.axis_size(self.name)):
+            place = source // self.inner % self.size
+            pairs.append((source, source + (1 - 2 * place) * self.inner))
+        return lax.ppermute(value, self.name, pairs)
+
+    def scatter(self, parts, axis):
+        size = self.size
+        if size == 1:
+            return pick(parts, axis, 0)
+        own = pick(parts, axis, self.place)
+        if size == 2:
+            return add_low(own, self.swap(pick(parts, axis, 1 - self.place)))
+        rising = pick(parts, axis, jnp.minimum(self.place + size - 1, size - 1))
+        falling = pick(parts, axis, jnp.maximum(self.place - size + 1, 0))
+        for step in range(1, size):
+            rising = self.move(rising, 1, range(step))
+            falling = self.move(falling, -1, range(size - step, size))
+            if step < size - 1:
+                up = jnp.minimum(self.place + size - step - 1, size - 1)
+                down = jnp.maximum(self.place - size + step + 1, 0)
+                rising = add_low(pick(parts, axis, up), rising)
+                falling = add_low(pick(parts, axis, down), falling)
+        return add_low(own, rising, falling)
+
+
+def lines():
+    rows = lax.axis_size("dp")
+    columns = lax.axis_size("fsdp")
+    short = 1 << ((columns.bit_length() - 1) // 2)
+    return (
+        Line("dp", 2, 1),
+        Line("dp", rows // 2, 2),
+        Line("fsdp", short, 1),
+        Line("fsdp", columns // short, short),
+    )
+
+
 def scatter_rows(terms, shards):
-    count = len(terms)
+    core, across, up, deep = lines()
     width = terms[0].shape[0] // shards
-    extra = -count * width % ROWS
-    pieces = [term.reshape(shards, width, D) for term in terms]
-    if extra:
-        pieces.append(jnp.zeros((shards, extra, D), terms[0].dtype))
-    stacked = jnp.concatenate(pieces, axis=1)
-    summed = lax.psum_scatter(
-        stacked.reshape(shards * (count * width + extra), D), AXES, scatter_dimension=0, tiled=True
-    )
-    return summed[: count * width].reshape(count, width, D)
+    half = D // 2
+    parts = jnp.stack(
+        [
+            term.reshape(across.size, 2, deep.size, up.size, width, D)
+            for term in terms
+        ]
+    )
+    parts = core.scatter(parts, 2)
+    left = up.scatter(across.scatter(parts[..., :half], 1), 2)
+    right = across.scatter(up.scatter(parts[..., half:], 3), 1)
+    return deep.scatter(jnp.concatenate([left, right], axis=-1), 1)
 
 
 def weight_term(left, right):
@@ -301,6 +365,9 @@
     mixed_low = mixed_grad.astype(jnp.bfloat16)
     gated_grad = forward_dot(mixed_low, out_t)
     gate_low = (gated_grad * attended_norm * mask).astype(jnp.bfloat16)
+    early_sums = scatter_rows(
+        (weight_term(mixed_low, gated), weight_term(gate_low, normed)), shards
+    ).astype(jnp.float32)
     attended_low = norm_back(attended, gated_grad * gate_pre * mask).astype(jnp.bfloat16)
     query_rot_grad, key_rot_grad, values_grad = lightning_backward(
         attended_low, query_rot, key_rot, values, saved, tables
@@ -312,13 +379,11 @@
         jnp.bfloat16
     )
     value_low = (values_grad * mask).astype(jnp.bfloat16)
-    attn_sums = scatter_rows(
+    late_sums = scatter_rows(
         (
             weight_term(query_low, normed),
             weight_term(key_low, normed),
             weight_term(value_low, normed),
-            weight_term(gate_low, normed),
-            weight_term(mixed_low, gated),
         ),
         shards,
     ).astype(jnp.float32)
@@ -329,9 +394,8 @@
         + forward_dot(gate_low, gate_t)
     )
     input_grad = mixed_grad + norm_back(inputs_f, normed_grad)
-    query_sum, key_sum, value_sum, gate_sum, out_sum = (
-        jnp.transpose(attn_sums[index]) for index in range(5)
-    )
+    query_sum, key_sum, value_sum = (jnp.transpose(late_sums[index]) for index in range(3))
+    out_sum, gate_sum = (jnp.transpose(early_sums[index]) for index in range(2))
     return (
         result.astype(jnp.bfloat16),
         input_grad,

time: 810 us -> 764 us (0.943)
  waiting for transfers between devices: 351 us -> 201 us
  starting transfers between devices: 0.16 us -> 52.9 us
  other arithmetic: 68.5 us -> 103 us
  local copies, waits for them, and re-layouts: 139 us -> 153 us
    reduce_scatter x2 -> x0, waiting for transfers between devices: 237 us -> none  [scatter_rows(): lax.psum_scatter(stacked.reshape(shards * (count * width + extra), D), AX...]
    ppermute x0 -> x33, waiting for transfers between devices: none -> 86.5 us  [the longest x15 69.8 us: swap(): return lax.ppermute(value, self.name, pairs)]
    ppermute x0 -> x33, starting transfers between devices: none -> 52.9 us  [the longest x18 39.9 us: move(): return lax.ppermute(value, self.name, pairs)]
    another operation x1 -> x4, other arithmetic: 3.84 us -> 26.2 us  [the longest x3 22.4 us: scatter_rows(): jnp.stack([term.reshape(across.size, 2, deep.size, up.size, width, D) for...]
    convert_element_type x1 -> x23, other arithmetic: 1.02 us -> 19.5 us  [the longest x21 19.3 us: add_low(): return total.astype(jnp.bfloat16)]
    squeeze x0 -> x12, local copies, waits for them, and re-layouts: none -> 11.4 us  [pick(): return lax.dynamic_index_in_dim(parts, index, axis, keepdims=False)]
    dot_general x8, matrix products: 55.1 us -> 64.2 us  [forward_dot(): return jnp.dot(left, right, preferred_element_type=jnp.float32)]
    unnamed x156 -> x202, local copies, waits for them, and re-layouts: 40.3 us -> 38.9 us
  transfers between devices with their start and end apart: 4 -> 35, of which waited for: 4 -> 17; matrix products, arithmetic and copies ran while one was open for 24% -> 25% of each run, Pallas kernels for 0% -> 0%
where the time goes in v2:
time: 764 us; the launch traced here: 754 us
  matrix products  227 us (30%)
  waiting for transfers between devices  201 us (26%)
  local copies, waits for them, and re-layouts  153 us (20%)
  other arithmetic  103 us (13%)
  starting transfers between devices  52.9 us (7%)
  between operations  16.8 us (2%)
    all_gather x2, waiting for transfers between devices, gather_rows(): lax.all_gather(local.reshape(count * width, D), AXES, axis=0, tiled=True)  114 us
    ppermute x15, waiting for transfers between devices, swap(): return lax.ppermute(value, self.name, pairs)  69.8 us
    dot_general x8, matrix products, forward_dot(): return jnp.dot(left, right, preferred_element_type=jnp.float32)  64.2 us
    dot_general x8, matrix products, back_dot(): lax.dot_general(left, right, (((1,), (1,)), ((), ())), preferred_element_...  54.7 us
    dot_general x8, matrix products, weight_dot(): lax.dot_general(left, right, (((0,), (0,)), ((), ())), preferred_element_...  43.9 us
    ppermute x18, starting transfers between devices, move(): return lax.ppermute(value, self.name, pairs)  39.9 us
    unnamed x202, local copies, waits for them, and re-layouts  38.9 us
    another operation x3, other arithmetic, scatter_rows(): jnp.stack([term.reshape(across.size, 2, deep.size, up.size, width, D) for...  22.4 us
  transfers between devices with their start and end apart: 35, of which 17 were waited for; matrix products, arithmetic and copies ran while one was open for 25% of the time, Pallas kernels for 0%

profile of v2, /device:TPU:0, one launch (start us, length us, event | category | flops | bytes accessed | tf_op | source)
XLA Modules:
  0.0 754.2 jit_solution(8468181267595614439)
XLA Ops:
  32.5 68.7 %all-gather.3.cloned.1.call-done = bf16[5120,1024]{1,0:T(8,128)(2,1)} async-done(((bf16[160,1024]{1,0:T(8,128)(2,1)}), bf16[5120,1024]{1,0:T(8,128)(2,1)}) %all-gather.3.cloned.1.call-update) | async-done | bytes 10485776 | tf_op jit(solution)/shard_map/all_gather | solution.py:224
  137.7 9.6 %while.30 = (s32[]{:T(128)}, f32[8,256,128]{2,1,0:T(8,128)S(1)}, bf16[4,8,256,128]{3,2,1,0:T(8,128)(2,1)}, f32[4,8,256,128]{3,2,1,0:T(8,128)}, s32[]{:T(128)}, /*index=5*/s32[]{:T(128)}) while((s32[]{:T(128)}, f32[8,256,128]{2,1,0:T(8,128)S(1)}, bf16[4,8,256,128]{3,2,1,0:T(8,128)(2,1)}, f32[4,8,256,128]{3,2,1,0:T(8,128)}, ...), condition=%wide.region_2.3_spmd.clone, body=%wide.region_1.2_spmd.clone.sunk | while | flops 1048603 | bytes 4718752 | solution.py:115
  174.2 45.4 %all-gather.5.cloned.1.call-done = bf16[8448,1024]{1,0:T(8,128)(2,1)} async-done(((bf16[264,1024]{1,0:T(8,128)(2,1)}), bf16[8448,1024]{1,0:T(8,128)(2,1)}) %all-gather.5.cloned.1.call-update) | async-done | bytes 17301520 | tf_op jit(solution)/shard_map/all_gather | solution.py:224
  219.6 13.1 %fusion.154 = (bf16[32,1,88,1024]{3,2,1,0:T(8,128)(2,1)}, bf16[32,1,88,1024]{3,2,1,0:T(8,128)(2,1)}, bf16[32,1,88,1024]{3,2,1,0:T(8,128)(2,1)}) fusion(bf16[32,3,88,1024]{3,2,1,0:T(8,128)(2,1)} %bitcast.429), kind=kLoop, calls=%fused_computation.341 | loop fusion | bytes 34603008 | tf_op jit(solution)/shard_map/slice | solution.py:226
  232.7 11.7 %reshape_reshape_squeeze.3 = bf16[1024,2816]{1,0:T(8,128)(2,1)} reshape(bf16[32,1,88,1024]{3,2,1,0:T(8,128)(2,1)} %get-tuple-element.212) | data formatting | bytes 11534336 | tf_op jit(solution)/shard_map/reshape;reshape;squeeze | solution.py:330
  244.4 12.0 %fusion.165 = f32[2816,1024]{0,1:T(8,128)} fusion(bf16[1024,1024]{1,0:T(8,128)(2,1)} %param.25, bf16[1024,2816]{1,0:T(8,128)(2,1)} %reshape_reshape_squeeze.3), kind=kOutput, calls=%fused_computation.352 | convolution fusion | flops 5905580032 | bytes 19398656 | tf_op jit(solution)/shard_map/dot_general | solution.py:32
  256.4 9.1 %fusion.160 = f32[1024,2816]{1,0:T(8,128)} fusion(bf16[1024,1024]{0,1:T(8,128)(2,1)S(1)} %multiply_convert_fusion.7, bf16[2816,1024]{1,0:T(8,128)(2,1)S(1)} %bitcast.455), kind=kOutput, calls=%fused_computation.347 | convolution fusion | flops 5905580032 | bytes 19398656 | tf_op jit(solution)/shard_map/dot_general | solution.py:36
  265.5 20.2 %fusion.9 = (bf16[1024,2816]{1,0:T(8,128)(2,1)}, bf16[1024,2816]{1,0:T(8,128)(2,1)}, bf16[1024,2816]{1,0:T(8,128)(2,1)}) fusion(f32[2816,1024]{0,1:T(8,128)} %fusion.165, f32[1024]{0:T(1024)S(1)} %fusion.150, f32[1024,2816]{1,0:T(8,128)} %fusion.160, bf16[1024,1024]{0,1:T(8,128)(2,1)S(1)} %multiply_convert_fusion.7, bf16[2816,1024]{1,0:T(8,128)(2,1)} %bitcast.427), kind=kOutput, calls=%fused_computation.18 | convolution fusion | flops 5931532288 | bytes 48238592 | tf_op jit(solution)/shard_map/dot_general | solution.py:36
  285.7 11.4 %fusion.161 = f32[1024,1024]{0,1:T(8,128)} fusion(bf16[1024,2816]{1,0:T(8,128)(2,1)} %get-tuple-element.216, bf16[2816,1024]{1,0:T(8,128)(2,1)} %bitcast.428), kind=kOutput, calls=%fused_computation.348 | convolution fusion | flops 5905580032 | bytes 15728640 | tf_op jit(solution)/shard_map/dot_general | solution.py:32
  297.1 11.4 %multiply_reduce_fusion = (f32[1024]{0:T(1024)S(1)}, f32[1024,1024]{0,1:T(8,128)}) fusion(f32[1024,1024]{0,1:T(8,128)S(1)} %copy-done.22, f32[1024,1024]{0,1:T(8,128)} %fusion.161, bf16[1024,2816]{1,0:T(8,128)(2,1)S(1)} %copy-done.32, bf16[2816,1024]{1,0:T(8,128)(2,1)} %bitcast.454), kind=kOutput, calls=%fused_computation.88 | convolution fusion | flops 5908724736 | bytes 24121344 | tf_op jit(solution)/shard_map/dot_general | solution.py:32
  348.2 8.5 %convolution_convert_fusion = bf16[2816,1024]{1,0:T(8,128)(2,1)} fusion(bf16[1024,2816]{1,0:T(8,128)(2,1)S(1)} %bitcast.443, bf16[1024,1024]{0,1:T(8,128)(2,1)S(1)} %copy-done.31), kind=kOutput, calls=%fused_computation.43 | convolution fusion | flops 5908463616 | bytes 13631488 | tf_op jit(solution)/shard_map/dot_general | solution.py:42
  356.7 8.4 %convolution_convert_fusion.1 = bf16[2816,1024]{1,0:T(8,128)(2,1)} fusion(bf16[1024,2816]{1,0:T(8,128)(2,1)S(1)} %bitcast.441, bf16[1024,1024]{0,1:T(8,128)(2,1)S(1)} %copy-done.31), kind=kOutput, calls=%fused_computation.44 | convolution fusion | flops 5908463616 | bytes 13631488 | tf_op jit(solution)/shard_map/dot_general | solution.py:42
  366.9 9.9 %while.31 = (s32[]{:T(128)}, bf16[8,256,128]{2,1,0:T(8,128)(2,1)S(1)}, bf16[4,8,256,128]{3,2,1,0:T(8,128)(2,1)}, f32[4,8,256,128]{3,2,1,0:T(8,128)}, s32[]{:T(128)}, /*index=5*/s32[]{:T(128)}, s32[]{:T(128)}) while((s32[]{:T(128)}, bf16[8,256,128]{2,1,0:T(8,128)(2,1)S(1)}, bf16[4,8,256,128]{3,2,1,0:T(8,128)(2,1)}, ...), condition=%wide.region_8.9_spmd.clone, body=%wide.region_7.8_spmd.clone.sunk | while | flops 1572892 | bytes 3145908 | solution.py:160
  396.3 11.4 %fusion.10 = f32[4,256,8,256]{3,1,2,0:T(8,128)} fusion(f32[4,8,256,256]{2,3,1,0:T(8,128)} %fusion.55, f32[256,8]{0,1:T(8,128)S(1)} %copy-done.66, bf16[4,8,256,256]{3,2,1,0:T(8,128)(2,1)} %multiply_convert_fusion.1, bf16[4,256,8,128]{3,1,2,0:T(8,128)(2,1)} %get-tuple-element.250, bf16[4,256,8,128]{3,1,2,0:T(8,128)(2,1)} %get-tuple-element.251), kind=kOutput, calls=%fused_computation.22 | convolution fusion | flops 1086324736 | bytes 25174016 | tf_op jit(solution)/shard_map/chts,cthf->cshf/dot_general | solution.py:140
  407.7 11.7 %copy.81 = f32[4,256,8,256]{3,2,1,0:T(8,128)} copy(f32[4,256,8,256]{3,1,2,0:T(8,128)} %fusion.10) | data formatting | bytes 16777216 | tf_op jit(solution)/shard_map/add | solution.py:166
  424.0 8.4 %copy.76 = f32[4,256,8,256]{3,2,1,0:T(8,128)S(1)} copy(f32[4,256,8,256]{3,1,2,0:T(8,128)} %fusion.11) | data formatting | bytes 16777216 | tf_op jit(solution)/shard_map/add | solution.py:149
  436.7 8.7 %fusion.22 = (bf16[1024,1024]{1,0:T(8,128)(2,1)}, bf16[1024,1024]{1,0:T(8,128)(2,1)S(1)}) fusion(f32[1024,1024]{1,0:T(8,128)} %copy-done.26, f32[128,8,8,128]{3,2,1,0:T(8,128)} %bitcast.434, f32[1024]{0:T(1024)S(1)} %fusion.150, f32[1024,1024]{1,0:T(8,128)S(1)} %copy-done.25, f32[128,8,8,128]{3,2,1,0:T(8,128)} %bitcast.435), kind=kLoop, calls=%fused_computation.60 | loop fusion | flops 23068672 | bytes 20975616 | tf_op jit(solution)/shard_map/convert_element_type | solution.py:378
  470.3 11.7 %stack_reshape_reshape.3 = bf16[1,2,2,4,2,88,1024]{6,5,4,3,2,1,0:T(8,128)(2,1)} reshape(bf16[1024,2816]{1,0:T(8,128)(2,1)} %copy.92) | data formatting | bytes 11534336 | tf_op jit(solution)/shard_map/stack;reshape;reshape | solution.py:296
  482.0 14.2 %pad_maximum_fusion = bf16[3,2,2,4,2,88,1024]{6,5,4,3,2,1,0:T(8,128)(2,1)} fusion(bf16[1,2,2,4,2,88,1024]{6,5,4,3,2,1,0:T(8,128)(2,1)} %stack_reshape_reshape.3, bf16[1,2,2,4,2,88,1024]{6,5,4,3,2,1,0:T(8,128)(2,1)} %bitcast.452, bf16[1,2,2,4,2,88,1024]{6,5,4,3,2,1,0:T(8,128)(2,1)} %bitcast.453), kind=kLoop, calls=%fused_computation.10 | loop fusion | flops 17301504 | bytes 34603008 | tf_op jit(solution)/shard_map/stack | solution.py:296
  496.2 8.6 %dynamic-slice_bitcast_fusion = bf16[3,2,4,2,88,1024]{5,4,3,2,1,0:T(8,128)(2,1)} fusion(bf16[3,2,2,4,2,88,1024]{6,5,4,3,2,1,0:T(8,128)(2,1)} %pad_maximum_fusion, s32[]{:T(128)S(6)} %select_n.154), kind=kLoop, calls=%fused_computation.20 | loop fusion | bytes 17301508 | tf_op jit(solution)/shard_map/jit(dynamic_index_in_dim)/squeeze | solution.py:230
  534.6 10.1 %fusion.26 = (f32[1024]{0:T(1024)S(1)}, f32[1024,1024]{0,1:T(8,128)}) fusion(bf16[1024,1024]{0,1:T(8,128)(2,1)S(1)} %copy-done.8, bf16[1024,1024]{1,0:T(8,128)(2,1)S(1)} %copy-done.40, bf16[1024,1024]{1,0:T(8,128)(2,1)S(1)} %bitcast.446, f32[1024,1024]{0,1:T(8,128)} %fusion.43, f32[1024,1024]{0,1:T(8,128)} %fusion.162, f32[1024,1024]{0,1:T(8,128)} %fusion.163), kind=kOutput, calls=%fused_computation.64 | convolution fusion | flops 2153774080 | bytes 23072768 | tf_op jit(solution)/shard_map/dot_general | solution.py:32
  621.9 20.9 %collective-permute-done.23 = bf16[3,4,2,88,512]{4,3,1,0,2:T(8,128)(2,1)} collective-permute-done((bf16[3,4,2,88,512]{4,3,1,0,2:T(8,128)(2,1)}, bf16[3,4,2,88,512]{4,3,1,0,2:T(8,128)(2,1)}, u32[]{:S(2)}, u32[]{:S(2)}) %collective-permute-start.23) | collective-permute-done | bytes 2162720 | tf_op jit(solution)/shard_map/ppermute | solution.py:258
  668.0 21.5 %collective-permute-done.24 = bf16[3,4,88,512]{3,2,1,0:T(8,128)(2,1)S(1)} collective-permute-done((bf16[3,4,88,512]{3,2,1,0:T(8,128)(2,1)S(1)}, bf16[3,4,88,512]{3,2,1,0:T(8,128)(2,1)S(1)}, u32[]{:S(2)}, u32[]{:S(2)}) %collective-permute-start.24) | collective-permute-done | bytes 1081376 | tf_op jit(solution)/shard_map/ppermute | solution.py:258
  721.4 9.1 %collective-permute-start.7 = (bf16[3,32,1024]{2,1,0:T(8,128)(2,1)S(1)}, bf16[3,32,1024]{2,1,0:T(8,128)(2,1)S(1)}, u32[]{:S(2)}, u32[]{:S(2)}) collective-permute-start(bf16[3,32,1024]{2,1,0:T(8,128)(2,1)S(1)} %get-tuple-element.254), channel_id=1, source_target_pairs={{0,2},{1,3},{2,4},{3,5},{4,6},{5,7},{8,10},{9,11},{10,12},{11,13},... | collective-permute-start | bytes 589832 | tf_op jit(solution)/shard_map/ppermute | solution.py:251
  (418 shorter events, 380.8 us)
Async XLA Ops:
  7.2 94.1 %all-gather.3.cloned.1.call-start = ((), (), s32[]{:S(2)}) async-start(), calls=%async_computation | async-start | bytes 10813440 | tf_op jit(solution)/shard_map/all_gather | solution.py:224
  12.2 207.4 %all-gather.5.cloned.1.call-start = ((), (), s32[]{:S(2)}) async-start(), calls=%async_computation.1 | async-start | bytes 17842176 | tf_op jit(solution)/shard_map/all_gather | solution.py:224
  504.8 76.5 %collective-permute-start.22 = (bf16[3,2,4,2,88,1024]{5,4,3,2,1,0:T(8,128)(2,1)}, bf16[3,2,4,2,88,1024]{5,4,3,2,1,0:T(8,128)(2,1)}, u32[]{:S(2)}, u32[]{:S(2)}) collective-permute-start(bf16[3,2,4,2,88,1024]{5,4,3,2,1,0:T(8,128)(2,1)} %dynamic-slice_bitcast_fusion), channel_id=1, source_target_pairs={{0,8},{8,0},{16,24},{24,16},{1,9},{9,1},{17,25},{25,17},{2,10},{10... | collective-permute-start | bytes 25952264 | tf_op jit(solution)/shard_map/ppermute | solution.py:258
  518.4 33.9 %collective-permute-start.11 = (bf16[2,2,4,2,32,1024]{5,4,0,2,1,3:T(8,128)(2,1)}, bf16[2,2,4,2,32,1024]{5,4,0,2,1,3:T(8,128)(2,1)S(1)}, u32[]{:S(2)}, u32[]{:S(2)}) collective-permute-start(bf16[2,2,4,2,32,1024]{5,4,0,2,1,3:T(8,128)(2,1)} %bitcast.403), channel_id=1, source_target_pairs={{0,8},{8,0},{16,24},{24,16},{1,9},{9,1},{17,25},{25,17},{2,10},{10... | collective-permute-start | bytes 6291464 | tf_op jit(solution)/shard_map/ppermute | solution.py:258
  553.6 14.1 %collective-permute-start.12 = (bf16[2,4,2,32,512]{4,3,0,1,2:T(8,128)(2,1)S(1)}, bf16[2,4,2,32,512]{4,3,0,1,2:T(8,128)(2,1)S(1)}, u32[]{:S(2)}, u32[]{:S(2)}) collective-permute-start(bf16[2,4,2,32,512]{4,3,0,1,2:T(8,128)(2,1)S(1)} %dynamic-slice_bitcast_fusion.7), channel_id=1, source_target_pairs={{0,16},{8,24},{16,0},{24,8},{1,17},{9,25},{17,1},{25,9},{2,18},{10... | collective-permute-start | bytes 1572872 | tf_op jit(solution)/shard_map/ppermute | solution.py:258
  559.6 15.0 %collective-permute-start.14 = (bf16[2,2,4,32,512]{4,3,0,2,1:T(8,128)(2,1)}, bf16[2,2,4,32,512]{4,3,0,2,1:T(8,128)(2,1)S(1)}, u32[]{:S(2)}, u32[]{:S(2)}) collective-permute-start(bf16[2,2,4,32,512]{4,3,0,2,1:T(8,128)(2,1)} %dynamic-slice_bitcast_fusion.6), channel_id=1, source_target_pairs={{0,1},{1,0},{2,3},{3,2},{4,5},{5,4},{6,7},{7,6},{8,9},{9,8},{10,11... | collective-permute-start | bytes 1572872 | tf_op jit(solution)/shard_map/ppermute | solution.py:258
  577.7 39.4 %collective-permute-start = (bf16[3,2,4,2,32,1024]{5,4,0,2,1,3:T(8,128)(2,1)}, bf16[3,2,4,2,32,1024]{5,4,0,2,1,3:T(8,128)(2,1)}, u32[]{:S(2)}, u32[]{:S(2)}) collective-permute-start(bf16[3,2,4,2,32,1024]{5,4,0,2,1,3:T(8,128)(2,1)} %bitcast.401), channel_id=1, source_target_pairs={{0,8},{8,0},{16,24},{24,16},{1,9},{9,1},{17,25},{25,17},{2,10},{10... | collective-permute-start | bytes 9437192 | tf_op jit(solution)/shard_map/ppermute | solution.py:258
  592.6 50.2 %collective-permute-start.23 = (bf16[3,4,2,88,512]{4,3,1,0,2:T(8,128)(2,1)}, bf16[3,4,2,88,512]{4,3,1,0,2:T(8,128)(2,1)}, u32[]{:S(2)}, u32[]{:S(2)}) collective-permute-start(bf16[3,4,2,88,512]{4,3,1,0,2:T(8,128)(2,1)} %bitcast.402), channel_id=1, source_target_pairs={{0,16},{8,24},{16,0},{24,8},{1,17},{9,25},{17,1},{25,9},{2,18},{10... | collective-permute-start | bytes 6488072 | tf_op jit(solution)/shard_map/ppermute | solution.py:258
  593.9 19.8 %collective-permute-start.16 = (bf16[2,32,1024]{2,1,0:T(8,128)(2,1)}, bf16[2,32,1024]{2,1,0:T(8,128)(2,1)S(1)}, u32[]{:S(2)}, u32[]{:S(2)}) collective-permute-start(bf16[2,32,1024]{2,1,0:T(8,128)(2,1)} %get-tuple-element.264), channel_id=1, source_target_pairs={{0,2},{1,3},{8,10},{9,11},{16,18},{17,19},{24,26},{25,27}} | collective-permute-start | bytes 393224 | tf_op jit(solution)/shard_map/ppermute | solution.py:251
  596.6 17.2 %collective-permute-start.19 = (bf16[2,32,1024]{2,1,0:T(8,128)(2,1)}, bf16[2,32,1024]{2,1,0:T(8,128)(2,1)}, u32[]{:S(2)}, u32[]{:S(2)}) collective-permute-start(bf16[2,32,1024]{2,1,0:T(8,128)(2,1)} %get-tuple-element.265), channel_id=1, source_target_pairs={{6,4},{7,5},{14,12},{15,13},{22,20},{23,21},{30,28},{31,29}} | collective-permute-start | bytes 393224 | tf_op jit(solution)/shard_map/ppermute | solution.py:251
  599.3 50.2 %collective-permute-start.25 = (bf16[3,2,4,88,512]{4,3,2,1,0:T(8,128)(2,1)}, bf16[3,2,4,88,512]{4,3,2,1,0:T(8,128)(2,1)}, u32[]{:S(2)}, u32[]{:S(2)}) collective-permute-start(bf16[3,2,4,88,512]{4,3,2,1,0:T(8,128)(2,1)} %dynamic-slice_bitcast_fusion.1), channel_id=1, source_target_pairs={{0,1},{1,0},{2,3},{3,2},{4,5},{5,4},{6,7},{7,6},{8,9},{9,8},{10,11... | collective-permute-start | bytes 6488072 | tf_op jit(solution)/shard_map/ppermute | solution.py:258
  614.8 38.4 %collective-permute-start.17 = (bf16[2,32,1024]{2,1,0:T(8,128)(2,1)S(1)}, bf16[2,32,1024]{2,1,0:T(8,128)(2,1)S(1)}, u32[]{:S(2)}, u32[]{:S(2)}) collective-permute-start(bf16[2,32,1024]{2,1,0:T(8,128)(2,1)S(1)} %get-tuple-element.262), channel_id=1, source_target_pairs={{0,2},{1,3},{2,4},{3,5},{8,10},{9,11},{10,12},{11,13},{16,18},{17,... | collective-permute-start | bytes 393224 | tf_op jit(solution)/shard_map/ppermute | solution.py:251
  616.1 37.9 %collective-permute-start.20 = (bf16[2,32,1024]{2,1,0:T(8,128)(2,1)S(1)}, bf16[2,32,1024]{2,1,0:T(8,128)(2,1)S(1)}, u32[]{:S(2)}, u32[]{:S(2)}) collective-permute-start(bf16[2,32,1024]{2,1,0:T(8,128)(2,1)S(1)} %get-tuple-element.263), channel_id=1, source_target_pairs={{4,2},{5,3},{6,4},{7,5},{12,10},{13,11},{14,12},{15,13},{20,18},{2... | collective-permute-start | bytes 393224 | tf_op jit(solution)/shard_map/ppermute | solution.py:251
  621.1 38.5 %collective-permute-start.1 = (bf16[3,4,2,32,512]{4,3,0,1,2:T(8,128)(2,1)S(1)}, bf16[3,4,2,32,512]{4,3,0,1,2:T(8,128)(2,1)S(1)}, u32[]{:S(2)}, u32[]{:S(2)}) collective-permute-start(bf16[3,4,2,32,512]{4,3,0,1,2:T(8,128)(2,1)S(1)} %dynamic-slice_bitcast_fusion.5), channel_id=1, source_target_pairs={{0,16},{8,24},{16,0},{24,8},{1,17},{9,25},{17,1},{25,9},{2,18},{10... | collective-permute-start | bytes 2359304 | tf_op jit(solution)/shard_map/ppermute | solution.py:258
  642.8 23.5 %collective-permute-start.3 = (bf16[3,2,4,32,512]{4,3,0,2,1:T(8,128)(2,1)S(1)}, bf16[3,2,4,32,512]{4,3,0,2,1:T(8,128)(2,1)S(1)}, u32[]{:S(2)}, u32[]{:S(2)}) collective-permute-start(bf16[3,2,4,32,512]{4,3,0,2,1:T(8,128)(2,1)S(1)} %dynamic-slice_bitcast_fusion.4), channel_id=1, source_target_pairs={{0,1},{1,0},{2,3},{3,2},{4,5},{5,4},{6,7},{7,6},{8,9},{9,8},{10,11... | collective-permute-start | bytes 2359304 | tf_op jit(solution)/shard_map/ppermute | solution.py:258
  649.6 39.9 %collective-permute-start.24 = (bf16[3,4,88,512]{3,2,1,0:T(8,128)(2,1)S(1)}, bf16[3,4,88,512]{3,2,1,0:T(8,128)(2,1)S(1)}, u32[]{:S(2)}, u32[]{:S(2)}) collective-permute-start(bf16[3,4,88,512]{3,2,1,0:T(8,128)(2,1)S(1)} %dynamic-slice_bitcast_fusion.3), channel_id=1, source_target_pairs={{0,1},{1,0},{2,3},{3,2},{4,5},{5,4},{6,7},{7,6},{8,9},{9,8},{10,11... | collective-permute-start | bytes 3244040 | tf_op jit(solution)/shard_map/ppermute | solution.py:258
  653.3 37.8 %collective-permute-start.26 = (bf16[3,4,88,512]{3,2,1,0:T(8,128)(2,1)S(1)}, bf16[3,4,88,512]{3,2,1,0:T(8,128)(2,1)S(1)}, u32[]{:S(2)}, u32[]{:S(2)}) collective-permute-start(bf16[3,4,88,512]{3,2,1,0:T(8,128)(2,1)S(1)} %dynamic-slice_bitcast_fusion.2), channel_id=1, source_target_pairs={{0,16},{8,24},{16,0},{24,8},{1,17},{9,25},{17,1},{25,9},{2,18},{10... | collective-permute-start | bytes 3244040 | tf_op jit(solution)/shard_map/ppermute | solution.py:258
  654.1 61.7 %collective-permute-start.21 = (bf16[2,32,1024]{2,1,0:T(8,128)(2,1)S(1)}, bf16[2,32,1024]{2,1,0:T(8,128)(2,1)S(1)}, u32[]{:S(2)}, u32[]{:S(2)}) collective-permute-start(bf16[2,32,1024]{2,1,0:T(8,128)(2,1)S(1)} %get-tuple-element.261), channel_id=1, source_target_pairs={{2,0},{3,1},{4,2},{5,3},{6,4},{7,5},{10,8},{11,9},{12,10},{13,11},... | collective-permute-start | bytes 393224 | tf_op jit(solution)/shard_map/ppermute | solution.py:251
  659.6 56.9 %collective-permute-start.18 = (bf16[2,32,1024]{2,1,0:T(8,128)(2,1)S(1)}, bf16[2,32,1024]{2,1,0:T(8,128)(2,1)S(1)}, u32[]{:S(2)}, u32[]{:S(2)}) collective-permute-start(bf16[2,32,1024]{2,1,0:T(8,128)(2,1)S(1)} %get-tuple-element.260), channel_id=1, source_target_pairs={{0,2},{1,3},{2,4},{3,5},{4,6},{5,7},{8,10},{9,11},{10,12},{11,13},... | collective-permute-start | bytes 393224 | tf_op jit(solution)/shard_map/ppermute | solution.py:251
  666.3 28.0 %collective-permute-start.2 = (bf16[3,4,32,512]{3,2,0,1:T(8,128)(2,1)S(1)}, bf16[3,4,32,512]{3,2,0,1:T(8,128)(2,1)S(1)}, u32[]{:S(2)}, u32[]{:S(2)}) collective-permute-start(bf16[3,4,32,512]{3,2,0,1:T(8,128)(2,1)S(1)} %dynamic-slice_bitcast_fusion.9), channel_id=1, source_target_pairs={{0,1},{1,0},{2,3},{3,2},{4,5},{5,4},{6,7},{7,6},{8,9},{9,8},{10,11... | collective-permute-start | bytes 1179656 | tf_op jit(solution)/shard_map/ppermute | solution.py:258
  706.6 23.9 %collective-permute-start.28 = (bf16[3,88,1024]{2,1,0:T(8,128)(2,1)S(1)}, bf16[3,88,1024]{2,1,0:T(8,128)(2,1)S(1)}, u32[]{:S(2)}, u32[]{:S(2)}) collective-permute-start(bf16[3,88,1024]{2,1,0:T(8,128)(2,1)S(1)} %get-tuple-element.241), channel_id=1, source_target_pairs={{0,2},{1,3},{2,4},{3,5},{8,10},{9,11},{10,12},{11,13},{16,18},{17,... | collective-permute-start | bytes 1622024 | tf_op jit(solution)/shard_map/ppermute | solution.py:251
  711.0 19.5 %collective-permute-start.31 = (bf16[3,88,1024]{2,1,0:T(8,128)(2,1)S(1)}, bf16[3,88,1024]{2,1,0:T(8,128)(2,1)S(1)}, u32[]{:S(2)}, u32[]{:S(2)}) collective-permute-start(bf16[3,88,1024]{2,1,0:T(8,128)(2,1)S(1)} %get-tuple-element.242), channel_id=1, source_target_pairs={{4,2},{5,3},{6,4},{7,5},{12,10},{13,11},{14,12},{15,13},{20,18},{2... | collective-permute-start | bytes 1622024 | tf_op jit(solution)/shard_map/ppermute | solution.py:251
  720.1 17.5 %collective-permute-start.10 = (bf16[3,32,1024]{2,1,0:T(8,128)(2,1)S(1)}, bf16[3,32,1024]{2,1,0:T(8,128)(2,1)S(1)}, u32[]{:S(2)}, u32[]{:S(2)}) collective-permute-start(bf16[3,32,1024]{2,1,0:T(8,128)(2,1)S(1)} %get-tuple-element.255), channel_id=1, source_target_pairs={{2,0},{3,1},{4,2},{5,3},{6,4},{7,5},{10,8},{11,9},{12,10},{13,11},... | collective-permute-start | bytes 589832 | tf_op jit(solution)/shard_map/ppermute | solution.py:251
  721.4 16.2 %collective-permute-start.7 = (bf16[3,32,1024]{2,1,0:T(8,128)(2,1)S(1)}, bf16[3,32,1024]{2,1,0:T(8,128)(2,1)S(1)}, u32[]{:S(2)}, u32[]{:S(2)}) collective-permute-start(bf16[3,32,1024]{2,1,0:T(8,128)(2,1)S(1)} %get-tuple-element.254), channel_id=1, source_target_pairs={{0,2},{1,3},{2,4},{3,5},{4,6},{5,7},{8,10},{9,11},{10,12},{11,13},... | collective-permute-start | bytes 589832 | tf_op jit(solution)/shard_map/ppermute | solution.py:251
  (104 other events, 1378.8 us)
Sparse Core Ops, SparseCore 0:
  12.3 88.8 all-gather.2
  104.1 115.3 all-gather.4

commit v3 on v2

v3 whole, which is shorter than its diff:
```python
import math

import jax
import jax.numpy as jnp
from jax import lax
from jax.experimental import pallas as pl
from jax.experimental.pallas import tpu as pltpu
from jax.sharding import PartitionSpec as P

D = 1024
HEADS = 8
HEAD = 128
SPAN = 256
LAYER = 12
LAYERS = 24


NORM_EPS = 1e-06


def simple_norm(values):
    return values * lax.rsqrt(jnp.mean(values * values, axis=-1, keepdims=True) + NORM_EPS)


def norm_back(values, upstream):
    return jax.vjp(simple_norm, values)[1](upstream)[0]


def forward_dot(left, right):
    return jnp.dot(left, right, preferred_element_type=jnp.float32)


def back_dot(left, right):
    return lax.dot_general(
        left, right, (((1,), (1,)), ((), ())), preferred_element_type=jnp.float32
    )


def weight_dot(left, right):
    return lax.dot_general(
        left, right, (((0,), (0,)), ((), ())), preferred_element_type=jnp.float32
    )


def make_tables(length):
    head_index = jnp.arange(HEADS, dtype=jnp.float32)
    slopes = jnp.exp2(-8.0 * (head_index + 1.0) / HEADS) * (1.0 - LAYER / LAYERS)
    places = jnp.arange(length, dtype=jnp.float32)
    frequency = jnp.exp(-jnp.arange(HEAD, dtype=jnp.float32) * (math.log(10000.0) / HEAD))
    angles = places[:, None] * frequency[None, :]
    return (jnp.cos(angles), jnp.sin(angles), slopes)


def dot_nn(left, right):
    return lax.dot_general(
        left, right, (((1,), (0,)), ((), ())), preferred_element_type=jnp.float32
    )


def decays(slope):
    rows = lax.broadcasted_iota(jnp.int32, (SPAN, SPAN), 0).astype(jnp.float32)
    columns = lax.broadcasted_iota(jnp.int32, (SPAN, SPAN), 1).astype(jnp.float32)
    distance = rows - columns
    within = jnp.where(distance >= 0.0, jnp.exp(-slope * jnp.maximum(distance, 0.0)), 0.0)
    query_decay = jnp.exp(-(rows + 1.0) * slope)
    key_decay = jnp.exp(-(SPAN - 1.0 - rows) * slope)
    block_decay = jnp.exp(jnp.full((1, HEAD), -SPAN, jnp.float32) * slope)
    return within, query_decay, key_decay, block_decay


def span_rows(block):
    return pl.ds(block * SPAN, SPAN)


def span_mask(block, count):
    places = lax.broadcasted_iota(jnp.int32, (SPAN, HEAD), 0) + block * SPAN
    return (places < count).astype(jnp.float32)


def turned(pre, mask, cosine, sine):
    active = pre * jax.nn.sigmoid(pre) * mask
    return jnp.concatenate([active * cosine, active * sine], axis=-1).astype(jnp.bfloat16)


def scaled(turned_block, decay):
    return (turned_block.astype(jnp.float32) * decay).astype(jnp.bfloat16)


def forward_kernel(count_ref, slope_ref, query_ref, key_ref, value_ref, cosine_ref, sine_ref, out_ref):
    within, query_decay, key_decay, block_decay = decays(slope_ref[pl.program_id(0)])
    state = jnp.zeros((2 * HEAD, HEAD), jnp.float32)
    for block in range(query_ref.shape[0] // SPAN):
        rows = span_rows(block)
        mask = span_mask(block, count_ref[0])
        cosine, sine = cosine_ref[rows, :], sine_ref[rows, :]
        query = turned(query_ref[rows, :], mask, cosine, sine)
        key = turned(key_ref[rows, :], mask, cosine, sine)
        value = (value_ref[rows, :] * mask).astype(jnp.bfloat16)
        weights_low = (back_dot(query, key) * within).astype(jnp.bfloat16)
        out_ref[rows, :] = dot_nn(weights_low, value) + dot_nn(
            scaled(query, query_decay), state.astype(jnp.bfloat16)
        )
        state = block_decay * state + weight_dot(scaled(key, key_decay), value)


def silu_slope(pre):
    gate = jax.nn.sigmoid(pre)
    return gate * (1.0 + pre * (1.0 - gate))


def backward_kernel(
    count_ref,
    slope_ref,
    query_ref,
    key_ref,
    value_ref,
    upstream_ref,
    cosine_ref,
    sine_ref,
    query_low_ref,
    key_low_ref,
    value_low_ref,
    state_ref,
):
    within, query_decay, key_decay, block_decay = decays(slope_ref[pl.program_id(0)])
    blocks = query_ref.shape[0] // SPAN
    state = jnp.zeros((2 * HEAD, HEAD), jnp.float32)
    for block in range(blocks):
        state_ref[block] = state.astype(jnp.bfloat16)
        if block + 1 < blocks:
            rows = span_rows(block)
            mask = span_mask(block, count_ref[0])
            key = turned(key_ref[rows, :], mask, cosine_ref[rows, :], sine_ref[rows, :])
            value = (value_ref[rows, :] * mask).astype(jnp.bfloat16)
            state = block_decay * state + weight_dot(scaled(key, key_decay), value)
    later = jnp.zeros((2 * HEAD, HEAD), jnp.bfloat16)
    for block in reversed(range(blocks)):
        rows = span_rows(block)
        mask = span_mask(block, count_ref[0])
        cosine, sine = cosine_ref[rows, :], sine_ref[rows, :]
        query_pre, key_pre = query_ref[rows, :], key_ref[rows, :]
        query = turned(query_pre, mask, cosine, sine)
        key = turned(key_pre, mask, cosine, sine)
        value = (value_ref[rows, :] * mask).astype(jnp.bfloat16)
        upstream = upstream_ref[rows, :]
        weights_low = (back_dot(query, key) * within).astype(jnp.bfloat16)
        score_low = (back_dot(upstream, value) * within).astype(jnp.bfloat16)
        query_grad = dot_nn(score_low, key) + query_decay * back_dot(upstream, state_ref[block])
        key_grad = weight_dot(score_low, query) + key_decay * back_dot(value, later)
        value_grad = weight_dot(weights_low, upstream) + dot_nn(scaled(key, key_decay), later)
        query_back = (query_grad[:, :HEAD] * cosine + query_grad[:, HEAD:] * sine) * mask
        key_back = (key_grad[:, :HEAD] * cosine + key_grad[:, HEAD:] * sine) * mask
        query_low_ref[rows, :] = (silu_slope(query_pre) * query_back).astype(jnp.bfloat16)
        key_low_ref[rows, :] = (silu_slope(key_pre) * key_back).astype(jnp.bfloat16)
        value_low_ref[rows, :] = (value_grad * mask).astype(jnp.bfloat16)
        if block > 0:
            term = weight_dot(scaled(query, query_decay), upstream)
            later = (block_decay * later.astype(jnp.float32) + term).astype(jnp.bfloat16)


def head_specs(length, count):
    return [pl.BlockSpec((length, HEAD), lambda head: (0, head)) for _ in range(count)]


def shared_specs(length):
    return [pl.BlockSpec((length, HEAD), lambda head: (0, 0)) for _ in range(2)]


def scalar_specs():
    return [pl.BlockSpec(memory_space=pltpu.SMEM) for _ in range(2)]


def lightning_forward(lengths, query_pre, key_pre, value_pre, tables, interpret=False):
    length = query_pre.shape[0]
    return pl.pallas_call(
        forward_kernel,
        grid=(HEADS,),
        in_specs=scalar_specs() + head_specs(length, 3) + shared_specs(length),
        out_specs=head_specs(length, 1)[0],
        out_shape=jax.ShapeDtypeStruct((length, D), jnp.float32),
        name="lightning_forward",
        interpret=interpret,
    )(lengths, tables[2], query_pre, key_pre, value_pre, tables[0], tables[1])


def lightning_backward(lengths, query_pre, key_pre, value_pre, upstream, tables, interpret=False):
    length = query_pre.shape[0]
    return pl.pallas_call(
        backward_kernel,
        grid=(HEADS,),
        in_specs=scalar_specs() + head_specs(length, 4) + shared_specs(length),
        out_specs=head_specs(length, 3),
        out_shape=[jax.ShapeDtypeStruct((length, D), jnp.bfloat16)] * 3,
        scratch_shapes=[pltpu.VMEM((length // SPAN, 2 * HEAD, HEAD), jnp.bfloat16)],
        name="lightning_backward",
        interpret=interpret,
    )(lengths, tables[2], query_pre, key_pre, value_pre, upstream, tables[0], tables[1])


AXES = ("dp", "fsdp")


def lane_rows(matrix):
    extra = -matrix.shape[-1] % D
    if extra:
        matrix = jnp.pad(matrix, [(0, 0)] * (matrix.ndim - 1) + [(0, extra)])
    return jnp.split(matrix, matrix.shape[-1] // D, axis=-1)


def gather_rows(matrices, shards):
    pieces = [piece for matrix in matrices for piece in lane_rows(jnp.transpose(matrix))]
    full = lax.all_gather(jnp.concatenate(pieces, axis=0), AXES, axis=0, tiled=True)
    full = full.reshape(shards, -1, D)
    gathered, start = [], 0
    for matrix in matrices:
        size, width = matrix.shape
        count = -(-size // D)
        columns = [
            full[:, start + index * width : start + (index + 1) * width].reshape(shards * width, D)
            for index in range(count)
        ]
        joined = columns[0] if count == 1 else jnp.concatenate(columns, axis=1)[:, :size]
        gathered.append(joined)
        start += count * width
    return gathered


def pick(parts, axis, index):
    return lax.dynamic_index_in_dim(parts, index, axis, keepdims=False)


def add_low(*pieces):
    total = pieces[0].astype(jnp.float32)
    for piece in pieces[1:]:
        total = total + piece.astype(jnp.float32)
    return total.astype(jnp.bfloat16)


class Line:
    def __init__(self, name, size, inner):
        self.name, self.size, self.inner = name, size, inner
        self.place = lax.axis_index(name) // inner % size

    def move(self, value, shift, allowed):
        pairs = []
        for source in range(lax.axis_size(self.name)):
            place = source // self.inner % self.size
            if place in allowed and 0 <= place + shift < self.size:
                pairs.append((source, source + shift * self.inner))
        return lax.ppermute(value, self.name, pairs)

    def swap(self, value):
        pairs = []
        for source in range(lax.axis_size(self.name)):
            place = source // self.inner % self.size
            pairs.append((source, source + (1 - 2 * place) * self.inner))
        return lax.ppermute(value, self.name, pairs)

    def scatter(self, parts, axis):
        size = self.size
        if size == 1:
            return pick(parts, axis, 0)
        own = pick(parts, axis, self.place)
        if size == 2:
            return add_low(own, self.swap(pick(parts, axis, 1 - self.place)))
        rising = pick(parts, axis, jnp.minimum(self.place + size - 1, size - 1))
        falling = pick(parts, axis, jnp.maximum(self.place - size + 1, 0))
        for step in range(1, size):
            rising = self.move(rising, 1, range(step))
            falling = self.move(falling, -1, range(size - step, size))
            if step < size - 1:
                up = jnp.minimum(self.place + size - step - 1, size - 1)
                down = jnp.maximum(self.place - size + step + 1, 0)
                rising = add_low(pick(parts, axis, up), rising)
                falling = add_low(pick(parts, axis, down), falling)
        return add_low(own, rising, falling)


def lines():
    rows = lax.axis_size("dp")
    columns = lax.axis_size("fsdp")
    short = 1 << ((columns.bit_length() - 1) // 2)
    return (
        Line("dp", 2, 1),
        Line("dp", rows // 2, 2),
        Line("fsdp", short, 1),
        Line("fsdp", columns // short, short),
    )


class Scatter:
    def __init__(self, terms):
        self.core, self.across, self.up, self.deep = lines()
        self.sizes = [term.shape[1] for term in terms]
        blocks = [
            term.reshape(self.across.size, 2, self.deep.size, self.up.size, -1, term.shape[1])
            for term in terms
        ]
        self.widths = [block.shape[4] for block in blocks]
        self.own = [pick(block, 1, self.core.place) for block in blocks]
        self.sent = [pick(block, 1, 1 - self.core.place) for block in blocks]

    def to_core(self):
        sums = [add_low(own, self.core.swap(sent)) for own, sent in zip(self.own, self.sent)]
        pieces = [piece for total in sums for piece in lane_rows(total)]
        parts = jnp.concatenate(pieces, axis=-2)
        self.left, self.right = parts[..., : D // 2], parts[..., D // 2 :]

    def to_first(self):
        self.left = self.across.scatter(self.left, 0)
        self.right = self.up.scatter(self.right, 2)

    def to_second(self):
        self.left = self.up.scatter(self.left, 1)
        self.right = self.across.scatter(self.right, 0)
        self.left = jnp.concatenate([self.left, self.right], axis=-1)

    def to_owner(self):
        summed = self.deep.scatter(self.left, 0).astype(jnp.float32)
        outs, start = [], 0
        for size, width in zip(self.sizes, self.widths):
            count = -(-size // D)
            columns = [
                summed[start + index * width : start + (index + 1) * width]
                for index in range(count)
            ]
            joined = columns[0] if count == 1 else jnp.concatenate(columns, axis=1)[:, :size]
            outs.append(jnp.transpose(joined))
            start += count * width
        return outs


def weight_term(left, right):
    return weight_dot(left, right).astype(jnp.bfloat16)


def per_device(
    inputs,
    lengths,
    query_weight,
    key_weight,
    value_weight,
    gate_weight,
    out_weight,
    first_weight,
    second_weight,
    down_weight,
    cotangent,
):
    shards = lax.axis_size(AXES)
    query_t, key_t, value_t, gate_t, out_t = gather_rows(
        (query_weight, key_weight, value_weight, gate_weight, out_weight), shards
    )
    first_t, second_t, down_t = gather_rows((first_weight, second_weight, down_weight), shards)
    inputs_f = inputs.astype(jnp.float32)
    length = inputs.shape[0]
    mask = (lax.iota(jnp.int32, length) < lengths[0]).astype(jnp.float32)[:, None]
    tables = make_tables(length)
    normed = simple_norm(inputs_f).astype(jnp.bfloat16)
    query_pre = back_dot(normed, query_t)
    key_pre = back_dot(normed, key_t)
    value_pre = back_dot(normed, value_t)
    gate_pre = back_dot(normed, gate_t)
    attended = lightning_forward(lengths, query_pre, key_pre, value_pre, tables)
    attended_norm = simple_norm(attended)
    gated = (attended_norm * gate_pre * mask).astype(jnp.bfloat16)
    mixed = inputs_f + back_dot(gated, out_t)
    normed_two = simple_norm(mixed).astype(jnp.bfloat16)
    first = back_dot(normed_two, first_t)
    second = back_dot(normed_two, second_t)
    product_low = (first * second * mask).astype(jnp.bfloat16)
    result = mixed + back_dot(product_low, down_t)
    product_grad = forward_dot(cotangent, down_t)
    first_low = (product_grad * second * mask).astype(jnp.bfloat16)
    second_low = (product_grad * first * mask).astype(jnp.bfloat16)
    normed_two_grad = forward_dot(first_low, first_t) + forward_dot(second_low, second_t)
    glu = Scatter(
        [
            weight_term(first_low, normed_two),
            weight_term(second_low, normed_two),
            weight_term(cotangent, product_low),
        ]
    )
    mixed_grad = cotangent.astype(jnp.float32) + norm_back(mixed, normed_two_grad)
    mixed_low = mixed_grad.astype(jnp.bfloat16)
    mixed_low, glu.sent = lax.optimization_barrier((mixed_low, glu.sent))
    glu.to_core()
    gated_grad = forward_dot(mixed_low, out_t)
    gate_low = (gated_grad * attended_norm * mask).astype(jnp.bfloat16)
    attended_low = norm_back(attended, gated_grad * gate_pre * mask).astype(jnp.bfloat16)
    attended_low, glu.left, glu.right = lax.optimization_barrier(
        (attended_low, glu.left, glu.right)
    )
    glu.to_first()
    query_low, key_low, value_low = lightning_backward(
        lengths, query_pre, key_pre, value_pre, attended_low, tables
    )
    query_low, key_low, value_low, glu.left, glu.right = lax.optimization_barrier(
        (query_low, key_low, value_low, glu.left, glu.right)
    )
    late = Scatter(
        [
            weight_term(mixed_low, gated),
            weight_term(gate_low, normed),
            weight_term(query_low, normed),
            weight_term(key_low, normed),
            weight_term(value_low, normed),
        ]
    )
    glu.to_second()
    late.sent, glu.left = lax.optimization_barrier((late.sent, glu.left))
    late.to_core()
    first_sum, second_sum, down_sum = glu.to_owner()
    normed_grad = (
        forward_dot(query_low, query_t)
        + forward_dot(key_low, key_t)
        + forward_dot(value_low, value_t)
        + forward_dot(gate_low, gate_t)
    )
    input_grad = mixed_grad + norm_back(inputs_f, normed_grad)
    late.to_first()
    late.to_second()
    out_sum, gate_sum, query_sum, key_sum, value_sum = late.to_owner()
    return (
        result.astype(jnp.bfloat16),
        input_grad,
        query_sum,
        key_sum,
        value_sum,
        gate_sum,
        out_sum,
        first_sum,
        second_sum,
        down_sum,
    )


def solution(mesh):
    return jax.shard_map(
        per_device,
        mesh=mesh,
        in_specs=(
            P(("dp", "fsdp"), None),
            P(("dp", "fsdp")),
            P(None, ("dp", "fsdp")),
            P(None, ("dp", "fsdp")),
            P(None, ("dp", "fsdp")),
            P(None, ("dp", "fsdp")),
            P(None, ("dp", "fsdp")),
            P(None, ("dp", "fsdp")),
            P(None, ("dp", "fsdp")),
            P(None, ("dp", "fsdp")),
            P(("dp", "fsdp"), None),
        ),
        out_specs=(
            P(("dp", "fsdp"), None),
            P(("dp", "fsdp"), None),
            P(None, ("dp", "fsdp")),
            P(None, ("dp", "fsdp")),
            P(None, ("dp", "fsdp")),
            P(None, ("dp", "fsdp")),
            P(None, ("dp", "fsdp")),
            P(None, ("dp", "fsdp")),
            P(None, ("dp", "fsdp")),
            P(None, ("dp", "fsdp")),
        ),
        check_vma=False,
    )
```

time: 764 us -> 596 us (0.78)
  matrix products: 227 us -> 160 us
  local copies, waits for them, and re-layouts: 153 us -> 90.1 us
  other arithmetic: 103 us -> 46.6 us
  Pallas kernels: 0 us -> 33 us
  starting transfers between devices: 52.9 us -> 38.7 us
    dot_general x12 -> x0, matrix products: 64.4 us -> none  [the longest x1 11.4 us: lightning_backward(): jnp.einsum('chts,cthf->cshf', score_low, query_blocks, preferred_element_...]
    pallas_call x0 -> x2, Pallas kernels: none -> 33 us  [the longest x1 19.5 us: lightning_backward(): pl.pallas_call(backward_kernel, grid=(HEADS,), in_specs=scalar_specs() +...]
    add x4 -> x0, local copies, waits for them, and re-layouts: 31.2 us -> none  [the longest x1 11.7 us: lightning_backward(): key_part = key_part + key_scaled_grad * key_decay[None, :, :, None]]
    all_gather x2, waiting for transfers between devices: 114 us -> 145 us  [gather_rows(): lax.all_gather(jnp.concatenate(pieces, axis=0), AXES, axis=0, tiled=True)]
    another operation x5 -> x0, other arithmetic: 28.1 us -> none  [the longest x3 22.4 us: scatter_rows(): jnp.stack([term.reshape(across.size, 2, deep.size, up.size, width, D) for...]
    ppermute x15 -> x16, waiting for transfers between devices: 69.8 us -> 42 us  [swap(): return lax.ppermute(value, self.name, pairs)]
    another operation x5 -> x0, local copies, waits for them, and re-layouts: 26.3 us -> none  [the longest x1 11.7 us: scatter_rows(): jnp.stack([term.reshape(across.size, 2, deep.size, up.size, width, D) for...]
    add x6 -> x0, other arithmetic: 13.6 us -> none  [the longest x4 5.85 us: advance(): return (block_decay[:, None, None] * state + update, state)]
  transfers between devices with their start and end apart: 35 -> 30, of which waited for: 17 -> 13; matrix products, arithmetic and copies ran while one was open for 25% -> 25% of each run, Pallas kernels for 0% -> 6%
where the time goes in v3:
time: 596 us; the launch traced here: 587 us
  waiting for transfers between devices  202 us (34%)
  matrix products  160 us (27%)
  local copies, waits for them, and re-layouts  90.1 us (15%)
  other arithmetic  46.6 us (8%)
  starting transfers between devices  38.7 us (6%)
  Pallas kernels  33 us (6%)
  between operations  16.2 us (3%)
    all_gather x2, waiting for transfers between devices, gather_rows(): lax.all_gather(jnp.concatenate(pieces, axis=0), AXES, axis=0, tiled=True)  145 us
    dot_general x8, matrix products, back_dot(): lax.dot_general(left, right, (((1,), (1,)), ((), ())), preferred_element_...  60.6 us
    dot_general x8, matrix products, forward_dot(): return jnp.dot(left, right, preferred_element_type=jnp.float32)  57.9 us
    ppermute x16, waiting for transfers between devices, swap(): return lax.ppermute(value, self.name, pairs)  42 us
    dot_general x8, matrix products, weight_dot(): lax.dot_general(left, right, (((0,), (0,)), ((), ())), preferred_element_...  41.4 us
    unnamed x130, local copies, waits for them, and re-layouts  40.7 us
    ppermute x12, starting transfers between devices, move(): return lax.ppermute(value, self.name, pairs)  27.3 us
    slice x3, local copies, waits for them, and re-layouts, gather_rows(): full[:, start + index * width:start + (index + 1) * width]  19.9 us
  transfers between devices with their start and end apart: 30, of which 13 were waited for; matrix products, arithmetic and copies ran while one was open for 25% of the time, Pallas kernels for 6%

profile of v3, /device:TPU:0, one launch (start us, length us, event | category | flops | bytes accessed | tf_op | source)
XLA Modules:
  0.0 586.5 jit_solution(16502848123634537060)
XLA Ops:
  29.0 72.3 %all-gather.3.cloned.1.call-done = bf16[5120,1024]{1,0:T(8,128)(2,1)} async-done(((bf16[160,1024]{1,0:T(8,128)(2,1)}), bf16[5120,1024]{1,0:T(8,128)(2,1)}) %all-gather.3.cloned.1.call-update) | async-done | bytes 10485776 | tf_op jit(solution)/shard_map/all_gather | solution.py:212
  101.2 6.1 %fusion.89 = (bf16[32,32,1024]{2,1,0:T(8,128)(2,1)}, bf16[32,32,1024]{2,1,0:T(8,128)(2,1)}, bf16[32,32,1024]{2,1,0:T(8,128)(2,1)S(1)}, bf16[32,32,1024]{2,1,0:T(8,128)(2,1)S(1)}, bf16[32,32,1024]{2,1,0:T(8,128)(2,1)S(1)}) fusion(bf16[32,160,1024]{2,1,0:T(8,128)(2,1)} %bitcast.262), kind=kLoop, calls=%fused_computation.228 | loop fusion | bytes 20971520 | tf_op jit(solution)/shard_map/slice | solution.py:219
  120.6 13.5 %lightning_forward.1 = f32[1024,1024]{1,0:T(8,128)} custom-call(s32[1]{0:T(128)} %copy.115.count_ref, f32[8]{0:T(128)} %exponential_multiply_fusion.slope_ref, f32[1024,1024]{1,0:T(8,128)} %fusion.63.query_ref, f32[1024,1024]{1,0:T(8,128)} %fusion.61.key_ref, f32[1024,1024]{1,0:T(8,128)} %fusion.59.value_ref, f32[1024,128]{1,0:T(8,128)} %get-tuple-element.118.cosine_ref, ...), custom_call_target="tpu_custom_call" | custom-call | tf_op jit(solution)/shard_map/lightning_forward/pallas_call | solution.py:175
  137.6 6.5 %multiply_convert_fusion.3 = (bf16[1024,1024]{1,0:T(8,128)(2,1)S(1)}, f32[1024,1024]{1,0:T(8,128)}) fusion(f32[1024,1024]{1,0:T(8,128)S(1)} %copy-done, f32[1024]{0:T(1024)S(1)} %fusion.81, f32[1024]{0:T(1024)S(1)} %fusion.83, bf16[1024,1024]{1,0:T(8,128)(2,1)} %bitcast.280, bf16[1024,1024]{0,1:T(8,128)(2,1)S(1)} %copy.21, f32[1024]{0:T(1024)S(1)} %fusion.82), kind=kOutput, calls=%fused_computation.44 | convolution fusion | flops 2154823680 | bytes 14692352 | tf_op jit(solution)/shard_map/dot_general | solution.py:34
  149.1 72.7 %all-gather.5.cloned.1.call-done = bf16[8704,1024]{1,0:T(8,128)(2,1)} async-done(((bf16[272,1024]{1,0:T(8,128)(2,1)}), bf16[8704,1024]{1,0:T(8,128)(2,1)}) %all-gather.5.cloned.1.call-update) | async-done | bytes 17825808 | tf_op jit(solution)/shard_map/all_gather | solution.py:212
  221.8 9.9 %fusion.88 = (bf16[32,88,1024]{2,1,0:T(8,128)(2,1)}, bf16[32,88,1024]{2,1,0:T(8,128)(2,1)}) fusion(bf16[32,272,1024]{2,1,0:T(8,128)(2,1)} %bitcast.258), kind=kLoop, calls=%fused_computation.227 | loop fusion | bytes 23068672 | tf_op jit(solution)/shard_map/slice | solution.py:219
  236.2 8.9 %fusion.93 = f32[1024,2816]{1,0:T(8,128)} fusion(bf16[1024,1024]{0,1:T(8,128)(2,1)S(1)} %multiply_convert_fusion.2, bf16[2816,1024]{1,0:T(8,128)(2,1)S(1)} %bitcast.273), kind=kOutput, calls=%fused_computation.232 | convolution fusion | flops 5905580032 | bytes 19398656 | tf_op jit(solution)/shard_map/dot_general | solution.py:34
  245.1 10.2 %fusion.27 = f32[2816,1024]{0,1:T(8,128)} fusion(bf16[1024,1024]{1,0:T(8,128)(2,1)S(1)} %copy-done.34, bf16[1024,1024]{1,0:T(8,128)(2,1)S(1)} %bitcast.289, bf16[1024,1024]{1,0:T(8,128)(2,1)S(1)} %bitcast.291, bf16[1024,1024]{1,0:T(8,128)(2,1)S(1)} %bitcast.287), kind=kOutput, calls=%fused_computation.91 | convolution fusion | flops 5922881536 | bytes 19922944 | tf_op jit(solution)/shard_map/dot_general | solution.py:30
  255.3 20.2 %fusion.3 = (bf16[1024,2816]{1,0:T(8,128)(2,1)}, bf16[1024,2816]{1,0:T(8,128)(2,1)}, bf16[1024,2816]{1,0:T(8,128)(2,1)}) fusion(f32[2816,1024]{0,1:T(8,128)} %fusion.27, f32[1024]{0:T(1024)S(1)} %fusion.81, f32[1024,2816]{1,0:T(8,128)} %fusion.93, bf16[1024,1024]{0,1:T(8,128)(2,1)S(1)} %multiply_convert_fusion.2, bf16[2816,1024]{1,0:T(8,128)(2,1)} %bitcast.256), kind=kOutput, calls=%fused_computation.5 | convolution fusion | flops 5931532288 | bytes 48238592 | tf_op jit(solution)/shard_map/dot_general | solution.py:34
  275.4 10.9 %convolution_convert_fusion.2 = bf16[2816,1024]{1,0:T(8,128)(2,1)} fusion(bf16[1024,2816]{1,0:T(8,128)(2,1)} %get-tuple-element.68, bf16[1024,1024]{0,1:T(8,128)(2,1)S(1)} %multiply_convert_fusion.2), kind=kOutput, calls=%fused_computation.25 | convolution fusion | flops 5908463616 | bytes 13631488 | tf_op jit(solution)/shard_map/dot_general | solution.py:40
  286.4 9.7 %fusion.94 = f32[1024,1024]{0,1:T(8,128)} fusion(bf16[1024,2816]{1,0:T(8,128)(2,1)S(1)} %copy-done.16, bf16[2816,1024]{1,0:T(8,128)(2,1)} %bitcast.257), kind=kOutput, calls=%fused_computation.233 | convolution fusion | flops 5905580032 | bytes 15728640 | tf_op jit(solution)/shard_map/dot_general | solution.py:30
  296.1 6.8 %convolution_convert_fusion.1 = bf16[2816,1024]{1,0:T(8,128)(2,1)S(1)} fusion(bf16[1024,2816]{1,0:T(8,128)(2,1)S(1)} %copy-done.15, bf16[1024,1024]{0,1:T(8,128)(2,1)S(1)} %multiply_convert_fusion.2), kind=kOutput, calls=%fused_computation.24 | convolution fusion | flops 5908463616 | bytes 13631488 | tf_op jit(solution)/shard_map/dot_general | solution.py:40
  312.6 10.8 %multiply_reduce_fusion.1 = (f32[1024]{0:T(1024)S(1)}, f32[1024,1024]{0,1:T(8,128)S(1)}) fusion(f32[1024,1024]{0,1:T(8,128)S(1)} %copy-done.3, f32[1024,1024]{0,1:T(8,128)} %fusion.94, bf16[1024,2816]{1,0:T(8,128)(2,1)} %get-tuple-element.67, bf16[2816,1024]{1,0:T(8,128)(2,1)} %bitcast.272), kind=kOutput, calls=%fused_computation.40 | convolution fusion | flops 5908724736 | bytes 24121344 | tf_op jit(solution)/shard_map/dot_general | solution.py:30
  323.5 8.7 %convolution_convert_fusion = bf16[2816,1024]{0,1:T(8,128)(2,1)S(1)} fusion(bf16[1024,2816]{1,0:T(8,128)(2,1)S(1)} %bitcast.261, bf16[1024,1024]{1,0:T(8,128)(2,1)} %param.21), kind=kOutput, calls=%fused_computation.23 | convolution fusion | flops 5908463616 | bytes 13631488 | tf_op jit(solution)/shard_map/dot_general | solution.py:40
  378.2 9.4 %add_convert_fusion = bf16[1024,1024]{0,1:T(8,128)(2,1)S(1)} fusion(f32[1024,1024]{0,1:T(8,128)S(1)} %copy-done.4, bf16[1024,2816]{1,0:T(8,128)(2,1)} %get-tuple-element.69, bf16[1024,1024]{1,0:T(8,128)(2,1)S(1)} %bitcast.290, bf16[1024,1024]{1,0:T(8,128)(2,1)} %bitcast.292, bf16[1024,1024]{1,0:T(8,128)(2,1)S(1)} %bitcast.288), kind=kOutput, calls=%fused_computation.41 | convolution fusion | flops 5924978688 | bytes 18350080 | tf_op jit(solution)/shard_map/dot_general | solution.py:34
  390.6 6.7 %fusion.97 = f32[1024,1024]{0,1:T(8,128)} fusion(bf16[1024,1024]{1,0:T(8,128)(2,1)} %get-tuple-element.78, bf16[1024,1024]{1,0:T(8,128)(2,1)} %bitcast.281), kind=kOutput, calls=%fused_computation.236 | convolution fusion | flops 2147483648 | bytes 8388608 | tf_op jit(solution)/shard_map/dot_general | solution.py:30
  401.1 19.5 %lightning_backward.1 = (bf16[1024,1024]{1,0:T(8,128)(2,1)}, bf16[1024,1024]{1,0:T(8,128)(2,1)}, bf16[1024,1024]{1,0:T(8,128)(2,1)}) custom-call(s32[1]{0:T(128)} %copy.115.count_ref, f32[8]{0:T(128)} %exponential_multiply_fusion.slope_ref, f32[1024,1024]{1,0:T(8,128)} %fusion.63.query_ref, f32[1024,1024]{1,0:T(8,128)} %fusion.61.key_ref, ...), custom_call_target="tpu_custom_call" | custom-call | tf_op jit(solution)/shard_map/lightning_backward/pallas_call | solution.py:188
  443.5 13.0 %collective-permute-done.5 = bf16[4,272,512]{2,1,0:T(8,128)(2,1)S(1)} collective-permute-done((bf16[4,272,512]{2,1,0:T(8,128)(2,1)S(1)}, bf16[4,272,512]{2,1,0:T(8,128)(2,1)S(1)}, u32[]{:S(2)}, u32[]{:S(2)}) %collective-permute-start.5) | collective-permute-done | bytes 1114144 | tf_op jit(solution)/shard_map/ppermute | solution.py:257
  491.0 8.4 %fusion.14 = (f32[1024]{0:T(1024)S(1)}, f32[1024,1024]{0,1:T(8,128)}) fusion(bf16[1024,1024]{0,1:T(8,128)(2,1)S(1)} %copy-done.7, f32[1024,1024]{0,1:T(8,128)S(1)} %copy-done.25, bf16[1024,1024]{1,0:T(8,128)(2,1)S(1)} %copy-done.31, bf16[1024,1024]{1,0:T(8,128)(2,1)S(1)} %bitcast.264, f32[1024,1024]{0,1:T(8,128)} %fusion.95, f32[1024,1024]{0,1:T(8,128)} %fusion.96), kind=kOutput, calls=%fused_computation.35 | convolution fusion | flops 2153774080 | bytes 23072768 | tf_op jit(solution)/shard_map/dot_general | solution.py:30
  502.7 15.9 %collective-permute-done.14 = bf16[2,4,160,512]{3,2,1,0:T(8,128)(2,1)S(1)} collective-permute-done((bf16[2,4,160,512]{3,2,1,0:T(8,128)(2,1)S(1)}, bf16[2,4,160,512]{3,2,1,0:T(8,128)(2,1)S(1)}, u32[]{:S(2)}, u32[]{:S(2)}) %collective-permute-start.14) | collective-permute-done | bytes 1310752 | tf_op jit(solution)/shard_map/ppermute | solution.py:257
  527.3 7.4 %collective-permute-done.15 = bf16[4,160,512]{2,1,0:T(8,128)(2,1)S(1)} collective-permute-done((bf16[4,160,512]{2,1,0:T(8,128)(2,1)S(1)}, bf16[4,160,512]{2,1,0:T(8,128)(2,1)S(1)}, u32[]{:S(2)}, u32[]{:S(2)}) %collective-permute-start.15) | collective-permute-done | bytes 655392 | tf_op jit(solution)/shard_map/ppermute | solution.py:257
  541.2 7.4 %fusion.11 = f32[1024,1024]{0,1:T(8,128)} fusion(bf16[1024,1024]{0,1:T(8,128)(2,1)S(1)} %copy-done.7, f32[1024,1024]{0,1:T(8,128)} %get-tuple-element.128, f32[1024]{0:T(1024)S(1)} %multiply_multiply_fusion.1, f32[1024]{0:T(1024)S(1)} %copy-done.48, f32[1024,1024]{0,1:T(8,128)S(1)} %copy-done.5, f32[1024]{0:T(1024)S(1)} %multiply_multiply_fusion.3, ...), kind=kLoop, calls=%fused_computation.32 | loop fusion | flops 12582912 | bytes 20987904 | tf_op jit(solution)/shard_map/add | solution.py:420
  548.6 5.3 copy.46
  563.7 5.6 collective-permute-start.18
  (272 shorter events, 204.5 us)
Async XLA Ops:
  7.2 94.1 %all-gather.3.cloned.1.call-start = ((), (), s32[]{:S(2)}) async-start(), calls=%async_computation | async-start | bytes 10813440 | tf_op jit(solution)/shard_map/all_gather | solution.py:212
  12.2 209.6 %all-gather.5.cloned.1.call-start = ((), (), s32[]{:S(2)}) async-start(), calls=%async_computation.1 | async-start | bytes 18382848 | tf_op jit(solution)/shard_map/all_gather | solution.py:212
  338.1 14.5 %collective-permute-start = (bf16[2,4,2,88,1024]{4,3,1,0,2:T(8,128)(2,1)}, bf16[2,4,2,88,1024]{4,3,1,0,2:T(8,128)(2,1)}, u32[]{:S(2)}, u32[]{:S(2)}) collective-permute-start(bf16[2,4,2,88,1024]{4,3,1,0,2:T(8,128)(2,1)} %bitcast.249), channel_id=1, source_target_pairs={{0,8},{8,0},{16,24},{24,16},{1,9},{9,1},{17,25},{25,17},{2,10},{10... | collective-permute-start | bytes 8650760 | tf_op jit(solution)/shard_map/ppermute | solution.py:257
  338.4 19.2 %collective-permute-start.2 = (bf16[2,4,2,32,2816]{4,3,1,0,2:T(8,128)(2,1)}, bf16[2,4,2,32,2816]{4,3,1,0,2:T(8,128)(2,1)S(1)}, u32[]{:S(2)}, u32[]{:S(2)}) collective-permute-start(bf16[2,4,2,32,2816]{4,3,1,0,2:T(8,128)(2,1)} %bitcast.275), channel_id=1, source_target_pairs={{0,8},{8,0},{16,24},{24,16},{1,9},{9,1},{17,25},{25,17},{2,10},{10... | collective-permute-start | bytes 8650760 | tf_op jit(solution)/shard_map/ppermute | solution.py:257
  338.7 19.8 %collective-permute-start.1 = (bf16[2,4,2,88,1024]{4,3,1,0,2:T(8,128)(2,1)}, bf16[2,4,2,88,1024]{4,3,1,0,2:T(8,128)(2,1)S(1)}, u32[]{:S(2)}, u32[]{:S(2)}) collective-permute-start(bf16[2,4,2,88,1024]{4,3,1,0,2:T(8,128)(2,1)} %bitcast.274), channel_id=1, source_target_pairs={{0,8},{8,0},{16,24},{24,16},{1,9},{9,1},{17,25},{25,17},{2,10},{10... | collective-permute-start | bytes 8650760 | tf_op jit(solution)/shard_map/ppermute | solution.py:257
  371.6 50.9 %collective-permute-start.4 = (bf16[2,4,272,512]{3,2,1,0:T(8,128)(2,1)}, bf16[2,4,272,512]{3,2,1,0:T(8,128)(2,1)}, u32[]{:S(2)}, u32[]{:S(2)}) collective-permute-start(bf16[2,4,272,512]{3,2,1,0:T(8,128)(2,1)} %dynamic-slice_bitcast_fusion), channel_id=1, source_target_pairs={{0,1},{1,0},{2,3},{3,2},{4,5},{5,4},{6,7},{7,6},{8,9},{9,8},{10,11... | collective-permute-start | bytes 6684680 | tf_op jit(solution)/shard_map/ppermute | solution.py:257
  376.6 50.9 %collective-permute-start.3 = (bf16[4,2,272,512]{3,2,0,1:T(8,128)(2,1)}, bf16[4,2,272,512]{3,2,0,1:T(8,128)(2,1)}, u32[]{:S(2)}, u32[]{:S(2)}) collective-permute-start(bf16[4,2,272,512]{3,2,0,1:T(8,128)(2,1)} %dynamic-slice_bitcast_fusion.1), channel_id=1, source_target_pairs={{0,16},{8,24},{16,0},{24,8},{1,17},{9,25},{17,1},{25,9},{2,18},{10... | collective-permute-start | bytes 6684680 | tf_op jit(solution)/shard_map/ppermute | solution.py:257
  430.6 25.9 %collective-permute-start.5 = (bf16[4,272,512]{2,1,0:T(8,128)(2,1)S(1)}, bf16[4,272,512]{2,1,0:T(8,128)(2,1)S(1)}, u32[]{:S(2)}, u32[]{:S(2)}) collective-permute-start(bf16[4,272,512]{2,1,0:T(8,128)(2,1)S(1)} %dynamic-slice_bitcast_fusion.5), channel_id=1, source_target_pairs={{0,1},{1,0},{2,3},{3,2},{4,5},{5,4},{6,7},{7,6},{8,9},{9,8},{10,11... | collective-permute-start | bytes 3342344 | tf_op jit(solution)/shard_map/ppermute | solution.py:257
  432.2 25.7 %collective-permute-start.6 = (bf16[4,272,512]{2,1,0:T(8,128)(2,1)S(1)}, bf16[4,272,512]{2,1,0:T(8,128)(2,1)S(1)}, u32[]{:S(2)}, u32[]{:S(2)}) collective-permute-start(bf16[4,272,512]{2,1,0:T(8,128)(2,1)S(1)} %dynamic-slice_bitcast_fusion.4), channel_id=1, source_target_pairs={{0,16},{8,24},{16,0},{24,8},{1,17},{9,25},{17,1},{25,9},{2,18},{10... | collective-permute-start | bytes 3342344 | tf_op jit(solution)/shard_map/ppermute | solution.py:257
  459.4 20.7 %collective-permute-start.7 = (bf16[2,4,2,32,1024]{4,3,1,0,2:T(8,128)(2,1)S(1)}, bf16[2,4,2,32,1024]{4,3,1,0,2:T(8,128)(2,1)S(1)}, u32[]{:S(2)}, u32[]{:S(2)}) collective-permute-start(bf16[2,4,2,32,1024]{4,3,1,0,2:T(8,128)(2,1)S(1)} %bitcast.293), channel_id=1, source_target_pairs={{0,8},{8,0},{16,24},{24,16},{1,9},{9,1},{17,25},{25,17},{2,10},{10... | collective-permute-start | bytes 3145736 | tf_op jit(solution)/shard_map/ppermute | solution.py:257
  466.5 13.5 %collective-permute-start.22 = (bf16[272,1024]{1,0:T(8,128)(2,1)S(1)}, bf16[272,1024]{1,0:T(8,128)(2,1)S(1)}, u32[]{:S(2)}, u32[]{:S(2)}) collective-permute-start(bf16[272,1024]{1,0:T(8,128)(2,1)S(1)} %get-tuple-element.89), channel_id=1, source_target_pairs={{0,2},{1,3},{8,10},{9,11},{16,18},{17,19},{24,26},{25,27}} | collective-permute-start | bytes 1671176 | tf_op jit(solution)/shard_map/ppermute | solution.py:250
  468.9 12.2 %collective-permute-start.8 = (bf16[2,4,2,32,1024]{4,3,1,0,2:T(8,128)(2,1)S(1)}, bf16[2,4,2,32,1024]{4,3,1,0,2:T(8,128)(2,1)S(1)}, u32[]{:S(2)}, u32[]{:S(2)}) collective-permute-start(bf16[2,4,2,32,1024]{4,3,1,0,2:T(8,128)(2,1)S(1)} %bitcast.297), channel_id=1, source_target_pairs={{0,8},{8,0},{16,24},{24,16},{1,9},{9,1},{17,25},{25,17},{2,10},{10... | collective-permute-start | bytes 3145736 | tf_op jit(solution)/shard_map/ppermute | solution.py:257
  469.0 17.0 %collective-permute-start.9 = (bf16[2,4,2,32,1024]{4,3,1,0,2:T(8,128)(2,1)S(1)}, bf16[2,4,2,32,1024]{4,3,1,0,2:T(8,128)(2,1)S(1)}, u32[]{:S(2)}, u32[]{:S(2)}) collective-permute-start(bf16[2,4,2,32,1024]{4,3,1,0,2:T(8,128)(2,1)S(1)} %bitcast.296), channel_id=1, source_target_pairs={{0,8},{8,0},{16,24},{24,16},{1,9},{9,1},{17,25},{25,17},{2,10},{10... | collective-permute-start | bytes 3145736 | tf_op jit(solution)/shard_map/ppermute | solution.py:257
  473.9 25.5 %collective-permute-start.25 = (bf16[272,1024]{1,0:T(8,128)(2,1)}, bf16[272,1024]{1,0:T(8,128)(2,1)}, u32[]{:S(2)}, u32[]{:S(2)}) collective-permute-start(bf16[272,1024]{1,0:T(8,128)(2,1)} %get-tuple-element.90), channel_id=1, source_target_pairs={{6,4},{7,5},{14,12},{15,13},{22,20},{23,21},{30,28},{31,29}} | collective-permute-start | bytes 1671176 | tf_op jit(solution)/shard_map/ppermute | solution.py:250
  481.2 18.2 %collective-permute-start.23 = (bf16[272,1024]{1,0:T(8,128)(2,1)S(1)}, bf16[272,1024]{1,0:T(8,128)(2,1)S(1)}, u32[]{:S(2)}, u32[]{:S(2)}) collective-permute-start(bf16[272,1024]{1,0:T(8,128)(2,1)S(1)} %fusion.32), channel_id=1, source_target_pairs={{0,2},{1,3},{2,4},{3,5},{8,10},{9,11},{10,12},{11,13},{16,18},{17,... | collective-permute-start | bytes 1671176 | tf_op jit(solution)/shard_map/ppermute | solution.py:250
  488.2 30.5 %collective-permute-start.14 = (bf16[2,4,160,512]{3,2,1,0:T(8,128)(2,1)S(1)}, bf16[2,4,160,512]{3,2,1,0:T(8,128)(2,1)S(1)}, u32[]{:S(2)}, u32[]{:S(2)}) collective-permute-start(bf16[2,4,160,512]{3,2,1,0:T(8,128)(2,1)S(1)} %dynamic-slice_bitcast_fusion.2), channel_id=1, source_target_pairs={{0,1},{1,0},{2,3},{3,2},{4,5},{5,4},{6,7},{7,6},{8,9},{9,8},{10,11... | collective-permute-start | bytes 3932168 | tf_op jit(solution)/shard_map/ppermute | solution.py:257
  488.9 30.8 %collective-permute-start.12 = (bf16[4,2,160,512]{3,2,0,1:T(8,128)(2,1)S(1)}, bf16[4,2,160,512]{3,2,0,1:T(8,128)(2,1)S(1)}, u32[]{:S(2)}, u32[]{:S(2)}) collective-permute-start(bf16[4,2,160,512]{3,2,0,1:T(8,128)(2,1)S(1)} %dynamic-slice_bitcast_fusion.3), channel_id=1, source_target_pairs={{0,16},{8,24},{16,0},{24,8},{1,17},{9,25},{17,1},{25,9},{2,18},{10... | collective-permute-start | bytes 3932168 | tf_op jit(solution)/shard_map/ppermute | solution.py:257
  501.8 23.0 %collective-permute-start.26 = (bf16[272,1024]{1,0:T(8,128)(2,1)S(1)}, bf16[272,1024]{1,0:T(8,128)(2,1)S(1)}, u32[]{:S(2)}, u32[]{:S(2)}) collective-permute-start(bf16[272,1024]{1,0:T(8,128)(2,1)S(1)} %get-tuple-element.88), channel_id=1, source_target_pairs={{4,2},{5,3},{6,4},{7,5},{12,10},{13,11},{14,12},{15,13},{20,18},{2... | collective-permute-start | bytes 1671176 | tf_op jit(solution)/shard_map/ppermute | solution.py:250
  519.1 15.6 %collective-permute-start.15 = (bf16[4,160,512]{2,1,0:T(8,128)(2,1)S(1)}, bf16[4,160,512]{2,1,0:T(8,128)(2,1)S(1)}, u32[]{:S(2)}, u32[]{:S(2)}) collective-permute-start(bf16[4,160,512]{2,1,0:T(8,128)(2,1)S(1)} %dynamic-slice_bitcast_fusion.6), channel_id=1, source_target_pairs={{0,16},{8,24},{16,0},{24,8},{1,17},{9,25},{17,1},{25,9},{2,18},{10... | collective-permute-start | bytes 1966088 | tf_op jit(solution)/shard_map/ppermute | solution.py:257
  520.2 15.3 %collective-permute-start.13 = (bf16[4,160,512]{2,1,0:T(8,128)(2,1)S(1)}, bf16[4,160,512]{2,1,0:T(8,128)(2,1)S(1)}, u32[]{:S(2)}, u32[]{:S(2)}) collective-permute-start(bf16[4,160,512]{2,1,0:T(8,128)(2,1)S(1)} %dynamic-slice_bitcast_fusion.7), channel_id=1, source_target_pairs={{0,1},{1,0},{2,3},{3,2},{4,5},{5,4},{6,7},{7,6},{8,9},{9,8},{10,11... | collective-permute-start | bytes 1966088 | tf_op jit(solution)/shard_map/ppermute | solution.py:257
  521.7 32.2 %collective-permute-start.24 = (bf16[272,1024]{1,0:T(8,128)(2,1)}, bf16[272,1024]{1,0:T(8,128)(2,1)}, u32[]{:S(2)}, u32[]{:S(2)}) collective-permute-start(bf16[272,1024]{1,0:T(8,128)(2,1)} %get-tuple-element.87), channel_id=1, source_target_pairs={{0,2},{1,3},{2,4},{3,5},{4,6},{5,7},{8,10},{9,11},{10,12},{11,13},... | collective-permute-start | bytes 1671176 | tf_op jit(solution)/shard_map/ppermute | solution.py:250
  525.8 28.1 %collective-permute-start.27 = (bf16[272,1024]{1,0:T(8,128)(2,1)}, bf16[272,1024]{1,0:T(8,128)(2,1)}, u32[]{:S(2)}, u32[]{:S(2)}) collective-permute-start(bf16[272,1024]{1,0:T(8,128)(2,1)} %fusion.31), channel_id=1, source_target_pairs={{2,0},{3,1},{4,2},{5,3},{6,4},{7,5},{10,8},{11,9},{12,10},{13,11},... | collective-permute-start | bytes 1671176 | tf_op jit(solution)/shard_map/ppermute | solution.py:250
  536.6 19.0 %collective-permute-start.16 = (bf16[160,1024]{1,0:T(8,128)(2,1)}, bf16[160,1024]{1,0:T(8,128)(2,1)}, u32[]{:S(2)}, u32[]{:S(2)}) collective-permute-start(bf16[160,1024]{1,0:T(8,128)(2,1)} %get-tuple-element.105), channel_id=1, source_target_pairs={{0,2},{1,3},{8,10},{9,11},{16,18},{17,19},{24,26},{25,27}} | collective-permute-start | bytes 983048 | tf_op jit(solution)/shard_map/ppermute | solution.py:250
  539.8 15.8 %collective-permute-start.19 = (bf16[160,1024]{1,0:T(8,128)(2,1)}, bf16[160,1024]{1,0:T(8,128)(2,1)}, u32[]{:S(2)}, u32[]{:S(2)}) collective-permute-start(bf16[160,1024]{1,0:T(8,128)(2,1)} %get-tuple-element.106), channel_id=1, source_target_pairs={{6,4},{7,5},{14,12},{15,13},{22,20},{23,21},{30,28},{31,29}} | collective-permute-start | bytes 983048 | tf_op jit(solution)/shard_map/ppermute | solution.py:250
  (64 other events, 759.5 us)
Sparse Core Ops, SparseCore 0:
  12.3 88.8 all-gather.2
  104.1 117.6 all-gather.4

commit v4 on v3

--- a/solution.py
+++ b/solution.py
@@ -207,24 +207,6 @@
     return jnp.split(matrix, matrix.shape[-1] // D, axis=-1)
 
 
-def gather_rows(matrices, shards):
-    pieces = [piece for matrix in matrices for piece in lane_rows(jnp.transpose(matrix))]
-    full = lax.all_gather(jnp.concatenate(pieces, axis=0), AXES, axis=0, tiled=True)
-    full = full.reshape(shards, -1, D)
-    gathered, start = [], 0
-    for matrix in matrices:
-        size, width = matrix.shape
-        count = -(-size // D)
-        columns = [
-            full[:, start + index * width : start + (index + 1) * width].reshape(shards * width, D)
-            for index in range(count)
-        ]
-        joined = columns[0] if count == 1 else jnp.concatenate(columns, axis=1)[:, :size]
-        gathered.append(joined)
-        start += count * width
-    return gathered
-
-
 def pick(parts, axis, index):
     return lax.dynamic_index_in_dim(parts, index, axis, keepdims=False)
 
@@ -276,6 +258,25 @@
         return add_low(own, rising, falling)
 
 
+    def paired(self, own, other, axis):
+        low = jnp.stack([own, other], axis=axis)
+        high = jnp.stack([other, own], axis=axis)
+        return jnp.where(self.place == 0, low, high)
+
+    def gather(self, shard, axis):
+        size = self.size
+        if size == 1:
+            return jnp.expand_dims(shard, axis)
+        if size == 2:
+            return self.paired(shard, self.swap(shard), axis)
+        rising, falling = [shard], [shard]
+        for step in range(1, size):
+            rising.append(self.move(rising[-1], 1, range(step - 1, size)))
+            falling.append(self.move(falling[-1], -1, range(size - step + 1)))
+        known = jnp.stack(rising[:0:-1] + falling, axis=axis)
+        return lax.dynamic_slice_in_dim(known, size - 1 - self.place, size, axis)
+
+
 def lines():
     rows = lax.axis_size("dp")
     columns = lax.axis_size("fsdp")
@@ -286,6 +287,50 @@
         Line("fsdp", short, 1),
         Line("fsdp", columns // short, short),
     )
+
+
+def packed(matrices):
+    return jnp.concatenate(
+        [piece for matrix in matrices for piece in lane_rows(jnp.transpose(matrix))], axis=0
+    )
+
+
+def unpacked(full, matrices, shards):
+    gathered, start = [], 0
+    for matrix in matrices:
+        size, width = matrix.shape
+        count = -(-size // D)
+        columns = [
+            full(start + index * width, start + (index + 1) * width).reshape(shards * width, D)
+            for index in range(count)
+        ]
+        joined = columns[0] if count == 1 else jnp.concatenate(columns, axis=1)[:, :size]
+        gathered.append(joined)
+        start += count * width
+    return gathered
+
+
+def gather_rows(matrices, shards):
+    full = lax.all_gather(packed(matrices), AXES, axis=0, tiled=True)
+    full = full.reshape(shards, -1, D)
+    return unpacked(lambda start, stop: full[:, start:stop], matrices, shards)
+
+
+def gather_stages(matrices, shards):
+    core, across, up, deep = lines()
+    shard = deep.gather(packed(matrices), 0)
+    left = up.gather(across.gather(shard[..., : D // 2], 0), 2)
+    right = across.gather(up.gather(shard[..., D // 2 :], 1), 0)
+    halves = [(half, core.swap(half)) for half in (left, right)]
+
+    def rows(start, stop):
+        pieces = [
+            core.paired(own[..., start:stop, :], other[..., start:stop, :], 1)
+            for own, other in halves
+        ]
+        return jnp.concatenate(pieces, axis=-1)
+
+    return unpacked(rows, matrices, shards)
 
 
 class Scatter:
@@ -316,7 +361,10 @@
         self.left = jnp.concatenate([self.left, self.right], axis=-1)
 
     def to_owner(self):
-        summed = self.deep.scatter(self.left, 0).astype(jnp.float32)
+        self.left = self.deep.scatter(self.left, 0)
+
+    def sums(self):
+        summed = self.left.astype(jnp.float32)
         outs, start = [], 0
         for size, width in zip(self.sizes, self.widths):
             count = -(-size // D)
@@ -328,6 +376,10 @@
             outs.append(jnp.transpose(joined))
             start += count * width
         return outs
+
+
+def tie(values):
+    return lax.optimization_barrier(values)
 
 
 def weight_term(left, right):
@@ -351,7 +403,8 @@
     query_t, key_t, value_t, gate_t, out_t = gather_rows(
         (query_weight, key_weight, value_weight, gate_weight, out_weight), shards
     )
-    first_t, second_t, down_t = gather_rows((first_weight, second_weight, down_weight), shards)
+    first_t, second_t = gather_stages((first_weight, second_weight), shards)
+    (down_t,) = gather_stages((down_weight,), shards)
     inputs_f = inputs.astype(jnp.float32)
     length = inputs.shape[0]
     mask = (lax.iota(jnp.int32, length) < lengths[0]).astype(jnp.float32)[:, None]
@@ -369,48 +422,55 @@
     first = back_dot(normed_two, first_t)
     second = back_dot(normed_two, second_t)
     product_low = (first * second * mask).astype(jnp.bfloat16)
-    result = mixed + back_dot(product_low, down_t)
-    product_grad = forward_dot(cotangent, down_t)
+    down = Scatter([weight_term(cotangent, product_low)])
+    upstream, product_low, down.sent = tie((cotangent, product_low, down.sent))
+    product_grad = forward_dot(upstream, down_t)
     first_low = (product_grad * second * mask).astype(jnp.bfloat16)
     second_low = (product_grad * first * mask).astype(jnp.bfloat16)
+    down.to_core()
+    first_low, second_low, down.left, down.right = tie(
+        (first_low, second_low, down.left, down.right)
+    )
+    pair = Scatter([weight_term(first_low, normed_two), weight_term(second_low, normed_two)])
+    first_low, second_low, pair.sent = tie((first_low, second_low, pair.sent))
     normed_two_grad = forward_dot(first_low, first_t) + forward_dot(second_low, second_t)
-    glu = Scatter(
-        [
-            weight_term(first_low, normed_two),
-            weight_term(second_low, normed_two),
-            weight_term(cotangent, product_low),
-        ]
+    pair.to_core()
+    down.to_first()
+    normed_two_grad, pair.left, pair.right, down.left, down.right = tie(
+        (normed_two_grad, pair.left, pair.right, down.left, down.right)
     )
     mixed_grad = cotangent.astype(jnp.float32) + norm_back(mixed, normed_two_grad)
     mixed_low = mixed_grad.astype(jnp.bfloat16)
-    mixed_low, glu.sent = lax.optimization_barrier((mixed_low, glu.sent))
-    glu.to_core()
     gated_grad = forward_dot(mixed_low, out_t)
     gate_low = (gated_grad * attended_norm * mask).astype(jnp.bfloat16)
     attended_low = norm_back(attended, gated_grad * gate_pre * mask).astype(jnp.bfloat16)
-    attended_low, glu.left, glu.right = lax.optimization_barrier(
-        (attended_low, glu.left, glu.right)
-    )
-    glu.to_first()
+    early = Scatter([weight_term(mixed_low, gated), weight_term(gate_low, normed)])
+    down.to_second()
+    attended_low, early.sent, down.left = tie((attended_low, early.sent, down.left))
     query_low, key_low, value_low = lightning_backward(
         lengths, query_pre, key_pre, value_pre, attended_low, tables
     )
-    query_low, key_low, value_low, glu.left, glu.right = lax.optimization_barrier(
-        (query_low, key_low, value_low, glu.left, glu.right)
+    early.to_core()
+    pair.to_first()
+    query_low, key_low, value_low, early.left, early.right, pair.left, pair.right = tie(
+        (query_low, key_low, value_low, early.left, early.right, pair.left, pair.right)
     )
     late = Scatter(
         [
-            weight_term(mixed_low, gated),
-            weight_term(gate_low, normed),
             weight_term(query_low, normed),
             weight_term(key_low, normed),
             weight_term(value_low, normed),
         ]
     )
-    glu.to_second()
-    late.sent, glu.left = lax.optimization_barrier((late.sent, glu.left))
+    down.to_owner()
+    pair.to_second()
+    query_low, key_low, value_low, gate_low, product_low, late.sent, pair.left, down.left = tie(
+        (query_low, key_low, value_low, gate_low, product_low, late.sent, pair.left, down.left)
+    )
     late.to_core()
-    first_sum, second_sum, down_sum = glu.to_owner()
+    early.to_first()
+    result = mixed + back_dot(product_low, down_t)
+    result, early.left, early.right = tie((result, early.left, early.right))
     normed_grad = (
         forward_dot(query_low, query_t)
         + forward_dot(key_low, key_t)
@@ -419,8 +479,15 @@
     )
     input_grad = mixed_grad + norm_back(inputs_f, normed_grad)
     late.to_first()
+    early.to_second()
+    pair.to_owner()
     late.to_second()
-    out_sum, gate_sum, query_sum, key_sum, value_sum = late.to_owner()
+    early.to_owner()
+    late.to_owner()
+    (down_sum,) = down.sums()
+    first_sum, second_sum = pair.sums()
+    out_sum, gate_sum = early.sums()
+    query_sum, key_sum, value_sum = late.sums()
     return (
         result.astype(jnp.bfloat16),
         input_grad,

time: 596 us -> 635 us (1.065)
  starting transfers between devices: 38.7 us -> 112 us
  waiting for transfers between devices: 202 us -> 162 us
  other arithmetic: 46.6 us -> 73 us
  matrix products: 160 us -> 144 us
    all_gather x2 -> x1, waiting for transfers between devices: 145 us -> 0.01 us  [gather_rows(): full = lax.all_gather(packed(matrices), AXES, axis=0, tiled=True)]
    ppermute x12 -> x36, waiting for transfers between devices: 15.1 us -> 78.8 us  [move(): return lax.ppermute(value, self.name, pairs)]
    ppermute x12 -> x36, starting transfers between devices: 27.3 us -> 82.4 us  [move(): return lax.ppermute(value, self.name, pairs)]
    ppermute x16 -> x36, waiting for transfers between devices: 42 us -> 83.2 us  [swap(): return lax.ppermute(value, self.name, pairs)]
    convert_element_type x14 -> x35, other arithmetic: 13.5 us -> 32.3 us  [add_low(): return total.astype(jnp.bfloat16)]
    ppermute x16 -> x36, starting transfers between devices: 11.3 us -> 29.1 us  [swap(): return lax.ppermute(value, self.name, pairs)]
    select_n x0 -> x19, other arithmetic: none -> 15.9 us  [paired(): return jnp.where(self.place == 0, low, high)]
    slice x4, local copies, waits for them, and re-layouts: 19.9 us -> 7.47 us  [the longest x1 6.31 us: gather_rows(): return unpacked(lambda start, stop: full[:, start:stop], matrices, shards)]
  transfers between devices with their start and end apart: 30 -> 73, of which waited for: 13 -> 28; matrix products, arithmetic and copies ran while one was open for 25% -> 33% of each run, Pallas kernels for 6% -> 3%
where the time goes in v4:
time: 635 us; the launch traced here: 630 us
  waiting for transfers between devices  162 us (26%)
  matrix products  144 us (23%)
  starting transfers between devices  112 us (18%)
  local copies, waits for them, and re-layouts  89.2 us (14%)
  other arithmetic  73 us (11%)
  Pallas kernels  33.4 us (5%)
  between operations  17.1 us (3%)
    ppermute x36, waiting for transfers between devices, swap(): return lax.ppermute(value, self.name, pairs)  83.2 us
    ppermute x36, starting transfers between devices, move(): return lax.ppermute(value, self.name, pairs)  82.4 us
    ppermute x36, waiting for transfers between devices, move(): return lax.ppermute(value, self.name, pairs)  78.8 us
    dot_general x8, matrix products, back_dot(): lax.dot_general(left, right, (((1,), (1,)), ((), ())), preferred_element_...  55.7 us
    dot_general x8, matrix products, forward_dot(): return jnp.dot(left, right, preferred_element_type=jnp.float32)  53.5 us
    unnamed x167, local copies, waits for them, and re-layouts  37.6 us
    dot_general x8, matrix products, weight_dot(): lax.dot_general(left, right, (((0,), (0,)), ((), ())), preferred_element_...  34.5 us
    convert_element_type x35, other arithmetic, add_low(): return total.astype(jnp.bfloat16)  32.3 us
  transfers between devices with their start and end apart: 73, of which 28 were waited for; matrix products, arithmetic and copies ran while one was open for 33% of the time, Pallas kernels for 3%

profile of v4, /device:TPU:0, one launch (start us, length us, event | category | flops | bytes accessed | tf_op | source)
XLA Modules:
  0.0 629.8 jit_solution(11274478780822490726)
XLA Ops:
  45.3 9.3 %collective-permute-done.16 = bf16[96,1024]{1,0:T(8,128)(2,1)S(1)} collective-permute-done((bf16[96,1024]{1,0:T(8,128)(2,1)}, bf16[96,1024]{1,0:T(8,128)(2,1)S(1)}, u32[]{:S(2)}, u32[]{:S(2)}) %collective-permute-start.16) | collective-permute-done | bytes 196640 | tf_op jit(solution)/shard_map/ppermute | solution.py:232
  59.6 16.1 %collective-permute-done.17 = bf16[96,1024]{1,0:T(8,128)(2,1)S(1)} collective-permute-done((bf16[96,1024]{1,0:T(8,128)(2,1)S(1)}, bf16[96,1024]{1,0:T(8,128)(2,1)S(1)}, u32[]{:S(2)}, u32[]{:S(2)}) %collective-permute-start.17) | collective-permute-done | bytes 196640 | tf_op jit(solution)/shard_map/ppermute | solution.py:232
  81.4 19.3 %collective-permute-done.5 = bf16[176,1024]{1,0:T(8,128)(2,1)S(1)} collective-permute-done((bf16[176,1024]{1,0:T(8,128)(2,1)S(1)}, bf16[176,1024]{1,0:T(8,128)(2,1)S(1)}, u32[]{:S(2)}, u32[]{:S(2)}) %collective-permute-start.5) | collective-permute-done | bytes 360480 | tf_op jit(solution)/shard_map/ppermute | solution.py:232
  124.7 6.3 collective-permute-done.9
  137.1 10.7 %collective-permute-done.19 = bf16[2,4,96,512]{3,2,1,0:T(8,128)(2,1)S(1)} collective-permute-done((bf16[2,4,96,512]{3,2,1,0:T(8,128)(2,1)S(1)}, bf16[2,4,96,512]{3,2,1,0:T(8,128)(2,1)S(1)}, u32[]{:S(2)}, u32[]{:S(2)}) %collective-permute-start.19) | collective-permute-done | bytes 786464 | tf_op jit(solution)/shard_map/ppermute | solution.py:239
  150.1 27.0 %collective-permute-done.7 = bf16[2,4,176,512]{3,2,1,0:T(8,128)(2,1)S(1)} collective-permute-done((bf16[2,4,176,512]{3,2,1,0:T(8,128)(2,1)S(1)}, bf16[2,4,176,512]{3,2,1,0:T(8,128)(2,1)S(1)}, u32[]{:S(2)}, u32[]{:S(2)}) %collective-permute-start.7) | collective-permute-done | bytes 1441824 | tf_op jit(solution)/shard_map/ppermute | solution.py:239
  195.9 6.3 %fusion.126 = (bf16[32,32,1024]{2,1,0:T(8,128)(2,1)}, bf16[32,32,1024]{2,1,0:T(8,128)(2,1)}, bf16[32,32,1024]{2,1,0:T(8,128)(2,1)S(1)}, bf16[32,32,1024]{2,1,0:T(8,128)(2,1)S(1)}, bf16[32,32,1024]{2,1,0:T(8,128)(2,1)S(1)}) fusion(bf16[32,160,1024]{2,1,0:T(8,128)(2,1)} %bitcast.429), kind=kLoop, calls=%fused_computation.379 | loop fusion | bytes 20971520 | tf_op jit(solution)/shard_map/slice | solution.py:316
  215.4 13.6 %lightning_forward.1 = f32[1024,1024]{1,0:T(8,128)} custom-call(s32[1]{0:T(128)} %copy.170.count_ref, f32[8]{0:T(128)} %exponential_multiply_fusion.slope_ref, f32[1024,1024]{1,0:T(8,128)} %fusion.80.query_ref, f32[1024,1024]{1,0:T(8,128)} %fusion.78.key_ref, f32[1024,1024]{1,0:T(8,128)} %fusion.76.value_ref, f32[1024,128]{1,0:T(8,128)} %get-tuple-element.214.cosine_ref, ...), custom_call_target="tpu_custom_call" | custom-call | tf_op jit(solution)/shard_map/lightning_forward/pallas_call | solution.py:175
  232.5 6.5 %multiply_convert_fusion.5 = (bf16[1024,1024]{1,0:T(8,128)(2,1)S(1)}, f32[1024,1024]{1,0:T(8,128)}) fusion(f32[1024,1024]{1,0:T(8,128)S(1)} %copy-done, f32[1024]{0:T(1024)S(1)} %fusion.118, f32[1024]{0:T(1024)S(1)} %fusion.120, bf16[1024,1024]{1,0:T(8,128)(2,1)} %bitcast.430, bf16[1024,1024]{0,1:T(8,128)(2,1)S(1)} %copy.48, f32[1024]{0:T(1024)S(1)} %fusion.119), kind=kOutput, calls=%fused_computation.41 | convolution fusion | flops 2154823680 | bytes 14692352 | tf_op jit(solution)/shard_map/dot_general | solution.py:34
  246.5 9.1 %fusion.14 = f32[1024,2816]{1,0:T(8,128)} fusion(bf16[1024,1024]{0,1:T(8,128)(2,1)S(1)} %multiply_convert_fusion.4, bf16[2816,512]{1,0:T(8,128)(2,1)S(1)} %bitcast.450, bf16[2816,512]{1,0:T(8,128)(2,1)S(1)} %bitcast.448), kind=kOutput, calls=%fused_computation.44 | convolution fusion | flops 5917114368 | bytes 19398656 | tf_op jit(solution)/shard_map/dot_general | solution.py:34
  255.6 15.2 %multiply_convert_fusion.2 = (bf16[1024,2816]{1,0:T(8,128)(2,1)}, f32[1024,2816]{1,0:T(8,128)}) fusion(f32[1024,2816]{1,0:T(8,128)} %fusion.14, f32[1024]{0:T(1024)S(1)} %fusion.118, bf16[1024,1024]{0,1:T(8,128)(2,1)} %copy-done.47, bf16[2816,512]{1,0:T(8,128)(2,1)S(1)} %bitcast.452, bf16[2816,512]{1,0:T(8,128)(2,1)S(1)} %bitcast.454), kind=kOutput, calls=%fused_computation.2 | convolution fusion | flops 5925765120 | bytes 36704256 | tf_op jit(solution)/shard_map/dot_general | solution.py:34
  270.8 9.1 %convolution_convert_fusion.2 = bf16[2816,1024]{0,1:T(8,128)(2,1)S(1)} fusion(bf16[1024,2816]{1,0:T(8,128)(2,1)} %get-tuple-element.81, bf16[1024,1024]{1,0:T(8,128)(2,1)S(1)} %copy-done.10), kind=kOutput, calls=%fused_computation.23 | convolution fusion | flops 5908463616 | bytes 13631488 | tf_op jit(solution)/shard_map/dot_general | solution.py:40
  289.0 15.2 %multiply_convert_fusion = (bf16[1024,2816]{1,0:T(8,128)(2,1)}, bf16[1024,2816]{1,0:T(8,128)(2,1)}) fusion(f32[1024,2816]{1,0:T(8,128)} %get-tuple-element.220, f32[1024]{0:T(1024)S(1)} %fusion.118, f32[1024,2816]{1,0:T(8,128)} %fusion.14, bf16[1024,1024]{1,0:T(8,128)(2,1)S(1)} %copy-done.10, bf16[1024,3072]{1,0:T(8,128)(2,1)} %constant_dynamic-update-slice_fusion), kind=kOutput, calls=%fused_computation | convolution fusion | flops 5922881536 | bytes 42471424 | tf_op jit(solution)/shard_map/dot_general | solution.py:30
  314.0 6.8 %convolution_convert_fusion = bf16[2816,1024]{1,0:T(8,128)(2,1)S(1)} fusion(bf16[1024,2816]{1,0:T(8,128)(2,1)S(1)} %bitcast.428, bf16[1024,1024]{0,1:T(8,128)(2,1)S(1)} %copy-done.48), kind=kOutput, calls=%fused_computation.21 | convolution fusion | flops 5908463616 | bytes 13631488 | tf_op jit(solution)/shard_map/dot_general | solution.py:40
  323.3 6.6 %convolution_convert_fusion.1 = bf16[2816,1024]{1,0:T(8,128)(2,1)S(1)} fusion(bf16[1024,2816]{1,0:T(8,128)(2,1)S(1)} %bitcast.426, bf16[1024,1024]{0,1:T(8,128)(2,1)S(1)} %copy-done.48), kind=kOutput, calls=%fused_computation.22 | convolution fusion | flops 5908463616 | bytes 13631488 | tf_op jit(solution)/shard_map/dot_general | solution.py:40
  333.0 10.9 %fusion.13 = f32[1024,1024]{0,1:T(8,128)} fusion(bf16[1024,2816]{1,0:T(8,128)(2,1)S(1)} %bitcast.428, bf16[2816,512]{1,0:T(8,128)(2,1)} %bitcast.449, bf16[2816,512]{1,0:T(8,128)(2,1)} %bitcast.447), kind=kOutput, calls=%fused_computation.43 | convolution fusion | flops 5917114368 | bytes 15728640 | tf_op jit(solution)/shard_map/dot_general | solution.py:30
  343.9 9.7 %fusion.20 = f32[1024,1024]{0,1:T(8,128)S(1)} fusion(f32[1024,1024]{0,1:T(8,128)} %fusion.13, bf16[1024,2816]{1,0:T(8,128)(2,1)S(1)} %bitcast.426, bf16[2816,512]{1,0:T(8,128)(2,1)} %bitcast.451, bf16[2816,512]{1,0:T(8,128)(2,1)} %bitcast.453), kind=kOutput, calls=%fused_computation.68 | convolution fusion | flops 5918162944 | bytes 19922944 | tf_op jit(solution)/shard_map/dot_general | solution.py:30
  421.1 19.8 %lightning_backward.1 = (bf16[1024,1024]{1,0:T(8,128)(2,1)}, bf16[1024,1024]{1,0:T(8,128)(2,1)}, bf16[1024,1024]{1,0:T(8,128)(2,1)}) custom-call(s32[1]{0:T(128)} %copy.170.count_ref, f32[8]{0:T(128)} %exponential_multiply_fusion.slope_ref, f32[1024,1024]{1,0:T(8,128)} %fusion.80.query_ref, f32[1024,1024]{1,0:T(8,128)} %fusion.78.key_ref, ...), custom_call_target="tpu_custom_call" | custom-call | tf_op jit(solution)/shard_map/lightning_backward/pallas_call | solution.py:188
  447.1 6.3 collective-permute-done.33
  473.6 9.7 %collective-permute-done.44 = bf16[2,4,64,512]{3,2,1,0:T(8,128)(2,1)S(1)} collective-permute-done((bf16[2,4,64,512]{3,2,1,0:T(8,128)(2,1)S(1)}, bf16[2,4,64,512]{3,2,1,0:T(8,128)(2,1)S(1)}, u32[]{:S(2)}, u32[]{:S(2)}) %collective-permute-start.44) | collective-permute-done | bytes 524320 | tf_op jit(solution)/shard_map/ppermute | solution.py:239
  491.7 9.3 %fusion.26 = bf16[1024,1024]{0,1:T(8,128)(2,1)} fusion(f32[1024,1024]{0,1:T(8,128)S(1)} %copy-done.6, bf16[1024,2816]{1,0:T(8,128)(2,1)S(1)} %bitcast.481, bf16[1024,3072]{1,0:T(8,128)(2,1)} %constant_dynamic-update-slice_fusion), kind=kOutput, calls=%fused_computation.81 | convolution fusion | flops 5907677184 | bytes 17825792 | tf_op jit(solution)/shard_map/dot_general | solution.py:34
  523.8 5.6 copy.91
  573.0 9.3 %collective-permute-done.48 = bf16[4,2,96,512]{3,2,0,1:T(8,128)(2,1)S(1)} collective-permute-done((bf16[4,2,96,512]{3,2,0,1:T(8,128)(2,1)S(1)}, bf16[4,2,96,512]{3,2,0,1:T(8,128)(2,1)S(1)}, u32[]{:S(2)}, u32[]{:S(2)}) %collective-permute-start.48) | collective-permute-done | bytes 786464 | tf_op jit(solution)/shard_map/ppermute | solution.py:239
  607.4 6.9 %collective-permute-start.54 = (bf16[96,1024]{1,0:T(8,128)(2,1)S(1)}, bf16[96,1024]{1,0:T(8,128)(2,1)S(1)}, u32[]{:S(2)}, u32[]{:S(2)}) collective-permute-start(bf16[96,1024]{1,0:T(8,128)(2,1)S(1)} %get-tuple-element.182), channel_id=1, source_target_pairs={{0,2},{1,3},{2,4},{3,5},{4,6},{5,7},{8,10},{9,11},{10,12},{11,13},... | collective-permute-start | bytes 589832 | tf_op jit(solution)/shard_map/ppermute | solution.py:232
  (473 shorter events, 348.0 us)
Async XLA Ops:
  7.2 188.7 %all-gather.2.cloned.1.call-start = ((), (), s32[]{:S(2)}) async-start(), calls=%async_computation | async-start | bytes 10813440 | tf_op jit(solution)/shard_map/all_gather | solution.py:314
  13.2 30.1 %collective-permute-start = (bf16[176,1024]{1,0:T(8,128)(2,1)S(1)}, bf16[176,1024]{1,0:T(8,128)(2,1)S(1)}, u32[]{:S(2)}, u32[]{:S(2)}) collective-permute-start(bf16[176,1024]{1,0:T(8,128)(2,1)S(1)} %pad_maximum_fusion.20), channel_id=1, source_target_pairs={{0,2},{1,3},{2,4},{3,5},{4,6},{5,7},{8,10},{9,11},{10,12},{11,13},... | collective-permute-start | bytes 1081352 | tf_op jit(solution)/shard_map/ppermute | solution.py:232
  44.0 35.7 %collective-permute-start.4 = (bf16[176,1024]{1,0:T(8,128)(2,1)S(1)}, bf16[176,1024]{1,0:T(8,128)(2,1)S(1)}, u32[]{:S(2)}, u32[]{:S(2)}) collective-permute-start(bf16[176,1024]{1,0:T(8,128)(2,1)S(1)} %collective-permute-done.3), channel_id=1, source_target_pairs={{2,0},{3,1},{4,2},{5,3},{10,8},{11,9},{12,10},{13,11},{18,16},{19,... | collective-permute-start | bytes 1081352 | tf_op jit(solution)/shard_map/ppermute | solution.py:232
  76.6 33.1 %collective-permute-start.21 = (bf16[4,96,512]{2,1,0:T(8,128)(2,1)}, bf16[4,96,512]{2,1,0:T(8,128)(2,1)}, u32[]{:S(2)}, u32[]{:S(2)}) collective-permute-start(bf16[4,96,512]{2,1,0:T(8,128)(2,1)} %get-tuple-element.180), channel_id=1, source_target_pairs={{0,1},{1,0},{2,3},{3,2},{4,5},{5,4},{6,7},{7,6},{8,9},{9,8},{10,11... | collective-permute-start | bytes 1179656 | tf_op jit(solution)/shard_map/ppermute | solution.py:239
  78.2 35.3 %collective-permute-start.18 = (bf16[4,96,512]{2,1,0:T(8,128)(2,1)}, bf16[4,96,512]{2,1,0:T(8,128)(2,1)}, u32[]{:S(2)}, u32[]{:S(2)}) collective-permute-start(bf16[4,96,512]{2,1,0:T(8,128)(2,1)} %get-tuple-element.181), channel_id=1, source_target_pairs={{0,16},{8,24},{16,0},{24,8},{1,17},{9,25},{17,1},{25,9},{2,18},{10... | collective-permute-start | bytes 1179656 | tf_op jit(solution)/shard_map/ppermute | solution.py:239
  115.1 32.7 %collective-permute-start.19 = (bf16[2,4,96,512]{3,2,1,0:T(8,128)(2,1)S(1)}, bf16[2,4,96,512]{3,2,1,0:T(8,128)(2,1)S(1)}, u32[]{:S(2)}, u32[]{:S(2)}) collective-permute-start(bf16[2,4,96,512]{3,2,1,0:T(8,128)(2,1)S(1)} %maximum_select_fusion.17), channel_id=1, source_target_pairs={{0,1},{1,0},{2,3},{3,2},{4,5},{5,4},{6,7},{7,6},{8,9},{9,8},{10,11... | collective-permute-start | bytes 2359304 | tf_op jit(solution)/shard_map/ppermute | solution.py:239
  121.6 55.5 %collective-permute-start.7 = (bf16[2,4,176,512]{3,2,1,0:T(8,128)(2,1)S(1)}, bf16[2,4,176,512]{3,2,1,0:T(8,128)(2,1)S(1)}, u32[]{:S(2)}, u32[]{:S(2)}) collective-permute-start(bf16[2,4,176,512]{3,2,1,0:T(8,128)(2,1)S(1)} %maximum_select_fusion.7), channel_id=1, source_target_pairs={{0,1},{1,0},{2,3},{3,2},{4,5},{5,4},{6,7},{7,6},{8,9},{9,8},{10,11... | collective-permute-start | bytes 4325384 | tf_op jit(solution)/shard_map/ppermute | solution.py:239
  131.3 46.5 %collective-permute-start.10 = (bf16[4,2,176,512]{3,2,0,1:T(8,128)(2,1)S(1)}, bf16[4,2,176,512]{3,2,0,1:T(8,128)(2,1)S(1)}, u32[]{:S(2)}, u32[]{:S(2)}) collective-permute-start(bf16[4,2,176,512]{3,2,0,1:T(8,128)(2,1)S(1)} %maximum_select_fusion.9), channel_id=1, source_target_pairs={{0,16},{8,24},{16,0},{24,8},{1,17},{9,25},{17,1},{25,9},{2,18},{10... | collective-permute-start | bytes 4325384 | tf_op jit(solution)/shard_map/ppermute | solution.py:239
  137.1 44.2 %collective-permute-start.23 = (bf16[2,4,2,96,512]{4,3,2,1,0:T(8,128)(2,1)S(1)}, bf16[2,4,2,96,512]{4,3,2,1,0:T(8,128)(2,1)S(1)}, u32[]{:S(2)}, u32[]{:S(2)}) collective-permute-start(bf16[2,4,2,96,512]{4,3,2,1,0:T(8,128)(2,1)S(1)} %maximum_select_fusion.6), channel_id=1, source_target_pairs={{0,8},{8,0},{16,24},{24,16},{1,9},{9,1},{17,25},{25,17},{2,10},{10... | collective-permute-start | bytes 4718600 | tf_op jit(solution)/shard_map/ppermute | solution.py:239
  148.3 31.3 %collective-permute-start.20 = (bf16[2,4,2,96,512]{4,3,2,1,0:T(8,128)(2,1)S(1)}, bf16[2,4,2,96,512]{4,3,2,1,0:T(8,128)(2,1)S(1)}, u32[]{:S(2)}, u32[]{:S(2)}) collective-permute-start(bf16[2,4,2,96,512]{4,3,2,1,0:T(8,128)(2,1)S(1)} %copy_select_fusion), channel_id=1, source_target_pairs={{0,8},{8,0},{16,24},{24,16},{1,9},{9,1},{17,25},{25,17},{2,10},{10... | collective-permute-start | bytes 4718600 | tf_op jit(solution)/shard_map/ppermute | solution.py:239
  310.1 43.6 %collective-permute-start.28 = (bf16[2,4,96,512]{3,2,1,0:T(8,128)(2,1)}, bf16[2,4,96,512]{3,2,1,0:T(8,128)(2,1)}, u32[]{:S(2)}, u32[]{:S(2)}) collective-permute-start(bf16[2,4,96,512]{3,2,1,0:T(8,128)(2,1)} %dynamic-slice_bitcast_fusion.4), channel_id=1, source_target_pairs={{0,1},{1,0},{2,3},{3,2},{4,5},{5,4},{6,7},{7,6},{8,9},{9,8},{10,11... | collective-permute-start | bytes 2359304 | tf_op jit(solution)/shard_map/ppermute | solution.py:239
  312.6 42.9 %collective-permute-start.27 = (bf16[4,2,96,512]{3,2,0,1:T(8,128)(2,1)}, bf16[4,2,96,512]{3,2,0,1:T(8,128)(2,1)}, u32[]{:S(2)}, u32[]{:S(2)}) collective-permute-start(bf16[4,2,96,512]{3,2,0,1:T(8,128)(2,1)} %dynamic-slice_bitcast_fusion.5), channel_id=1, source_target_pairs={{0,16},{8,24},{16,0},{24,8},{1,17},{9,25},{17,1},{25,9},{2,18},{10... | collective-permute-start | bytes 2359304 | tf_op jit(solution)/shard_map/ppermute | solution.py:239
  400.6 40.4 %collective-permute-start.31 = (bf16[2,4,2,32,1024]{4,3,1,0,2:T(8,128)(2,1)}, bf16[2,4,2,32,1024]{4,3,1,0,2:T(8,128)(2,1)}, u32[]{:S(2)}, u32[]{:S(2)}) collective-permute-start(bf16[2,4,2,32,1024]{4,3,1,0,2:T(8,128)(2,1)} %bitcast.472), channel_id=1, source_target_pairs={{0,8},{8,0},{16,24},{24,16},{1,9},{9,1},{17,25},{25,17},{2,10},{10... | collective-permute-start | bytes 3145736 | tf_op jit(solution)/shard_map/ppermute | solution.py:239
  409.0 36.1 %collective-permute-start.34 = (bf16[2,4,176,512]{3,2,1,0:T(8,128)(2,1)}, bf16[2,4,176,512]{3,2,1,0:T(8,128)(2,1)}, u32[]{:S(2)}, u32[]{:S(2)}) collective-permute-start(bf16[2,4,176,512]{3,2,1,0:T(8,128)(2,1)} %dynamic-slice_bitcast_fusion), channel_id=1, source_target_pairs={{0,1},{1,0},{2,3},{3,2},{4,5},{5,4},{6,7},{7,6},{8,9},{9,8},{10,11... | collective-permute-start | bytes 4325384 | tf_op jit(solution)/shard_map/ppermute | solution.py:239
  409.8 33.2 %collective-permute-start.32 = (bf16[2,4,2,32,1024]{4,3,1,0,2:T(8,128)(2,1)}, bf16[2,4,2,32,1024]{4,3,1,0,2:T(8,128)(2,1)}, u32[]{:S(2)}, u32[]{:S(2)}) collective-permute-start(bf16[2,4,2,32,1024]{4,3,1,0,2:T(8,128)(2,1)} %bitcast.471), channel_id=1, source_target_pairs={{0,8},{8,0},{16,24},{24,16},{1,9},{9,1},{17,25},{25,17},{2,10},{10... | collective-permute-start | bytes 3145736 | tf_op jit(solution)/shard_map/ppermute | solution.py:239
  419.9 33.5 %collective-permute-start.33 = (bf16[4,2,176,512]{3,2,0,1:T(8,128)(2,1)}, bf16[4,2,176,512]{3,2,0,1:T(8,128)(2,1)}, u32[]{:S(2)}, u32[]{:S(2)}) collective-permute-start(bf16[4,2,176,512]{3,2,0,1:T(8,128)(2,1)} %dynamic-slice_bitcast_fusion.1), channel_id=1, source_target_pairs={{0,16},{8,24},{16,0},{24,8},{1,17},{9,25},{17,1},{25,9},{2,18},{10... | collective-permute-start | bytes 4325384 | tf_op jit(solution)/shard_map/ppermute | solution.py:239
  455.2 29.4 %collective-permute-start.35 = (bf16[4,176,512]{2,1,0:T(8,128)(2,1)S(1)}, bf16[4,176,512]{2,1,0:T(8,128)(2,1)S(1)}, u32[]{:S(2)}, u32[]{:S(2)}) collective-permute-start(bf16[4,176,512]{2,1,0:T(8,128)(2,1)S(1)} %dynamic-slice_bitcast_fusion.7), channel_id=1, source_target_pairs={{0,1},{1,0},{2,3},{3,2},{4,5},{5,4},{6,7},{7,6},{8,9},{9,8},{10,11... | collective-permute-start | bytes 2162696 | tf_op jit(solution)/shard_map/ppermute | solution.py:239
  456.6 28.2 %collective-permute-start.36 = (bf16[4,176,512]{2,1,0:T(8,128)(2,1)S(1)}, bf16[4,176,512]{2,1,0:T(8,128)(2,1)S(1)}, u32[]{:S(2)}, u32[]{:S(2)}) collective-permute-start(bf16[4,176,512]{2,1,0:T(8,128)(2,1)S(1)} %dynamic-slice_bitcast_fusion.6), channel_id=1, source_target_pairs={{0,16},{8,24},{16,0},{24,8},{1,17},{9,25},{17,1},{25,9},{2,18},{10... | collective-permute-start | bytes 2162696 | tf_op jit(solution)/shard_map/ppermute | solution.py:239
  486.2 49.7 %collective-permute-start.66 = (bf16[176,1024]{1,0:T(8,128)(2,1)}, bf16[176,1024]{1,0:T(8,128)(2,1)}, u32[]{:S(2)}, u32[]{:S(2)}) collective-permute-start(bf16[176,1024]{1,0:T(8,128)(2,1)} %get-tuple-element.178), channel_id=1, source_target_pairs={{0,2},{1,3},{8,10},{9,11},{16,18},{17,19},{24,26},{25,27}} | collective-permute-start | bytes 1081352 | tf_op jit(solution)/shard_map/ppermute | solution.py:232
  501.8 30.1 %collective-permute-start.59 = (bf16[4,64,512]{2,1,0:T(8,128)(2,1)}, bf16[4,64,512]{2,1,0:T(8,128)(2,1)}, u32[]{:S(2)}, u32[]{:S(2)}) collective-permute-start(bf16[4,64,512]{2,1,0:T(8,128)(2,1)} %dynamic-slice_bitcast_fusion.16), channel_id=1, source_target_pairs={{0,16},{8,24},{16,0},{24,8},{1,17},{9,25},{17,1},{25,9},{2,18},{10... | collective-permute-start | bytes 786440 | tf_op jit(solution)/shard_map/ppermute | solution.py:239
  503.3 29.9 %collective-permute-start.58 = (bf16[4,64,512]{2,1,0:T(8,128)(2,1)}, bf16[4,64,512]{2,1,0:T(8,128)(2,1)}, u32[]{:S(2)}, u32[]{:S(2)}) collective-permute-start(bf16[4,64,512]{2,1,0:T(8,128)(2,1)} %dynamic-slice_bitcast_fusion.17), channel_id=1, source_target_pairs={{0,1},{1,0},{2,3},{3,2},{4,5},{5,4},{6,7},{7,6},{8,9},{9,8},{10,11... | collective-permute-start | bytes 786440 | tf_op jit(solution)/shard_map/ppermute | solution.py:239
  504.5 40.1 %collective-permute-start.45 = (bf16[2,4,2,32,1024]{4,3,1,0,2:T(8,128)(2,1)}, bf16[2,4,2,32,1024]{4,3,1,0,2:T(8,128)(2,1)}, u32[]{:S(2)}, u32[]{:S(2)}) collective-permute-start(bf16[2,4,2,32,1024]{4,3,1,0,2:T(8,128)(2,1)} %bitcast.421), channel_id=1, source_target_pairs={{0,8},{8,0},{16,24},{24,16},{1,9},{9,1},{17,25},{25,17},{2,10},{10... | collective-permute-start | bytes 3145736 | tf_op jit(solution)/shard_map/ppermute | solution.py:239
  504.5 45.6 %collective-permute-start.46 = (bf16[2,4,2,32,1024]{4,3,1,0,2:T(8,128)(2,1)}, bf16[2,4,2,32,1024]{4,3,1,0,2:T(8,128)(2,1)}, u32[]{:S(2)}, u32[]{:S(2)}) collective-permute-start(bf16[2,4,2,32,1024]{4,3,1,0,2:T(8,128)(2,1)} %bitcast.420), channel_id=1, source_target_pairs={{0,8},{8,0},{16,24},{24,16},{1,9},{9,1},{17,25},{25,17},{2,10},{10... | collective-permute-start | bytes 3145736 | tf_op jit(solution)/shard_map/ppermute | solution.py:239
  567.3 37.4 %collective-permute-start.68 = (bf16[176,1024]{1,0:T(8,128)(2,1)S(1)}, bf16[176,1024]{1,0:T(8,128)(2,1)S(1)}, u32[]{:S(2)}, u32[]{:S(2)}) collective-permute-start(bf16[176,1024]{1,0:T(8,128)(2,1)S(1)} %get-tuple-element.176), channel_id=1, source_target_pairs={{0,2},{1,3},{2,4},{3,5},{4,6},{5,7},{8,10},{9,11},{10,12},{11,13},... | collective-permute-start | bytes 1081352 | tf_op jit(solution)/shard_map/ppermute | solution.py:232
  (121 other events, 1673.6 us)
Sparse Core Ops, SparseCore 0:
  12.3 107.4 all-gather.1

commit v5 on v3

--- a/solution.py
+++ b/solution.py
@@ -198,6 +198,7 @@
 
 
 AXES = ("dp", "fsdp")
+ROWS = 24
 
 
 def lane_rows(matrix):
@@ -207,16 +208,67 @@
     return jnp.split(matrix, matrix.shape[-1] // D, axis=-1)
 
 
-def gather_rows(matrices, shards):
-    pieces = [piece for matrix in matrices for piece in lane_rows(jnp.transpose(matrix))]
-    full = lax.all_gather(jnp.concatenate(pieces, axis=0), AXES, axis=0, tiled=True)
-    full = full.reshape(shards, -1, D)
+def pick(parts, axis, index):
+    return lax.dynamic_index_in_dim(parts, index, axis, keepdims=False)
+
+
+def add_low(*pieces):
+    total = pieces[0].astype(jnp.float32)
+    for piece in pieces[1:]:
+        total = total + piece.astype(jnp.float32)
+    return total.astype(jnp.bfloat16)
+
+
+class Bit:
+    def __init__(self, name, stride):
+        self.name, self.stride = name, stride
+        self.place = lax.axis_index(name) // stride % 2
+
+    def swap(self, value):
+        members = lax.axis_size(self.name)
+        pairs = [(source, source ^ self.stride) for source in range(members)]
+        return lax.ppermute(value, self.name, pairs)
+
+    def paired(self, own, other, axis):
+        low = jnp.stack([own, other], axis=axis)
+        high = jnp.stack([other, own], axis=axis)
+        return jnp.where(self.place == 0, low, high)
+
+
+class Cube:
+    def __init__(self):
+        rows = lax.axis_size("dp")
+        columns = lax.axis_size("fsdp")
+        short = 1 << ((columns.bit_length() - 1) // 2)
+        strides = [("dp", 1 << digit) for digit in reversed(range(rows.bit_length() - 1))]
+        strides += [("fsdp", 1 << digit) for digit in reversed(range(columns.bit_length() - 1))]
+        self.bits = [Bit(name, stride) for name, stride in strides]
+        labels = {key: index for index, key in enumerate(strides)}
+        self.core = labels[("dp", 1)]
+        across = [labels[key] for key in reversed(strides) if key[0] == "dp" and key[1] > 1]
+        up = [labels[key] for key in reversed(strides) if key[0] == "fsdp" and key[1] < short]
+        deep = [labels[("fsdp", short)]]
+        self.far = [labels[key] for key in reversed(strides) if key[0] == "fsdp" and key[1] > short]
+        self.streams = [across + up + deep, up + deep + across, deep + across + up]
+        self.cuts = [0, 3 * D // 8, 6 * D // 8, D]
+
+    def columns(self, value):
+        return [value[..., low:high] for low, high in zip(self.cuts, self.cuts[1:])]
+
+
+def packed(matrices):
+    return jnp.concatenate(
+        [piece for matrix in matrices for piece in lane_rows(jnp.transpose(matrix))], axis=0
+    )
+
+
+def unpacked(full, matrices, shards):
     gathered, start = [], 0
     for matrix in matrices:
         size, width = matrix.shape
         count = -(-size // D)
         columns = [
-            full[:, start + index * width : start + (index + 1) * width].reshape(shards * width, D)
+            full(start + index * width, start + (index + 1) * width).reshape(shards * width, D)
             for index in range(count)
         ]
         joined = columns[0] if count == 1 else jnp.concatenate(columns, axis=1)[:, :size]
@@ -225,109 +277,109 @@
     return gathered
 
 
-def pick(parts, axis, index):
-    return lax.dynamic_index_in_dim(parts, index, axis, keepdims=False)
-
-
-def add_low(*pieces):
-    total = pieces[0].astype(jnp.float32)
-    for piece in pieces[1:]:
-        total = total + piece.astype(jnp.float32)
-    return total.astype(jnp.bfloat16)
-
-
-class Line:
-    def __init__(self, name, size, inner):
-        self.name, self.size, self.inner = name, size, inner
-        self.place = lax.axis_index(name) // inner % size
-
-    def move(self, value, shift, allowed):
-        pairs = []
-        for source in range(lax.axis_size(self.name)):
-            place = source // self.inner % self.size
-            if place in allowed and 0 <= place + shift < self.size:
-                pairs.append((source, source + shift * self.inner))
-        return lax.ppermute(value, self.name, pairs)
-
-    def swap(self, value):
-        pairs = []
-        for source in range(lax.axis_size(self.name)):
-            place = source // self.inner % self.size
-            pairs.append((source, source + (1 - 2 * place) * self.inner))
-        return lax.ppermute(value, self.name, pairs)
-
-    def scatter(self, parts, axis):
-        size = self.size
-        if size == 1:
-            return pick(parts, axis, 0)
-        own = pick(parts, axis, self.place)
-        if size == 2:
-            return add_low(own, self.swap(pick(parts, axis, 1 - self.place)))
-        rising = pick(parts, axis, jnp.minimum(self.place + size - 1, size - 1))
-        falling = pick(parts, axis, jnp.maximum(self.place - size + 1, 0))
-        for step in range(1, size):
-            rising = self.move(rising, 1, range(step))
-            falling = self.move(falling, -1, range(size - step, size))
-            if step < size - 1:
-                up = jnp.minimum(self.place + size - step - 1, size - 1)
-                down = jnp.maximum(self.place - size + step + 1, 0)
-                rising = add_low(pick(parts, axis, up), rising)
-                falling = add_low(pick(parts, axis, down), falling)
-        return add_low(own, rising, falling)
-
-
-def lines():
-    rows = lax.axis_size("dp")
-    columns = lax.axis_size("fsdp")
-    short = 1 << ((columns.bit_length() - 1) // 2)
-    return (
-        Line("dp", 2, 1),
-        Line("dp", rows // 2, 2),
-        Line("fsdp", short, 1),
-        Line("fsdp", columns // short, short),
-    )
+def gather_rows(matrices, shards):
+    full = lax.all_gather(packed(matrices), AXES, axis=0, tiled=True)
+    full = full.reshape(shards, -1, D)
+    return unpacked(lambda start, stop: full[:, start:stop], matrices, shards)
+
+
+class Gather:
+    def __init__(self, matrices):
+        self.matrices = matrices
+        self.cube = Cube()
+        value, self.known = packed(matrices), []
+        for label in reversed(self.cube.far):
+            value = self.join(value, label, self.known)
+            self.known = sorted(self.known + [label])
+        self.parts = self.cube.columns(value)
+        self.done = 0
+
+    def join(self, value, label, known):
+        bit = self.cube.bits[label]
+        axis = sum(other < label for other in known)
+        return bit.paired(value, bit.swap(value), axis)
+
+    def advance(self, stages):
+        for stage in range(self.done, self.done + stages):
+            for index, stream in enumerate(self.cube.streams):
+                order = stream[::-1]
+                known = self.known + order[:stage]
+                self.parts[index] = self.join(self.parts[index], order[stage], known)
+        self.done += stages
+
+    def finish(self, shards):
+        bit = self.cube.bits[self.cube.core]
+        axis = self.cube.core
+        halves = [(part, bit.swap(part)) for part in self.parts]
+
+        def rows(start, stop):
+            pieces = [
+                bit.paired(own[..., start:stop, :], other[..., start:stop, :], axis)
+                for own, other in halves
+            ]
+            return jnp.concatenate(pieces, axis=-1)
+
+        return unpacked(rows, self.matrices, shards)
 
 
 class Scatter:
     def __init__(self, terms):
-        self.core, self.across, self.up, self.deep = lines()
-        self.sizes = [term.shape[1] for term in terms]
-        blocks = [
-            term.reshape(self.across.size, 2, self.deep.size, self.up.size, -1, term.shape[1])
-            for term in terms
+        self.cube = Cube()
+        digits = len(self.cube.bits)
+        bit = self.cube.bits[self.cube.core]
+        blocks = [term.reshape((2,) * digits + (-1, D)) for term in terms]
+        self.own = [pick(block, self.cube.core, bit.place) for block in blocks]
+        self.sent = [pick(block, self.cube.core, 1 - bit.place) for block in blocks]
+
+    def meet(self, value, label, left):
+        bit = self.cube.bits[label]
+        axis = sum(other < label for other in left)
+        return add_low(pick(value, axis, bit.place), bit.swap(pick(value, axis, 1 - bit.place)))
+
+    def finish(self):
+        bit = self.cube.bits[self.cube.core]
+        sums = [add_low(own, bit.swap(sent)) for own, sent in zip(self.own, self.sent)]
+        parts = self.cube.columns(jnp.stack(sums, axis=-3))
+        for stage in range(len(self.cube.streams[0])):
+            for index, stream in enumerate(self.cube.streams):
+                left = self.cube.far + stream[stage:]
+                parts[index] = self.meet(parts[index], stream[stage], left)
+        value = jnp.concatenate(parts, axis=-1)
+        for position, label in enumerate(self.cube.far):
+            value = self.meet(value, label, self.cube.far[position:])
+        return [jnp.transpose(value[index].astype(jnp.float32)) for index in range(len(sums))]
+
+
+def scatter_call(terms, shards):
+    pieces, widths = [], []
+    for term in terms:
+        size = term.shape[1]
+        block = term.reshape(shards, -1, size)
+        widths.append((size, block.shape[1]))
+        pieces += lane_rows(block)
+    rows = sum(piece.shape[1] for piece in pieces)
+    if rows % ROWS:
+        pieces.append(jnp.zeros((shards, -rows % ROWS, D), pieces[0].dtype))
+    return jnp.concatenate(pieces, axis=1).reshape(-1, D), widths
+
+
+def scatter_sums(stacked, widths):
+    summed = lax.psum_scatter(stacked, AXES, scatter_dimension=0, tiled=True)
+    summed = summed.astype(jnp.float32)
+    outs, start = [], 0
+    for size, width in widths:
+        count = -(-size // D)
+        columns = [
+            summed[start + index * width : start + (index + 1) * width] for index in range(count)
         ]
-        self.widths = [block.shape[4] for block in blocks]
-        self.own = [pick(block, 1, self.core.place) for block in blocks]
-        self.sent = [pick(block, 1, 1 - self.core.place) for block in blocks]
-
-    def to_core(self):
-        sums = [add_low(own, self.core.swap(sent)) for own, sent in zip(self.own, self.sent)]
-        pieces = [piece for total in sums for piece in lane_rows(total)]
-        parts = jnp.concatenate(pieces, axis=-2)
-        self.left, self.right = parts[..., : D // 2], parts[..., D // 2 :]
-
-    def to_first(self):
-        self.left = self.across.scatter(self.left, 0)
-        self.right = self.up.scatter(self.right, 2)
-
-    def to_second(self):
-        self.left = self.up.scatter(self.left, 1)
-        self.right = self.across.scatter(self.right, 0)
-        self.left = jnp.concatenate([self.left, self.right], axis=-1)
-
-    def to_owner(self):
-        summed = self.deep.scatter(self.left, 0).astype(jnp.float32)
-        outs, start = [], 0
-        for size, width in zip(self.sizes, self.widths):
-            count = -(-size // D)
-            columns = [
-                summed[start + index * width : start + (index + 1) * width]
-                for index in range(count)
-            ]
-            joined = columns[0] if count == 1 else jnp.concatenate(columns, axis=1)[:, :size]
-            outs.append(jnp.transpose(joined))
-            start += count * width
-        return outs
+        joined = columns[0] if count == 1 else jnp.concatenate(columns, axis=1)[:, :size]
+        outs.append(jnp.transpose(joined))
+        start += count * width
+    return outs
+
+
+def tie(values):
+    return lax.optimization_barrier(values)
 
 
 def weight_term(left, right):
@@ -351,54 +403,55 @@
     query_t, key_t, value_t, gate_t, out_t = gather_rows(
         (query_weight, key_weight, value_weight, gate_weight, out_weight), shards
     )
-    first_t, second_t, down_t = gather_rows((first_weight, second_weight, down_weight), shards)
+    glu = Gather((first_weight, second_weight, down_weight))
+    middle = len(glu.cube.streams[0]) - 1
+    glu.advance(middle)
     inputs_f = inputs.astype(jnp.float32)
     length = inputs.shape[0]
     mask = (lax.iota(jnp.int32, length) < lengths[0]).astype(jnp.float32)[:, None]
     tables = make_tables(length)
     normed = simple_norm(inputs_f).astype(jnp.bfloat16)
+    normed, glu.parts = tie((normed, glu.parts))
+    glu.advance(1)
     query_pre = back_dot(normed, query_t)
     key_pre = back_dot(normed, key_t)
     value_pre = back_dot(normed, value_t)
     gate_pre = back_dot(normed, gate_t)
     attended = lightning_forward(lengths, query_pre, key_pre, value_pre, tables)
+    attended, glu.parts = tie((attended, glu.parts))
     attended_norm = simple_norm(attended)
     gated = (attended_norm * gate_pre * mask).astype(jnp.bfloat16)
     mixed = inputs_f + back_dot(gated, out_t)
+    first_t, second_t, down_t = glu.finish(shards)
     normed_two = simple_norm(mixed).astype(jnp.bfloat16)
     first = back_dot(normed_two, first_t)
     second = back_dot(normed_two, second_t)
     product_low = (first * second * mask).astype(jnp.bfloat16)
-    result = mixed + back_dot(product_low, down_t)
     product_grad = forward_dot(cotangent, down_t)
     first_low = (product_grad * second * mask).astype(jnp.bfloat16)
     second_low = (product_grad * first * mask).astype(jnp.bfloat16)
-    normed_two_grad = forward_dot(first_low, first_t) + forward_dot(second_low, second_t)
-    glu = Scatter(
+    stacked, widths = scatter_call(
         [
             weight_term(first_low, normed_two),
             weight_term(second_low, normed_two),
             weight_term(cotangent, product_low),
-        ]
-    )
+        ],
+        shards,
+    )
+    first_low, second_low, product_low, stacked = tie(
+        (first_low, second_low, product_low, stacked)
+    )
+    first_sum, second_sum, down_sum = scatter_sums(stacked, widths)
+    normed_two_grad = forward_dot(first_low, first_t) + forward_dot(second_low, second_t)
     mixed_grad = cotangent.astype(jnp.float32) + norm_back(mixed, normed_two_grad)
     mixed_low = mixed_grad.astype(jnp.bfloat16)
-    mixed_low, glu.sent = lax.optimization_barrier((mixed_low, glu.sent))
-    glu.to_core()
     gated_grad = forward_dot(mixed_low, out_t)
     gate_low = (gated_grad * attended_norm * mask).astype(jnp.bfloat16)
     attended_low = norm_back(attended, gated_grad * gate_pre * mask).astype(jnp.bfloat16)
-    attended_low, glu.left, glu.right = lax.optimization_barrier(
-        (attended_low, glu.left, glu.right)
-    )
-    glu.to_first()
     query_low, key_low, value_low = lightning_backward(
         lengths, query_pre, key_pre, value_pre, attended_low, tables
     )
-    query_low, key_low, value_low, glu.left, glu.right = lax.optimization_barrier(
-        (query_low, key_low, value_low, glu.left, glu.right)
-    )
-    late = Scatter(
+    attention = Scatter(
         [
             weight_term(mixed_low, gated),
             weight_term(gate_low, normed),
@@ -407,10 +460,10 @@
             weight_term(value_low, normed),
         ]
     )
-    glu.to_second()
-    late.sent, glu.left = lax.optimization_barrier((late.sent, glu.left))
-    late.to_core()
-    first_sum, second_sum, down_sum = glu.to_owner()
+    query_low, key_low, value_low, gate_low, product_low, attention.sent = tie(
+        (query_low, key_low, value_low, gate_low, product_low, attention.sent)
+    )
+    result = mixed + back_dot(product_low, down_t)
     normed_grad = (
         forward_dot(query_low, query_t)
         + forward_dot(key_low, key_t)
@@ -418,9 +471,7 @@
         + forward_dot(gate_low, gate_t)
     )
     input_grad = mixed_grad + norm_back(inputs_f, normed_grad)
-    late.to_first()
-    late.to_second()
-    out_sum, gate_sum, query_sum, key_sum, value_sum = late.to_owner()
+    out_sum, gate_sum, query_sum, key_sum, value_sum = attention.finish()
     return (
         result.astype(jnp.bfloat16),
         input_grad,

time: 596 us -> 561 us (0.941)
  waiting for transfers between devices: 202 us -> 182 us
  local copies, waits for them, and re-layouts: 90.1 us -> 80.6 us
  starting transfers between devices: 38.7 us -> 29.4 us
  other arithmetic: 46.6 us -> 55 us
    all_gather x2 -> x1, waiting for transfers between devices: 145 us -> 0.01 us  [gather_rows(): full = lax.all_gather(packed(matrices), AXES, axis=0, tiled=True)]
    ppermute x16 -> x28, waiting for transfers between devices: 42 us -> 165 us  [swap(): return lax.ppermute(value, self.name, pairs)]
    ppermute x12 -> x0, starting transfers between devices: 27.3 us -> none  [move(): return lax.ppermute(value, self.name, pairs)]
    select_n x0 -> x25, other arithmetic: none -> 22.9 us  [paired(): return jnp.where(self.place == 0, low, high)]
    ppermute x16 -> x28, starting transfers between devices: 11.3 us -> 29.3 us  [swap(): return lax.ppermute(value, self.name, pairs)]
    reduce_scatter x0 -> x1, waiting for transfers between devices: none -> 17.3 us  [scatter_sums(): summed = lax.psum_scatter(stacked, AXES, scatter_dimension=0, tiled=True)]
    slice x6 -> x4, local copies, waits for them, and re-layouts: 24.8 us -> 8.45 us  [the longest x1 6.44 us: gather_rows(): return unpacked(lambda start, stop: full[:, start:stop], matrices, shards)]
    unnamed x130 -> x138, local copies, waits for them, and re-layouts: 40.7 us -> 56.4 us
  transfers between devices with their start and end apart: 30 -> 30, of which waited for: 13 -> 18; matrix products, arithmetic and copies ran while one was open for 25% -> 28% of each run, Pallas kernels for 6% -> 4%
where the time goes in v5:
time: 561 us; the launch traced here: 553 us
  waiting for transfers between devices  182 us (32%)
  matrix products  156 us (28%)
  local copies, waits for them, and re-layouts  80.6 us (14%)
  other arithmetic  55 us (10%)
  Pallas kernels  34.1 us (6%)
  starting transfers between devices  29.4 us (5%)
  between operations  16.6 us (3%)
    ppermute x28, waiting for transfers between devices, swap(): return lax.ppermute(value, self.name, pairs)  165 us
    dot_general x8, matrix products, back_dot(): lax.dot_general(left, right, (((1,), (1,)), ((), ())), preferred_element_...  61.4 us
    unnamed x138, local copies, waits for them, and re-layouts  56.4 us
    dot_general x8, matrix products, forward_dot(): return jnp.dot(left, right, preferred_element_type=jnp.float32)  51.7 us
    dot_general x8, matrix products, weight_dot(): lax.dot_general(left, right, (((0,), (0,)), ((), ())), preferred_element_...  42.6 us
    ppermute x28, starting transfers between devices, swap(): return lax.ppermute(value, self.name, pairs)  29.3 us
    select_n x25, other arithmetic, paired(): return jnp.where(self.place == 0, low, high)  22.9 us
    pallas_call x1, Pallas kernels, lightning_backward(): pl.pallas_call(backward_kernel, grid=(HEADS,), in_specs=scalar_specs() +...  20.6 us
  transfers between devices with their start and end apart: 30, of which 18 were waited for; matrix products, arithmetic and copies ran while one was open for 28% of the time, Pallas kernels for 4%

profile of v5, /device:TPU:0, one launch (start us, length us, event | category | flops | bytes accessed | tf_op | source)
XLA Modules:
  0.0 553.2 jit_solution(2389447893169241580)
XLA Ops:
  23.6 28.6 %collective-permute-done = bf16[272,1024]{1,0:T(8,128)(2,1)S(1)} collective-permute-done((bf16[272,1024]{1,0:T(8,128)(2,1)S(1)}, bf16[272,1024]{1,0:T(8,128)(2,1)S(1)}, u32[]{:S(2)}, u32[]{:S(2)}) %collective-permute-start) | collective-permute-done | bytes 557088 | tf_op jit(solution)/shard_map/ppermute | solution.py:230
  58.9 8.7 %collective-permute-done.5 = bf16[2,272,256]{2,1,0:T(8,128)(2,1)} collective-permute-done((bf16[2,272,256]{2,1,0:T(8,128)(2,1)}, bf16[2,272,256]{2,1,0:T(8,128)(2,1)}, u32[]{:S(2)}, u32[]{:S(2)}) %collective-permute-start.5) | collective-permute-done | bytes 278560 | tf_op jit(solution)/shard_map/ppermute | solution.py:230
  91.5 18.2 %collective-permute-done.4 = bf16[2,2,272,384]{3,2,1,0:T(8,128)(2,1)S(1)} collective-permute-done((bf16[2,2,272,384]{3,2,1,0:T(8,128)(2,1)S(1)}, bf16[2,2,272,384]{3,2,1,0:T(8,128)(2,1)S(1)}, u32[]{:S(2)}, u32[]{:S(2)}) %collective-permute-start.4) | collective-permute-done | bytes 835616 | tf_op jit(solution)/shard_map/ppermute | solution.py:230
  119.7 33.4 %collective-permute-done.9 = bf16[2,2,2,272,256]{4,3,1,2,0:T(8,128)(2,1)} collective-permute-done((bf16[2,2,2,272,256]{4,3,1,2,0:T(8,128)(2,1)S(1)}, bf16[2,2,2,272,256]{4,3,1,2,0:T(8,128)(2,1)}, u32[]{:S(2)}, u32[]{:S(2)}) %collective-permute-start.9) | collective-permute-done | bytes 1114144 | tf_op jit(solution)/shard_map/ppermute | solution.py:230
  167.3 6.4 %fusion.57 = (bf16[32,32,1024]{2,1,0:T(8,128)(2,1)}, bf16[32,32,1024]{2,1,0:T(8,128)(2,1)}, bf16[32,32,1024]{2,1,0:T(8,128)(2,1)S(1)}, bf16[32,32,1024]{2,1,0:T(8,128)(2,1)S(1)}, bf16[32,32,1024]{2,1,0:T(8,128)(2,1)S(1)}) fusion(bf16[32,160,1024]{2,1,0:T(8,128)(2,1)} %bitcast.350), kind=kLoop, calls=%fused_computation.246 | loop fusion | bytes 20971520 | tf_op jit(solution)/shard_map/slice | solution.py:283
  186.9 13.5 %lightning_forward.1 = f32[1024,1024]{1,0:T(8,128)} custom-call(s32[1]{0:T(128)} %copy.148.count_ref, f32[8]{0:T(128)} %exponential_multiply_fusion.slope_ref, f32[1024,1024]{1,0:T(8,128)} %fusion.60.query_ref, f32[1024,1024]{1,0:T(8,128)} %fusion.61.key_ref, f32[1024,1024]{1,0:T(8,128)} %fusion.62.value_ref, f32[1024,128]{1,0:T(8,128)} %get-tuple-element.152.cosine_ref, ...), custom_call_target="tpu_custom_call" | custom-call | tf_op jit(solution)/shard_map/lightning_forward/pallas_call | solution.py:175
  203.9 7.1 %multiply_convert_fusion.3 = (bf16[1024,1024]{1,0:T(8,128)(2,1)S(1)}, f32[1024,1024]{1,0:T(8,128)}) fusion(f32[1024,1024]{1,0:T(8,128)S(1)} %copy-done, f32[1024]{0:T(1024)S(1)} %fusion.49, f32[1024]{0:T(1024)S(1)} %fusion.51, bf16[1024,1024]{0,1:T(8,128)(2,1)} %fusion.8, bf16[1024,1024]{1,0:T(8,128)(2,1)} %bitcast.345), kind=kOutput, calls=%fused_computation.35 | convolution fusion | flops 2151677952 | bytes 14688256 | tf_op jit(solution)/shard_map/dot_general | solution.py:34
  233.4 11.5 %fusion.63 = f32[2816,1024]{1,0:T(8,128)} fusion(bf16[1024,2816]{1,0:T(8,128)(2,1)} %constant_dynamic-update-slice_fusion, bf16[1024,1024]{1,0:T(8,128)(2,1)S(1)} %copy-done.37), kind=kOutput, calls=%fused_computation.252 | convolution fusion | flops 5905580032 | bytes 19398656 | tf_op jit(solution)/shard_map/dot_general | solution.py:30
  245.0 8.9 %fusion.13 = f32[1024,2816]{0,1:T(8,128)} fusion(bf16[1024,1024]{0,1:T(8,128)(2,1)S(1)} %multiply_convert_fusion.2, bf16[2816,256]{1,0:T(8,128)(2,1)S(1)} %bitcast.385, bf16[2816,384]{1,0:T(8,128)(2,1)S(1)} %bitcast.362, bf16[2816,384]{1,0:T(8,128)(2,1)S(1)} %bitcast.364), kind=kOutput, calls=%fused_computation.44 | convolution fusion | flops 5922881536 | bytes 19398656 | tf_op jit(solution)/shard_map/dot_general | solution.py:34
  253.9 18.6 %multiply_convert_fusion = (bf16[1024,2816]{0,1:T(8,128)(2,1)}, bf16[1024,2816]{0,1:T(8,128)(2,1)}, bf16[1024,2816]{0,1:T(8,128)(2,1)}) fusion(f32[1024,2816]{0,1:T(8,128)} %fusion.13, f32[1024]{0:T(1024)S(1)} %fusion.49, f32[2816,1024]{1,0:T(8,128)} %fusion.63, bf16[1024,1024]{0,1:T(8,128)(2,1)S(1)} %multiply_convert_fusion.2, ...), kind=kOutput, calls=%fused_computation.6 | convolution fusion | flops 5948833792 | bytes 48238592 | tf_op jit(solution)/shard_map/dot_general | solution.py:34
  272.5 9.1 %convolution_convert_fusion.2 = bf16[2816,1024]{1,0:T(8,128)(2,1)S(1)} fusion(bf16[1024,2816]{0,1:T(8,128)(2,1)} %get-tuple-element.43, bf16[1024,1024]{0,1:T(8,128)(2,1)S(1)} %multiply_convert_fusion.2), kind=kOutput, calls=%fused_computation.20 | convolution fusion | flops 5908463616 | bytes 13631488 | tf_op jit(solution)/shard_map/dot_general | solution.py:40
  284.6 9.1 %convolution_convert_fusion.1 = bf16[2816,1024]{1,0:T(8,128)(2,1)S(1)} fusion(bf16[1024,2816]{0,1:T(8,128)(2,1)} %get-tuple-element.44, bf16[1024,1024]{0,1:T(8,128)(2,1)S(1)} %multiply_convert_fusion.2), kind=kOutput, calls=%fused_computation.19 | convolution fusion | flops 5908463616 | bytes 13631488 | tf_op jit(solution)/shard_map/dot_general | solution.py:40
  293.7 9.3 %convolution_convert_fusion = bf16[2816,1024]{0,1:T(8,128)(2,1)S(1)} fusion(bf16[1024,2816]{0,1:T(8,128)(2,1)} %get-tuple-element.49, bf16[1024,1024]{1,0:T(8,128)(2,1)S(1)} %copy-done.37), kind=kOutput, calls=%fused_computation.18 | convolution fusion | flops 5908463616 | bytes 13631488 | tf_op jit(solution)/shard_map/dot_general | solution.py:40
  315.3 12.7 %fusion.10 = f32[1024,1024]{0,1:T(8,128)} fusion(bf16[1024,2816]{0,1:T(8,128)(2,1)} %get-tuple-element.43, bf16[2816,256]{1,0:T(8,128)(2,1)} %bitcast.388, bf16[2816,384]{1,0:T(8,128)(2,1)} %bitcast.367, bf16[2816,384]{1,0:T(8,128)(2,1)} %bitcast.369), kind=kOutput, calls=%fused_computation.41 | convolution fusion | flops 5922881536 | bytes 15728640 | tf_op jit(solution)/shard_map/dot_general | solution.py:30
  328.1 12.2 %multiply_reduce_fusion.1 = (f32[1024]{0:T(1024)S(1)}, f32[1024,1024]{0,1:T(8,128)}) fusion(f32[1024,1024]{0,1:T(8,128)S(1)} %copy-done.9, f32[1024,1024]{0,1:T(8,128)} %fusion.10, bf16[1024,2816]{0,1:T(8,128)(2,1)} %get-tuple-element.44, bf16[2816,256]{1,0:T(8,128)(2,1)S(1)} %bitcast.386, bf16[2816,384]{1,0:T(8,128)(2,1)S(1)} %bitcast.363, ...), kind=kOutput, calls=%fused_computation.32 | convolution fusion | flops 5926026240 | bytes 24121344 | tf_op jit(solution)/shard_map/dot_general | solution.py:30
  354.0 20.6 %lightning_backward.1 = (bf16[1024,1024]{1,0:T(8,128)(2,1)}, bf16[1024,1024]{1,0:T(8,128)(2,1)}, bf16[1024,1024]{1,0:T(8,128)(2,1)}) custom-call(s32[1]{0:T(128)} %copy.148.count_ref, f32[8]{0:T(128)} %exponential_multiply_fusion.slope_ref, f32[1024,1024]{1,0:T(8,128)} %fusion.60.query_ref, f32[1024,1024]{1,0:T(8,128)} %fusion.61.key_ref, ...), custom_call_target="tpu_custom_call" | custom-call | tf_op jit(solution)/shard_map/lightning_backward/pallas_call | solution.py:188
  400.2 11.3 %add_convert_fusion = bf16[1024,1024]{0,1:T(8,128)(2,1)} fusion(f32[1024,1024]{0,1:T(8,128)S(1)} %copy-done.10, bf16[1024,2816]{1,0:T(8,128)(2,1)} %constant_dynamic-update-slice_fusion, bf16[1024,2816]{0,1:T(8,128)(2,1)} %get-tuple-element.49), kind=kOutput, calls=%fused_computation.28 | convolution fusion | flops 5907677184 | bytes 17825792 | tf_op jit(solution)/shard_map/dot_general | solution.py:34
  444.1 18.8 %collective-permute-done.21 = bf16[2,2,2,5,32,384]{5,4,3,1,0,2:T(8,128)(2,1)} collective-permute-done((bf16[2,2,2,5,32,384]{5,4,3,1,0,2:T(8,128)(2,1)}, bf16[2,2,2,5,32,384]{5,4,3,1,0,2:T(8,128)(2,1)}, u32[]{:S(2)}, u32[]{:S(2)}) %collective-permute-start.21) | collective-permute-done | bytes 983072 | tf_op jit(solution)/shard_map/ppermute | solution.py:230
  465.0 6.1 %collective-permute-done.18 = bf16[2,2,2,5,32,384]{5,4,3,0,2,1:T(8,128)(2,1)S(1)} collective-permute-done((bf16[2,2,2,5,32,384]{5,4,3,0,2,1:T(8,128)(2,1)S(1)}, bf16[2,2,2,5,32,384]{5,4,3,0,2,1:T(8,128)(2,1)S(1)}, u32[]{:S(2)}, u32[]{:S(2)}) %collective-permute-start.18) | collective-permute-done | bytes 983072 | tf_op jit(solution)/shard_map/ppermute | solution.py:230
  472.5 9.1 %collective-permute-done.25 = bf16[2,2,5,32,256]{4,3,2,0,1:T(8,128)(2,1)S(1)} collective-permute-done((bf16[2,2,5,32,256]{4,3,2,0,1:T(8,128)(2,1)S(1)}, bf16[2,2,5,32,256]{4,3,2,0,1:T(8,128)(2,1)S(1)}, u32[]{:S(2)}, u32[]{:S(2)}) %collective-permute-start.25) | collective-permute-done | bytes 327712 | tf_op jit(solution)/shard_map/ppermute | solution.py:230
  482.5 6.1 %collective-permute-done.22 = bf16[2,2,5,32,384]{4,3,2,1,0:T(8,128)(2,1)S(1)} collective-permute-done((bf16[2,2,5,32,384]{4,3,2,1,0:T(8,128)(2,1)S(1)}, bf16[2,2,5,32,384]{4,3,2,1,0:T(8,128)(2,1)S(1)}, u32[]{:S(2)}, u32[]{:S(2)}) %collective-permute-start.22) | collective-permute-done | bytes 491552 | tf_op jit(solution)/shard_map/ppermute | solution.py:230
  495.1 13.1 %collective-permute-done.20 = bf16[2,5,32,384]{3,2,1,0:T(8,128)(2,1)S(1)} collective-permute-done((bf16[2,5,32,384]{3,2,1,0:T(8,128)(2,1)S(1)}, bf16[2,5,32,384]{3,2,1,0:T(8,128)(2,1)S(1)}, u32[]{:S(2)}, u32[]{:S(2)}) %collective-permute-start.20) | collective-permute-done | bytes 245792 | tf_op jit(solution)/shard_map/ppermute | solution.py:230
  518.8 5.9 %collective-permute-done.27 = bf16[5,32,1024]{2,1,0:T(8,128)(2,1)S(1)} collective-permute-done((bf16[5,32,1024]{2,1,0:T(8,128)(2,1)S(1)}, bf16[5,32,1024]{2,1,0:T(8,128)(2,1)S(1)}, u32[]{:S(2)}, u32[]{:S(2)}) %collective-permute-start.27) | collective-permute-done | bytes 327712 | tf_op jit(solution)/shard_map/ppermute | solution.py:230
  525.7 17.3 %reduce-scatter.2.cloned.1.call-done = bf16[288,1024]{1,0:T(8,128)(2,1)} async-done(((bf16[9216,1024]{1,0:T(8,128)(2,1)}), bf16[288,1024]{1,0:T(8,128)(2,1)}) %reduce-scatter.2.cloned.1.call-update) | async-done | bytes 589840 | tf_op jit(solution)/shard_map/reduce_scatter | solution.py:367
  (318 shorter events, 220.9 us)
Async XLA Ops:
  7.2 160.1 %all-gather.2.cloned.1.call-start = ((), (), s32[]{:S(2)}) async-start(), calls=%async_computation.1 | async-start | bytes 10813440 | tf_op jit(solution)/shard_map/all_gather | solution.py:281
  12.2 530.7 %reduce-scatter.2.cloned.1.call-start = ((), (), s32[]{:S(2)}) async-start(), calls=%async_computation.2 | async-start | bytes 19464192 | tf_op jit(solution)/shard_map/reduce_scatter | solution.py:367
  16.6 35.6 %collective-permute-start = (bf16[272,1024]{1,0:T(8,128)(2,1)S(1)}, bf16[272,1024]{1,0:T(8,128)(2,1)S(1)}, u32[]{:S(2)}, u32[]{:S(2)}) collective-permute-start(bf16[272,1024]{1,0:T(8,128)(2,1)S(1)} %fusion.48), channel_id=1, source_target_pairs={{0,4},{1,5},{2,6},{3,7},{4,0},{5,1},{6,2},{7,3},{8,12},{9,13},{10,... | collective-permute-start | bytes 1671176 | tf_op jit(solution)/shard_map/ppermute | solution.py:230
  53.5 18.2 %collective-permute-start.1 = (bf16[2,272,384]{2,1,0:T(8,128)(2,1)}, bf16[2,272,384]{2,1,0:T(8,128)(2,1)}, u32[]{:S(2)}, u32[]{:S(2)}) collective-permute-start(bf16[2,272,384]{2,1,0:T(8,128)(2,1)} %get-tuple-element.142), channel_id=1, source_target_pairs={{0,2},{1,3},{2,0},{3,1},{4,6},{5,7},{6,4},{7,5},{8,10},{9,11},{10,... | collective-permute-start | bytes 1253384 | tf_op jit(solution)/shard_map/ppermute | solution.py:230
  57.3 21.3 %collective-permute-start.3 = (bf16[2,272,384]{2,1,0:T(8,128)(2,1)}, bf16[2,272,384]{2,1,0:T(8,128)(2,1)S(1)}, u32[]{:S(2)}, u32[]{:S(2)}) collective-permute-start(bf16[2,272,384]{2,1,0:T(8,128)(2,1)} %get-tuple-element.141), channel_id=1, source_target_pairs={{0,16},{8,24},{16,0},{24,8},{1,17},{9,25},{17,1},{25,9},{2,18},{10... | collective-permute-start | bytes 1253384 | tf_op jit(solution)/shard_map/ppermute | solution.py:230
  68.9 21.0 %collective-permute-start.6 = (bf16[2,2,272,256]{3,2,0,1:T(8,128)(2,1)S(1)}, bf16[2,2,272,256]{3,2,0,1:T(8,128)(2,1)S(1)}, u32[]{:S(2)}, u32[]{:S(2)}) collective-permute-start(bf16[2,2,272,256]{3,2,0,1:T(8,128)(2,1)S(1)} %maximum_select_fusion.22), channel_id=1, source_target_pairs={{0,16},{8,24},{16,0},{24,8},{1,17},{9,25},{17,1},{25,9},{2,18},{10... | collective-permute-start | bytes 1671176 | tf_op jit(solution)/shard_map/ppermute | solution.py:230
  73.3 16.7 %collective-permute-start.2 = (bf16[2,2,272,384]{3,2,0,1:T(8,128)(2,1)S(1)}, bf16[2,2,272,384]{3,2,0,1:T(8,128)(2,1)S(1)}, u32[]{:S(2)}, u32[]{:S(2)}) collective-permute-start(bf16[2,2,272,384]{3,2,0,1:T(8,128)(2,1)S(1)} %maximum_select_fusion.13), channel_id=1, source_target_pairs={{0,1},{1,0},{2,3},{3,2},{4,5},{5,4},{6,7},{7,6},{8,9},{9,8},{10,11... | collective-permute-start | bytes 2506760 | tf_op jit(solution)/shard_map/ppermute | solution.py:230
  78.8 30.9 %collective-permute-start.4 = (bf16[2,2,272,384]{3,2,1,0:T(8,128)(2,1)S(1)}, bf16[2,2,272,384]{3,2,1,0:T(8,128)(2,1)S(1)}, u32[]{:S(2)}, u32[]{:S(2)}) collective-permute-start(bf16[2,2,272,384]{3,2,1,0:T(8,128)(2,1)S(1)} %maximum_select_fusion.14), channel_id=1, source_target_pairs={{0,2},{1,3},{2,0},{3,1},{4,6},{5,7},{6,4},{7,5},{8,10},{9,11},{10,... | collective-permute-start | bytes 2506760 | tf_op jit(solution)/shard_map/ppermute | solution.py:230
  111.2 45.3 %collective-permute-start.7 = (bf16[2,2,2,272,384]{4,3,0,1,2:T(8,128)(2,1)}, bf16[2,2,2,272,384]{4,3,0,1,2:T(8,128)(2,1)}, u32[]{:S(2)}, u32[]{:S(2)}) collective-permute-start(bf16[2,2,2,272,384]{4,3,0,1,2:T(8,128)(2,1)} %maximum_select_fusion.6), channel_id=1, source_target_pairs={{0,16},{8,24},{16,0},{24,8},{1,17},{9,25},{17,1},{25,9},{2,18},{10... | collective-permute-start | bytes 5013512 | tf_op jit(solution)/shard_map/ppermute | solution.py:230
  115.6 44.7 %collective-permute-start.8 = (bf16[2,2,2,272,384]{4,3,2,1,0:T(8,128)(2,1)}, bf16[2,2,2,272,384]{4,3,2,1,0:T(8,128)(2,1)}, u32[]{:S(2)}, u32[]{:S(2)}) collective-permute-start(bf16[2,2,2,272,384]{4,3,2,1,0:T(8,128)(2,1)} %maximum_select_fusion.7), channel_id=1, source_target_pairs={{0,1},{1,0},{2,3},{3,2},{4,5},{5,4},{6,7},{7,6},{8,9},{9,8},{10,11... | collective-permute-start | bytes 5013512 | tf_op jit(solution)/shard_map/ppermute | solution.py:230
  115.6 37.5 %collective-permute-start.9 = (bf16[2,2,2,272,256]{4,3,1,2,0:T(8,128)(2,1)S(1)}, bf16[2,2,2,272,256]{4,3,1,2,0:T(8,128)(2,1)}, u32[]{:S(2)}, u32[]{:S(2)}) collective-permute-start(bf16[2,2,2,272,256]{4,3,1,2,0:T(8,128)(2,1)S(1)} %maximum_select_fusion.11), channel_id=1, source_target_pairs={{0,2},{1,3},{2,0},{3,1},{4,6},{5,7},{6,4},{7,5},{8,10},{9,11},{10,... | collective-permute-start | bytes 3342344 | tf_op jit(solution)/shard_map/ppermute | solution.py:230
  203.2 17.3 %collective-permute-start.10 = (bf16[2,2,2,2,272,384]{5,4,3,2,1,0:T(8,128)(2,1)}, bf16[2,2,2,2,272,384]{5,4,3,2,1,0:T(8,128)(2,1)S(1)}, u32[]{:S(2)}, u32[]{:S(2)}) collective-permute-start(bf16[2,2,2,2,272,384]{5,4,3,2,1,0:T(8,128)(2,1)} %copy_select_fusion), channel_id=1, source_target_pairs={{0,8},{8,0},{16,24},{24,16},{1,9},{9,1},{17,25},{25,17},{2,10},{10... | collective-permute-start | bytes 10027016 | tf_op jit(solution)/shard_map/ppermute | solution.py:230
  203.3 18.7 %collective-permute-start.11 = (bf16[2,2,2,2,272,384]{5,4,3,2,1,0:T(8,128)(2,1)}, bf16[2,2,2,2,272,384]{5,4,3,2,1,0:T(8,128)(2,1)S(1)}, u32[]{:S(2)}, u32[]{:S(2)}) collective-permute-start(bf16[2,2,2,2,272,384]{5,4,3,2,1,0:T(8,128)(2,1)} %maximum_select_fusion), channel_id=1, source_target_pairs={{0,8},{8,0},{16,24},{24,16},{1,9},{9,1},{17,25},{25,17},{2,10},{10... | collective-permute-start | bytes 10027016 | tf_op jit(solution)/shard_map/ppermute | solution.py:230
  203.8 15.0 %collective-permute-start.12 = (bf16[2,2,2,2,272,256]{5,4,1,3,0,2:T(8,128)(2,1)}, bf16[2,2,2,2,272,256]{5,4,1,3,0,2:T(8,128)(2,1)S(1)}, u32[]{:S(2)}, u32[]{:S(2)}) collective-permute-start(bf16[2,2,2,2,272,256]{5,4,1,3,0,2:T(8,128)(2,1)} %maximum_select_fusion.1), channel_id=1, source_target_pairs={{0,8},{8,0},{16,24},{24,16},{1,9},{9,1},{17,25},{25,17},{2,10},{10... | collective-permute-start | bytes 6684680 | tf_op jit(solution)/shard_map/ppermute | solution.py:230
  396.4 21.1 %collective-permute-start.13 = (bf16[2,2,2,2,32,1024]{5,4,1,3,0,2:T(8,128)(2,1)S(1)}, bf16[2,2,2,2,32,1024]{5,4,1,3,0,2:T(8,128)(2,1)S(1)}, u32[]{:S(2)}, u32[]{:S(2)}) collective-permute-start(bf16[2,2,2,2,32,1024]{5,4,1,3,0,2:T(8,128)(2,1)S(1)} %bitcast.392), channel_id=1, source_target_pairs={{0,8},{8,0},{16,24},{24,16},{1,9},{9,1},{17,25},{25,17},{2,10},{10... | collective-permute-start | bytes 3145736 | tf_op jit(solution)/shard_map/ppermute | solution.py:230
  396.9 21.0 %collective-permute-start.14 = (bf16[2,2,2,2,32,1024]{5,4,1,3,0,2:T(8,128)(2,1)S(1)}, bf16[2,2,2,2,32,1024]{5,4,1,3,0,2:T(8,128)(2,1)S(1)}, u32[]{:S(2)}, u32[]{:S(2)}) collective-permute-start(bf16[2,2,2,2,32,1024]{5,4,1,3,0,2:T(8,128)(2,1)S(1)} %bitcast.393), channel_id=1, source_target_pairs={{0,8},{8,0},{16,24},{24,16},{1,9},{9,1},{17,25},{25,17},{2,10},{10... | collective-permute-start | bytes 3145736 | tf_op jit(solution)/shard_map/ppermute | solution.py:230
  421.4 19.8 %collective-permute-start.24 = (bf16[2,2,2,5,32,256]{5,4,3,1,2,0:T(8,128)(2,1)}, bf16[2,2,2,5,32,256]{5,4,3,1,2,0:T(8,128)(2,1)}, u32[]{:S(2)}, u32[]{:S(2)}) collective-permute-start(bf16[2,2,2,5,32,256]{5,4,3,1,2,0:T(8,128)(2,1)} %dynamic-slice_bitcast_fusion.2), channel_id=1, source_target_pairs={{0,2},{1,3},{2,0},{3,1},{4,6},{5,7},{6,4},{7,5},{8,10},{9,11},{10,... | collective-permute-start | bytes 1966088 | tf_op jit(solution)/shard_map/ppermute | solution.py:230
  426.8 36.1 %collective-permute-start.21 = (bf16[2,2,2,5,32,384]{5,4,3,1,0,2:T(8,128)(2,1)}, bf16[2,2,2,5,32,384]{5,4,3,1,0,2:T(8,128)(2,1)}, u32[]{:S(2)}, u32[]{:S(2)}) collective-permute-start(bf16[2,2,2,5,32,384]{5,4,3,1,0,2:T(8,128)(2,1)} %dynamic-slice_bitcast_fusion), channel_id=1, source_target_pairs={{0,1},{1,0},{2,3},{3,2},{4,5},{5,4},{6,7},{7,6},{8,9},{9,8},{10,11... | collective-permute-start | bytes 2949128 | tf_op jit(solution)/shard_map/ppermute | solution.py:230
  438.0 33.1 %collective-permute-start.18 = (bf16[2,2,2,5,32,384]{5,4,3,0,2,1:T(8,128)(2,1)S(1)}, bf16[2,2,2,5,32,384]{5,4,3,0,2,1:T(8,128)(2,1)S(1)}, u32[]{:S(2)}, u32[]{:S(2)}) collective-permute-start(bf16[2,2,2,5,32,384]{5,4,3,0,2,1:T(8,128)(2,1)S(1)} %dynamic-slice_bitcast_fusion.1), channel_id=1, source_target_pairs={{0,16},{8,24},{16,0},{24,8},{1,17},{9,25},{17,1},{25,9},{2,18},{10... | collective-permute-start | bytes 2949128 | tf_op jit(solution)/shard_map/ppermute | solution.py:230
  442.6 39.0 %collective-permute-start.25 = (bf16[2,2,5,32,256]{4,3,2,0,1:T(8,128)(2,1)S(1)}, bf16[2,2,5,32,256]{4,3,2,0,1:T(8,128)(2,1)S(1)}, u32[]{:S(2)}, u32[]{:S(2)}) collective-permute-start(bf16[2,2,5,32,256]{4,3,2,0,1:T(8,128)(2,1)S(1)} %dynamic-slice_bitcast_fusion.6), channel_id=1, source_target_pairs={{0,16},{8,24},{16,0},{24,8},{1,17},{9,25},{17,1},{25,9},{2,18},{10... | collective-permute-start | bytes 983048 | tf_op jit(solution)/shard_map/ppermute | solution.py:230
  464.4 24.1 %collective-permute-start.22 = (bf16[2,2,5,32,384]{4,3,2,1,0:T(8,128)(2,1)S(1)}, bf16[2,2,5,32,384]{4,3,2,1,0:T(8,128)(2,1)S(1)}, u32[]{:S(2)}, u32[]{:S(2)}) collective-permute-start(bf16[2,2,5,32,384]{4,3,2,1,0:T(8,128)(2,1)S(1)} %dynamic-slice_bitcast_fusion.3), channel_id=1, source_target_pairs={{0,2},{1,3},{2,0},{3,1},{4,6},{5,7},{6,4},{7,5},{8,10},{9,11},{10,... | collective-permute-start | bytes 1474568 | tf_op jit(solution)/shard_map/ppermute | solution.py:230
  471.4 21.7 %collective-permute-start.19 = (bf16[2,2,5,32,384]{4,3,2,0,1:T(8,128)(2,1)S(1)}, bf16[2,2,5,32,384]{4,3,2,0,1:T(8,128)(2,1)S(1)}, u32[]{:S(2)}, u32[]{:S(2)}) collective-permute-start(bf16[2,2,5,32,384]{4,3,2,0,1:T(8,128)(2,1)S(1)} %dynamic-slice_bitcast_fusion.4), channel_id=1, source_target_pairs={{0,1},{1,0},{2,3},{3,2},{4,5},{5,4},{6,7},{7,6},{8,9},{9,8},{10,11... | collective-permute-start | bytes 1474568 | tf_op jit(solution)/shard_map/ppermute | solution.py:230
  493.3 14.9 %collective-permute-start.20 = (bf16[2,5,32,384]{3,2,1,0:T(8,128)(2,1)S(1)}, bf16[2,5,32,384]{3,2,1,0:T(8,128)(2,1)S(1)}, u32[]{:S(2)}, u32[]{:S(2)}) collective-permute-start(bf16[2,5,32,384]{3,2,1,0:T(8,128)(2,1)S(1)} %dynamic-slice_bitcast_fusion.8), channel_id=1, source_target_pairs={{0,2},{1,3},{2,0},{3,1},{4,6},{5,7},{6,4},{7,5},{8,10},{9,11},{10,... | collective-permute-start | bytes 737288 | tf_op jit(solution)/shard_map/ppermute | solution.py:230
  508.4 16.3 %collective-permute-start.27 = (bf16[5,32,1024]{2,1,0:T(8,128)(2,1)S(1)}, bf16[5,32,1024]{2,1,0:T(8,128)(2,1)S(1)}, u32[]{:S(2)}, u32[]{:S(2)}) collective-permute-start(bf16[5,32,1024]{2,1,0:T(8,128)(2,1)S(1)} %dynamic-slice_bitcast_fusion.5), channel_id=1, source_target_pairs={{0,4},{1,5},{2,6},{3,7},{4,0},{5,1},{6,2},{7,3},{8,12},{9,13},{10,... | collective-permute-start | bytes 983048 | tf_op jit(solution)/shard_map/ppermute | solution.py:230
  (63 other events, 771.7 us)
Sparse Core Ops, SparseCore 0:
  12.3 135.4 all-gather.1
  312.5 230.3 reduce-scatter.1

commit v6 on v5

--- a/solution.py
+++ b/solution.py
@@ -277,22 +277,18 @@
     return gathered
 
 
-def gather_rows(matrices, shards):
-    full = lax.all_gather(packed(matrices), AXES, axis=0, tiled=True)
-    full = full.reshape(shards, -1, D)
-    return unpacked(lambda start, stop: full[:, start:stop], matrices, shards)
-
-
 class Gather:
     def __init__(self, matrices):
         self.matrices = matrices
         self.cube = Cube()
-        value, self.known = packed(matrices), []
+        self.value, self.known = packed(matrices), []
+        self.done = 0
+
+    def begin(self):
         for label in reversed(self.cube.far):
-            value = self.join(value, label, self.known)
+            self.value = self.join(self.value, label, self.known)
             self.known = sorted(self.known + [label])
-        self.parts = self.cube.columns(value)
-        self.done = 0
+        self.parts = self.cube.columns(self.value)
 
     def join(self, value, label, known):
         bit = self.cube.bits[label]
@@ -400,18 +396,25 @@
     cotangent,
 ):
     shards = lax.axis_size(AXES)
-    query_t, key_t, value_t, gate_t, out_t = gather_rows(
-        (query_weight, key_weight, value_weight, gate_weight, out_weight), shards
-    )
+    heads = Gather((query_weight, key_weight, value_weight, gate_weight, out_weight))
     glu = Gather((first_weight, second_weight, down_weight))
-    middle = len(glu.cube.streams[0]) - 1
-    glu.advance(middle)
+    last = len(glu.cube.streams[0])
+    heads.begin()
+    heads.parts, glu.value = tie((heads.parts, glu.value))
+    glu.begin()
+    heads.advance(last - 1)
+    heads.parts, glu.parts = tie((heads.parts, glu.parts))
+    heads.advance(1)
+    glu.advance(last - 2)
+    heads.parts, glu.parts = tie((heads.parts, glu.parts))
+    glu.advance(1)
+    query_t, key_t, value_t, gate_t, out_t = heads.finish(shards)
     inputs_f = inputs.astype(jnp.float32)
     length = inputs.shape[0]
     mask = (lax.iota(jnp.int32, length) < lengths[0]).astype(jnp.float32)[:, None]
     tables = make_tables(length)
     normed = simple_norm(inputs_f).astype(jnp.bfloat16)
-    normed, glu.parts = tie((normed, glu.parts))
+    query_t, glu.parts = tie((query_t, glu.parts))
     glu.advance(1)
     query_pre = back_dot(normed, query_t)
     key_pre = back_dot(normed, key_t)
@@ -424,9 +427,9 @@
     mixed = inputs_f + back_dot(gated, out_t)
     first_t, second_t, down_t = glu.finish(shards)
     normed_two = simple_norm(mixed).astype(jnp.bfloat16)
-    first = back_dot(normed_two, first_t)
-    second = back_dot(normed_two, second_t)
-    product_low = (first * second * mask).astype(jnp.bfloat16)
+    first = back_dot(normed_two, first_t).astype(jnp.bfloat16)
+    second = back_dot(normed_two, second_t).astype(jnp.bfloat16)
+    product_low = (first.astype(jnp.float32) * second * mask).astype(jnp.bfloat16)
     product_grad = forward_dot(cotangent, down_t)
     first_low = (product_grad * second * mask).astype(jnp.bfloat16)
     second_low = (product_grad * first * mask).astype(jnp.bfloat16)

time: 561 us -> 529 us (0.943)
  waiting for transfers between devices: 182 us -> 153 us
  matrix products: 156 us -> 146 us
  starting transfers between devices: 29.4 us -> 36.2 us
    ppermute x28 -> x41, waiting for transfers between devices: 165 us -> 135 us  [swap(): return lax.ppermute(value, self.name, pairs)]
    select_n x13 -> x28, local copies, waits for them, and re-layouts: 1.63 us -> 10.6 us  [paired(): return jnp.where(self.place == 0, low, high)]
    ppermute x28 -> x41, starting transfers between devices: 29.3 us -> 36.1 us  [swap(): return lax.ppermute(value, self.name, pairs)]
    slice x1 -> x0, local copies, waits for them, and re-layouts: 6.44 us -> none  [gather_rows(): return unpacked(lambda start, stop: full[:, start:stop], matrices, shards)]
    select_n x25 -> x46, other arithmetic: 22.9 us -> 26.8 us  [paired(): return jnp.where(self.place == 0, low, high)]
    unnamed x138 -> x184, local copies, waits for them, and re-layouts: 56.4 us -> 53.3 us
  transfers between devices with their start and end apart: 30 -> 42, of which waited for: 18 -> 22; matrix products, arithmetic and copies ran while one was open for 28% -> 33% of each run, Pallas kernels for 4% -> 6%
where the time goes in v6:
time: 529 us; the launch traced here: 523 us
  waiting for transfers between devices  153 us (29%)
  matrix products  146 us (28%)
  local copies, waits for them, and re-layouts  81.4 us (15%)
  other arithmetic  56.3 us (11%)
  starting transfers between devices  36.2 us (7%)
  Pallas kernels  33.4 us (6%)
  between operations  16.9 us (3%)
    ppermute x41, waiting for transfers between devices, swap(): return lax.ppermute(value, self.name, pairs)  135 us
    dot_general x8, matrix products, back_dot(): lax.dot_general(left, right, (((1,), (1,)), ((), ())), preferred_element_...  56.5 us
    unnamed x184, local copies, waits for them, and re-layouts  53.3 us
    dot_general x8, matrix products, forward_dot(): return jnp.dot(left, right, preferred_element_type=jnp.float32)  49.1 us
    dot_general x8, matrix products, weight_dot(): lax.dot_general(left, right, (((0,), (0,)), ((), ())), preferred_element_...  40 us
    ppermute x41, starting transfers between devices, swap(): return lax.ppermute(value, self.name, pairs)  36.1 us
    select_n x46, other arithmetic, paired(): return jnp.where(self.place == 0, low, high)  26.8 us
    pallas_call x1, Pallas kernels, lightning_backward(): pl.pallas_call(backward_kernel, grid=(HEADS,), in_specs=scalar_specs() +...  20.2 us
  transfers between devices with their start and end apart: 42, of which 22 were waited for; matrix products, arithmetic and copies ran while one was open for 33% of the time, Pallas kernels for 6%

profile of v6, /device:TPU:0, one launch (start us, length us, event | category | flops | bytes accessed | tf_op | source)
XLA Modules:
  0.0 522.8 jit_solution(126139425496441161)
XLA Ops:
  20.6 9.7 %collective-permute-done = bf16[160,1024]{1,0:T(8,128)(2,1)S(1)} collective-permute-done((bf16[160,1024]{1,0:T(8,128)(2,1)S(1)}, bf16[160,1024]{1,0:T(8,128)(2,1)S(1)}, u32[]{:S(2)}, u32[]{:S(2)}) %collective-permute-start) | collective-permute-done | bytes 327712 | tf_op jit(solution)/shard_map/ppermute | solution.py:230
  48.4 14.3 %collective-permute-done.7 = bf16[272,1024]{1,0:T(8,128)(2,1)S(1)} collective-permute-done((bf16[272,1024]{1,0:T(8,128)(2,1)S(1)}, bf16[272,1024]{1,0:T(8,128)(2,1)S(1)}, u32[]{:S(2)}, u32[]{:S(2)}) %collective-permute-start.7) | collective-permute-done | bytes 557088 | tf_op jit(solution)/shard_map/ppermute | solution.py:230
  76.2 11.9 %collective-permute-done.11 = bf16[2,272,384]{2,1,0:T(8,128)(2,1)S(1)} collective-permute-done((bf16[2,272,384]{2,1,0:T(8,128)(2,1)S(1)}, bf16[2,272,384]{2,1,0:T(8,128)(2,1)S(1)}, u32[]{:S(2)}, u32[]{:S(2)}) %collective-permute-start.11) | collective-permute-done | bytes 417824 | tf_op jit(solution)/shard_map/ppermute | solution.py:230
  89.1 5.9 %collective-permute-done.12 = bf16[2,272,384]{2,1,0:T(8,128)(2,1)S(1)} collective-permute-done((bf16[2,272,384]{2,1,0:T(8,128)(2,1)S(1)}, bf16[2,272,384]{2,1,0:T(8,128)(2,1)S(1)}, u32[]{:S(2)}, u32[]{:S(2)}) %collective-permute-start.12) | collective-permute-done | bytes 417824 | tf_op jit(solution)/shard_map/ppermute | solution.py:230
  114.9 10.1 %collective-permute-done.17 = bf16[2,2,272,384]{3,2,1,0:T(8,128)(2,1)S(1)} collective-permute-done((bf16[2,2,272,384]{3,2,1,0:T(8,128)(2,1)}, bf16[2,2,272,384]{3,2,1,0:T(8,128)(2,1)S(1)}, u32[]{:S(2)}, u32[]{:S(2)}) %collective-permute-start.17) | collective-permute-done | bytes 835616 | tf_op jit(solution)/shard_map/ppermute | solution.py:230
  155.4 13.2 %lightning_forward.1 = f32[1024,1024]{1,0:T(8,128)} custom-call(s32[1]{0:T(128)} %copy.166.count_ref, f32[8]{0:T(128)} %exponential_multiply_fusion.slope_ref, f32[1024,1024]{1,0:T(8,128)} %fusion.58.query_ref, f32[1024,1024]{1,0:T(8,128)} %fusion.43.key_ref, f32[1024,1024]{1,0:T(8,128)} %fusion.41.value_ref, f32[1024,128]{1,0:T(8,128)} %get-tuple-element.206.cosine_ref, ...), custom_call_target="tpu_custom_call" | custom-call | tf_op jit(solution)/shard_map/lightning_forward/pallas_call | solution.py:175
  181.9 5.4 %multiply_convert_fusion.2 = (bf16[1024,1024]{1,0:T(8,128)(2,1)}, f32[1024,1024]{1,0:T(8,128)}) fusion(f32[1024,1024]{1,0:T(8,128)S(1)} %copy-done, f32[1024]{0:T(1024)S(1)} %fusion.62, f32[1024]{0:T(1024)S(1)} %fusion.64, bf16[1024,256]{1,0:T(8,128)(2,1)S(1)} %bitcast.434, bf16[1024,384]{1,0:T(8,128)(2,1)S(1)} %bitcast.417, ...), kind=kOutput, calls=%fused_computation.39 | convolution fusion | flops 2161115136 | bytes 14692352 | tf_op jit(solution)/shard_map/dot_general | solution.py:34
  209.0 9.1 %fusion.82 = f32[2816,1024]{1,0:T(8,128)} fusion(bf16[1024,2816]{1,0:T(8,128)(2,1)S(1)} %constant_dynamic-update-slice_fusion, bf16[1024,1024]{1,0:T(8,128)(2,1)S(1)} %copy-done.35), kind=kOutput, calls=%fused_computation.320 | convolution fusion | flops 5905580032 | bytes 19398656 | tf_op jit(solution)/shard_map/dot_general | solution.py:30
  218.2 8.1 %convolution_convert_fusion.1 = bf16[1024,2816]{0,1:T(8,128)(2,1)} fusion(bf16[1024,1024]{0,1:T(8,128)(2,1)S(1)} %multiply_convert_fusion.1, bf16[2816,256]{1,0:T(8,128)(2,1)S(1)} %bitcast.450, bf16[2816,384]{1,0:T(8,128)(2,1)S(1)} %bitcast.426, bf16[2816,384]{1,0:T(8,128)(2,1)S(1)} %bitcast.428), kind=kOutput, calls=%fused_computation.21 | convolution fusion | flops 5925765120 | bytes 13631488 | tf_op jit(solution)/shard_map/dot_general | solution.py:34
  226.2 16.2 %fusion.3 = (bf16[1024,2816]{0,1:T(8,128)(2,1)}, bf16[1024,2816]{0,1:T(8,128)(2,1)}, bf16[1024,2816]{0,1:T(8,128)(2,1)}) fusion(f32[2816,1024]{1,0:T(8,128)} %fusion.82, f32[1024]{0:T(1024)S(1)} %fusion.62, bf16[1024,2816]{0,1:T(8,128)(2,1)} %convolution_convert_fusion.1, bf16[1024,1024]{0,1:T(8,128)(2,1)} %copy-done.39, bf16[2816,256]{1,0:T(8,128)(2,1)} %bitcast.452, ...), kind=kOutput, calls=%fused_computation.6 | convolution fusion | flops 5957484544 | bytes 42471424 | tf_op jit(solution)/shard_map/dot_general | solution.py:34
  242.4 9.8 %convolution_convert_fusion.4 = bf16[2816,1024]{1,0:T(8,128)(2,1)S(1)} fusion(bf16[1024,2816]{0,1:T(8,128)(2,1)} %get-tuple-element.75, bf16[1024,1024]{0,1:T(8,128)(2,1)} %copy-done.39), kind=kOutput, calls=%fused_computation.24 | convolution fusion | flops 5908463616 | bytes 13631488 | tf_op jit(solution)/shard_map/dot_general | solution.py:40
  257.6 6.7 %convolution_convert_fusion.3 = bf16[2816,1024]{1,0:T(8,128)(2,1)S(1)} fusion(bf16[1024,2816]{0,1:T(8,128)(2,1)S(1)} %copy-done.75, bf16[1024,1024]{0,1:T(8,128)(2,1)S(1)} %copy-done.40), kind=kOutput, calls=%fused_computation.23 | convolution fusion | flops 5908463616 | bytes 13631488 | tf_op jit(solution)/shard_map/dot_general | solution.py:40
  264.3 9.2 %convolution_convert_fusion.2 = bf16[2816,1024]{0,1:T(8,128)(2,1)S(1)} fusion(bf16[1024,2816]{0,1:T(8,128)(2,1)} %get-tuple-element.81, bf16[1024,1024]{1,0:T(8,128)(2,1)S(1)} %copy-done.36), kind=kOutput, calls=%fused_computation.22 | convolution fusion | flops 5908463616 | bytes 13631488 | tf_op jit(solution)/shard_map/dot_general | solution.py:40
  285.7 13.2 %fusion.12 = f32[1024,1024]{0,1:T(8,128)} fusion(bf16[1024,2816]{0,1:T(8,128)(2,1)} %get-tuple-element.75, bf16[2816,256]{1,0:T(8,128)(2,1)} %bitcast.453, bf16[2816,384]{1,0:T(8,128)(2,1)} %bitcast.431, bf16[2816,384]{1,0:T(8,128)(2,1)} %bitcast.433), kind=kOutput, calls=%fused_computation.45 | convolution fusion | flops 5922881536 | bytes 15728640 | tf_op jit(solution)/shard_map/dot_general | solution.py:30
  298.9 11.9 %multiply_reduce_fusion.1 = (f32[1024]{0:T(1024)S(1)}, f32[1024,1024]{0,1:T(8,128)}) fusion(f32[1024,1024]{0,1:T(8,128)S(1)} %copy-done.9, f32[1024,1024]{0,1:T(8,128)} %fusion.12, bf16[1024,2816]{0,1:T(8,128)(2,1)} %get-tuple-element.76, bf16[2816,256]{1,0:T(8,128)(2,1)S(1)} %bitcast.451, bf16[2816,384]{1,0:T(8,128)(2,1)S(1)} %bitcast.427, ...), kind=kOutput, calls=%fused_computation.36 | convolution fusion | flops 5926026240 | bytes 24121344 | tf_op jit(solution)/shard_map/dot_general | solution.py:30
  324.5 20.2 %lightning_backward.1 = (bf16[1024,1024]{1,0:T(8,128)(2,1)}, bf16[1024,1024]{1,0:T(8,128)(2,1)}, bf16[1024,1024]{1,0:T(8,128)(2,1)}) custom-call(s32[1]{0:T(128)} %copy.166.count_ref, f32[8]{0:T(128)} %exponential_multiply_fusion.slope_ref, f32[1024,1024]{1,0:T(8,128)} %fusion.58.query_ref, f32[1024,1024]{1,0:T(8,128)} %fusion.43.key_ref, ...), custom_call_target="tpu_custom_call" | custom-call | tf_op jit(solution)/shard_map/lightning_backward/pallas_call | solution.py:188
  369.2 9.1 %add_convert_fusion = bf16[1024,1024]{0,1:T(8,128)(2,1)} fusion(f32[1024,1024]{0,1:T(8,128)S(1)} %copy-done.10, bf16[1024,2816]{1,0:T(8,128)(2,1)S(1)} %bitcast.495, bf16[1024,2816]{0,1:T(8,128)(2,1)} %get-tuple-element.81), kind=kOutput, calls=%fused_computation.32 | convolution fusion | flops 5907677184 | bytes 17825792 | tf_op jit(solution)/shard_map/dot_general | solution.py:34
  412.9 18.8 %collective-permute-done.34 = bf16[2,2,2,5,32,384]{5,4,3,1,0,2:T(8,128)(2,1)} collective-permute-done((bf16[2,2,2,5,32,384]{5,4,3,1,0,2:T(8,128)(2,1)}, bf16[2,2,2,5,32,384]{5,4,3,1,0,2:T(8,128)(2,1)}, u32[]{:S(2)}, u32[]{:S(2)}) %collective-permute-start.34) | collective-permute-done | bytes 983072 | tf_op jit(solution)/shard_map/ppermute | solution.py:230
  433.7 6.2 %collective-permute-done.31 = bf16[2,2,2,5,32,384]{5,4,3,0,2,1:T(8,128)(2,1)S(1)} collective-permute-done((bf16[2,2,2,5,32,384]{5,4,3,0,2,1:T(8,128)(2,1)S(1)}, bf16[2,2,2,5,32,384]{5,4,3,0,2,1:T(8,128)(2,1)S(1)}, u32[]{:S(2)}, u32[]{:S(2)}) %collective-permute-start.31) | collective-permute-done | bytes 983072 | tf_op jit(solution)/shard_map/ppermute | solution.py:230
  440.9 9.1 %collective-permute-done.38 = bf16[2,2,5,32,256]{4,3,2,0,1:T(8,128)(2,1)S(1)} collective-permute-done((bf16[2,2,5,32,256]{4,3,2,0,1:T(8,128)(2,1)S(1)}, bf16[2,2,5,32,256]{4,3,2,0,1:T(8,128)(2,1)S(1)}, u32[]{:S(2)}, u32[]{:S(2)}) %collective-permute-start.38) | collective-permute-done | bytes 327712 | tf_op jit(solution)/shard_map/ppermute | solution.py:230
  450.3 6.9 %collective-permute-done.35 = bf16[2,2,5,32,384]{4,3,2,1,0:T(8,128)(2,1)S(1)} collective-permute-done((bf16[2,2,5,32,384]{4,3,2,1,0:T(8,128)(2,1)S(1)}, bf16[2,2,5,32,384]{4,3,2,1,0:T(8,128)(2,1)S(1)}, u32[]{:S(2)}, u32[]{:S(2)}) %collective-permute-start.35) | collective-permute-done | bytes 491552 | tf_op jit(solution)/shard_map/ppermute | solution.py:230
  463.7 13.1 %collective-permute-done.33 = bf16[2,5,32,384]{3,2,1,0:T(8,128)(2,1)S(1)} collective-permute-done((bf16[2,5,32,384]{3,2,1,0:T(8,128)(2,1)S(1)}, bf16[2,5,32,384]{3,2,1,0:T(8,128)(2,1)S(1)}, u32[]{:S(2)}, u32[]{:S(2)}) %collective-permute-start.33) | collective-permute-done | bytes 245792 | tf_op jit(solution)/shard_map/ppermute | solution.py:230
  487.5 6.1 %collective-permute-done.40 = bf16[5,32,1024]{2,1,0:T(8,128)(2,1)S(1)} collective-permute-done((bf16[5,32,1024]{2,1,0:T(8,128)(2,1)S(1)}, bf16[5,32,1024]{2,1,0:T(8,128)(2,1)S(1)}, u32[]{:S(2)}, u32[]{:S(2)}) %collective-permute-start.40) | collective-permute-done | bytes 327712 | tf_op jit(solution)/shard_map/ppermute | solution.py:230
  494.6 18.2 %reduce-scatter.2.cloned.1.call-done = bf16[288,1024]{1,0:T(8,128)(2,1)} async-done(((bf16[9216,1024]{1,0:T(8,128)(2,1)}), bf16[288,1024]{1,0:T(8,128)(2,1)}) %reduce-scatter.2.cloned.1.call-update) | async-done | bytes 589840 | tf_op jit(solution)/shard_map/reduce_scatter | solution.py:363
  (435 shorter events, 243.7 us)
Async XLA Ops:
  7.2 505.6 %reduce-scatter.2.cloned.1.call-start = ((), (), s32[]{:S(2)}) async-start(), calls=%async_computation.1 | async-start | bytes 19464192 | tf_op jit(solution)/shard_map/reduce_scatter | solution.py:363
  11.4 18.8 %collective-permute-start = (bf16[160,1024]{1,0:T(8,128)(2,1)S(1)}, bf16[160,1024]{1,0:T(8,128)(2,1)S(1)}, u32[]{:S(2)}, u32[]{:S(2)}) collective-permute-start(bf16[160,1024]{1,0:T(8,128)(2,1)S(1)} %bitcast_dynamic-update-slice_fusion.2), channel_id=1, source_target_pairs={{0,4},{1,5},{2,6},{3,7},{4,0},{5,1},{6,2},{7,3},{8,12},{9,13},{10,... | collective-permute-start | bytes 983048 | tf_op jit(solution)/shard_map/ppermute | solution.py:230
  35.3 27.4 %collective-permute-start.7 = (bf16[272,1024]{1,0:T(8,128)(2,1)S(1)}, bf16[272,1024]{1,0:T(8,128)(2,1)S(1)}, u32[]{:S(2)}, u32[]{:S(2)}) collective-permute-start(bf16[272,1024]{1,0:T(8,128)(2,1)S(1)} %fusion.61), channel_id=1, source_target_pairs={{0,4},{1,5},{2,6},{3,7},{4,0},{5,1},{6,2},{7,3},{8,12},{9,13},{10,... | collective-permute-start | bytes 1671176 | tf_op jit(solution)/shard_map/ppermute | solution.py:230
  41.5 21.5 %collective-permute-start.2 = (bf16[2,2,160,384]{3,2,0,1:T(8,128)(2,1)S(1)}, bf16[2,2,160,384]{3,2,0,1:T(8,128)(2,1)S(1)}, u32[]{:S(2)}, u32[]{:S(2)}) collective-permute-start(bf16[2,2,160,384]{3,2,0,1:T(8,128)(2,1)S(1)} %maximum_select_fusion.45), channel_id=1, source_target_pairs={{0,1},{1,0},{2,3},{3,2},{4,5},{5,4},{6,7},{7,6},{8,9},{9,8},{10,11... | collective-permute-start | bytes 1474568 | tf_op jit(solution)/shard_map/ppermute | solution.py:230
  42.6 21.9 %collective-permute-start.4 = (bf16[2,2,160,384]{3,2,1,0:T(8,128)(2,1)S(1)}, bf16[2,2,160,384]{3,2,1,0:T(8,128)(2,1)S(1)}, u32[]{:S(2)}, u32[]{:S(2)}) collective-permute-start(bf16[2,2,160,384]{3,2,1,0:T(8,128)(2,1)S(1)} %maximum_select_fusion.47), channel_id=1, source_target_pairs={{0,2},{1,3},{2,0},{3,1},{4,6},{5,7},{6,4},{7,5},{8,10},{9,11},{10,... | collective-permute-start | bytes 1474568 | tf_op jit(solution)/shard_map/ppermute | solution.py:230
  64.7 31.6 %collective-permute-start.8 = (bf16[2,2,2,160,384]{4,3,0,1,2:T(8,128)(2,1)S(1)}, bf16[2,2,2,160,384]{4,3,0,1,2:T(8,128)(2,1)S(1)}, u32[]{:S(2)}, u32[]{:S(2)}) collective-permute-start(bf16[2,2,2,160,384]{4,3,0,1,2:T(8,128)(2,1)S(1)} %maximum_select_fusion.14), channel_id=1, source_target_pairs={{0,16},{8,24},{16,0},{24,8},{1,17},{9,25},{17,1},{25,9},{2,18},{10... | collective-permute-start | bytes 2949128 | tf_op jit(solution)/shard_map/ppermute | solution.py:230
  64.8 31.2 %collective-permute-start.10 = (bf16[2,2,2,160,256]{4,3,1,2,0:T(8,128)(2,1)S(1)}, bf16[2,2,2,160,256]{4,3,1,2,0:T(8,128)(2,1)S(1)}, u32[]{:S(2)}, u32[]{:S(2)}) collective-permute-start(bf16[2,2,2,160,256]{4,3,1,2,0:T(8,128)(2,1)S(1)} %maximum_select_fusion.35), channel_id=1, source_target_pairs={{0,2},{1,3},{2,0},{3,1},{4,6},{5,7},{6,4},{7,5},{8,10},{9,11},{10,... | collective-permute-start | bytes 1966088 | tf_op jit(solution)/shard_map/ppermute | solution.py:230
  64.8 23.2 %collective-permute-start.11 = (bf16[2,272,384]{2,1,0:T(8,128)(2,1)S(1)}, bf16[2,272,384]{2,1,0:T(8,128)(2,1)S(1)}, u32[]{:S(2)}, u32[]{:S(2)}) collective-permute-start(bf16[2,272,384]{2,1,0:T(8,128)(2,1)S(1)} %get-tuple-element.58), channel_id=1, source_target_pairs={{0,2},{1,3},{2,0},{3,1},{4,6},{5,7},{6,4},{7,5},{8,10},{9,11},{10,... | collective-permute-start | bytes 1253384 | tf_op jit(solution)/shard_map/ppermute | solution.py:230
  67.4 27.6 %collective-permute-start.12 = (bf16[2,272,384]{2,1,0:T(8,128)(2,1)S(1)}, bf16[2,272,384]{2,1,0:T(8,128)(2,1)S(1)}, u32[]{:S(2)}, u32[]{:S(2)}) collective-permute-start(bf16[2,272,384]{2,1,0:T(8,128)(2,1)S(1)} %get-tuple-element.59), channel_id=1, source_target_pairs={{0,16},{8,24},{16,0},{24,8},{1,17},{9,25},{17,1},{25,9},{2,18},{10... | collective-permute-start | bytes 1253384 | tf_op jit(solution)/shard_map/ppermute | solution.py:230
  74.6 23.6 %collective-permute-start.9 = (bf16[2,2,2,160,384]{4,3,1,0,2:T(8,128)(2,1)S(1)}, bf16[2,2,2,160,384]{4,3,1,0,2:T(8,128)(2,1)S(1)}, u32[]{:S(2)}, u32[]{:S(2)}) collective-permute-start(bf16[2,2,2,160,384]{4,3,1,0,2:T(8,128)(2,1)S(1)} %maximum_select_fusion.15), channel_id=1, source_target_pairs={{0,1},{1,0},{2,3},{3,2},{4,5},{5,4},{6,7},{7,6},{8,9},{9,8},{10,11... | collective-permute-start | bytes 2949128 | tf_op jit(solution)/shard_map/ppermute | solution.py:230
  103.1 26.4 %collective-permute-start.16 = (bf16[2,2,2,2,160,256]{5,4,1,3,0,2:T(8,128)(2,1)S(1)}, bf16[2,2,2,2,160,256]{5,4,1,3,0,2:T(8,128)(2,1)S(1)}, u32[]{:S(2)}, u32[]{:S(2)}) collective-permute-start(bf16[2,2,2,2,160,256]{5,4,1,3,0,2:T(8,128)(2,1)S(1)} %maximum_select_fusion.11), channel_id=1, source_target_pairs={{0,8},{8,0},{16,24},{24,16},{1,9},{9,1},{17,25},{25,17},{2,10},{10... | collective-permute-start | bytes 3932168 | tf_op jit(solution)/shard_map/ppermute | solution.py:230
  103.2 28.1 %collective-permute-start.15 = (bf16[2,2,2,2,160,384]{5,4,1,0,2,3:T(8,128)(2,1)}, bf16[2,2,2,2,160,384]{5,4,1,0,2,3:T(8,128)(2,1)S(1)}, u32[]{:S(2)}, u32[]{:S(2)}) collective-permute-start(bf16[2,2,2,2,160,384]{5,4,1,0,2,3:T(8,128)(2,1)} %maximum_select_fusion.6), channel_id=1, source_target_pairs={{0,8},{8,0},{16,24},{24,16},{1,9},{9,1},{17,25},{25,17},{2,10},{10... | collective-permute-start | bytes 5898248 | tf_op jit(solution)/shard_map/ppermute | solution.py:230
  103.7 28.3 %collective-permute-start.14 = (bf16[2,2,2,2,160,384]{5,4,3,2,1,0:T(8,128)(2,1)}, bf16[2,2,2,2,160,384]{5,4,3,2,1,0:T(8,128)(2,1)S(1)}, u32[]{:S(2)}, u32[]{:S(2)}) collective-permute-start(bf16[2,2,2,2,160,384]{5,4,3,2,1,0:T(8,128)(2,1)} %copy_select_fusion.1), channel_id=1, source_target_pairs={{0,8},{8,0},{16,24},{24,16},{1,9},{9,1},{17,25},{25,17},{2,10},{10... | collective-permute-start | bytes 5898248 | tf_op jit(solution)/shard_map/ppermute | solution.py:230
  103.8 21.1 %collective-permute-start.17 = (bf16[2,2,272,384]{3,2,1,0:T(8,128)(2,1)}, bf16[2,2,272,384]{3,2,1,0:T(8,128)(2,1)S(1)}, u32[]{:S(2)}, u32[]{:S(2)}) collective-permute-start(bf16[2,2,272,384]{3,2,1,0:T(8,128)(2,1)} %maximum_select_fusion.16), channel_id=1, source_target_pairs={{0,1},{1,0},{2,3},{3,2},{4,5},{5,4},{6,7},{7,6},{8,9},{9,8},{10,11... | collective-permute-start | bytes 2506760 | tf_op jit(solution)/shard_map/ppermute | solution.py:230
  133.4 37.9 %collective-permute-start.20 = (bf16[2,2,2,272,384]{4,3,2,1,0:T(8,128)(2,1)}, bf16[2,2,2,272,384]{4,3,2,1,0:T(8,128)(2,1)}, u32[]{:S(2)}, u32[]{:S(2)}) collective-permute-start(bf16[2,2,2,272,384]{4,3,2,1,0:T(8,128)(2,1)} %maximum_select_fusion.7), channel_id=1, source_target_pairs={{0,16},{8,24},{16,0},{24,8},{1,17},{9,25},{17,1},{25,9},{2,18},{10... | collective-permute-start | bytes 5013512 | tf_op jit(solution)/shard_map/ppermute | solution.py:230
  134.1 40.5 %collective-permute-start.21 = (bf16[2,2,2,272,384]{4,3,1,0,2:T(8,128)(2,1)}, bf16[2,2,2,272,384]{4,3,1,0,2:T(8,128)(2,1)}, u32[]{:S(2)}, u32[]{:S(2)}) collective-permute-start(bf16[2,2,2,272,384]{4,3,1,0,2:T(8,128)(2,1)} %maximum_select_fusion.8), channel_id=1, source_target_pairs={{0,1},{1,0},{2,3},{3,2},{4,5},{5,4},{6,7},{7,6},{8,9},{9,8},{10,11... | collective-permute-start | bytes 5013512 | tf_op jit(solution)/shard_map/ppermute | solution.py:230
  135.6 33.0 %collective-permute-start.22 = (bf16[2,2,2,272,256]{4,3,1,2,0:T(8,128)(2,1)}, bf16[2,2,2,272,256]{4,3,1,2,0:T(8,128)(2,1)}, u32[]{:S(2)}, u32[]{:S(2)}) collective-permute-start(bf16[2,2,2,272,256]{4,3,1,2,0:T(8,128)(2,1)} %maximum_select_fusion.13), channel_id=1, source_target_pairs={{0,2},{1,3},{2,0},{3,1},{4,6},{5,7},{6,4},{7,5},{8,10},{9,11},{10,... | collective-permute-start | bytes 3342344 | tf_op jit(solution)/shard_map/ppermute | solution.py:230
  367.2 19.8 %collective-permute-start.26 = (bf16[2,2,2,2,32,1024]{5,4,1,3,0,2:T(8,128)(2,1)}, bf16[2,2,2,2,32,1024]{5,4,1,3,0,2:T(8,128)(2,1)S(1)}, u32[]{:S(2)}, u32[]{:S(2)}) collective-permute-start(bf16[2,2,2,2,32,1024]{5,4,1,3,0,2:T(8,128)(2,1)} %bitcast.394), channel_id=1, source_target_pairs={{0,8},{8,0},{16,24},{24,16},{1,9},{9,1},{17,25},{25,17},{2,10},{10... | collective-permute-start | bytes 3145736 | tf_op jit(solution)/shard_map/ppermute | solution.py:230
  390.8 19.1 %collective-permute-start.37 = (bf16[2,2,2,5,32,256]{5,4,3,1,2,0:T(8,128)(2,1)}, bf16[2,2,2,5,32,256]{5,4,3,1,2,0:T(8,128)(2,1)}, u32[]{:S(2)}, u32[]{:S(2)}) collective-permute-start(bf16[2,2,2,5,32,256]{5,4,3,1,2,0:T(8,128)(2,1)} %dynamic-slice_bitcast_fusion.2), channel_id=1, source_target_pairs={{0,2},{1,3},{2,0},{3,1},{4,6},{5,7},{6,4},{7,5},{8,10},{9,11},{10,... | collective-permute-start | bytes 1966088 | tf_op jit(solution)/shard_map/ppermute | solution.py:230
  395.3 36.3 %collective-permute-start.34 = (bf16[2,2,2,5,32,384]{5,4,3,1,0,2:T(8,128)(2,1)}, bf16[2,2,2,5,32,384]{5,4,3,1,0,2:T(8,128)(2,1)}, u32[]{:S(2)}, u32[]{:S(2)}) collective-permute-start(bf16[2,2,2,5,32,384]{5,4,3,1,0,2:T(8,128)(2,1)} %dynamic-slice_bitcast_fusion), channel_id=1, source_target_pairs={{0,1},{1,0},{2,3},{3,2},{4,5},{5,4},{6,7},{7,6},{8,9},{9,8},{10,11... | collective-permute-start | bytes 2949128 | tf_op jit(solution)/shard_map/ppermute | solution.py:230
  406.8 33.1 %collective-permute-start.31 = (bf16[2,2,2,5,32,384]{5,4,3,0,2,1:T(8,128)(2,1)S(1)}, bf16[2,2,2,5,32,384]{5,4,3,0,2,1:T(8,128)(2,1)S(1)}, u32[]{:S(2)}, u32[]{:S(2)}) collective-permute-start(bf16[2,2,2,5,32,384]{5,4,3,0,2,1:T(8,128)(2,1)S(1)} %dynamic-slice_bitcast_fusion.1), channel_id=1, source_target_pairs={{0,16},{8,24},{16,0},{24,8},{1,17},{9,25},{17,1},{25,9},{2,18},{10... | collective-permute-start | bytes 2949128 | tf_op jit(solution)/shard_map/ppermute | solution.py:230
  411.3 38.7 %collective-permute-start.38 = (bf16[2,2,5,32,256]{4,3,2,0,1:T(8,128)(2,1)S(1)}, bf16[2,2,5,32,256]{4,3,2,0,1:T(8,128)(2,1)S(1)}, u32[]{:S(2)}, u32[]{:S(2)}) collective-permute-start(bf16[2,2,5,32,256]{4,3,2,0,1:T(8,128)(2,1)S(1)} %dynamic-slice_bitcast_fusion.6), channel_id=1, source_target_pairs={{0,16},{8,24},{16,0},{24,8},{1,17},{9,25},{17,1},{25,9},{2,18},{10... | collective-permute-start | bytes 983048 | tf_op jit(solution)/shard_map/ppermute | solution.py:230
  433.2 24.0 %collective-permute-start.35 = (bf16[2,2,5,32,384]{4,3,2,1,0:T(8,128)(2,1)S(1)}, bf16[2,2,5,32,384]{4,3,2,1,0:T(8,128)(2,1)S(1)}, u32[]{:S(2)}, u32[]{:S(2)}) collective-permute-start(bf16[2,2,5,32,384]{4,3,2,1,0:T(8,128)(2,1)S(1)} %dynamic-slice_bitcast_fusion.3), channel_id=1, source_target_pairs={{0,2},{1,3},{2,0},{3,1},{4,6},{5,7},{6,4},{7,5},{8,10},{9,11},{10,... | collective-permute-start | bytes 1474568 | tf_op jit(solution)/shard_map/ppermute | solution.py:230
  440.3 21.2 %collective-permute-start.32 = (bf16[2,2,5,32,384]{4,3,2,0,1:T(8,128)(2,1)S(1)}, bf16[2,2,5,32,384]{4,3,2,0,1:T(8,128)(2,1)S(1)}, u32[]{:S(2)}, u32[]{:S(2)}) collective-permute-start(bf16[2,2,5,32,384]{4,3,2,0,1:T(8,128)(2,1)S(1)} %dynamic-slice_bitcast_fusion.4), channel_id=1, source_target_pairs={{0,1},{1,0},{2,3},{3,2},{4,5},{5,4},{6,7},{7,6},{8,9},{9,8},{10,11... | collective-permute-start | bytes 1474568 | tf_op jit(solution)/shard_map/ppermute | solution.py:230
  (98 other events, 1139.7 us)
Sparse Core Ops, SparseCore 0:
  282.7 229.9 reduce-scatter.1

commit v7 on v6

--- a/solution.py
+++ b/solution.py
@@ -319,31 +319,56 @@
 
 
 class Scatter:
-    def __init__(self, terms):
+    def __init__(self, terms, single=False):
         self.cube = Cube()
-        digits = len(self.cube.bits)
         bit = self.cube.bits[self.cube.core]
-        blocks = [term.reshape((2,) * digits + (-1, D)) for term in terms]
+        shape = (2,) * len(self.cube.bits)
+        blocks = [term.reshape(shape + (-1, term.shape[-1])) for term in terms]
         self.own = [pick(block, self.cube.core, bit.place) for block in blocks]
         self.sent = [pick(block, self.cube.core, 1 - bit.place) for block in blocks]
-
-    def meet(self, value, label, left):
+        self.streams = self.cube.streams[:1] if single else self.cube.streams
+        self.stage = 0
+
+    def to_core(self):
+        bit = self.cube.bits[self.cube.core]
+        sums = [add_low(own, bit.swap(sent)) for own, sent in zip(self.own, self.sent)]
+        value = jnp.stack(sums, axis=-3)
+        self.parts = [value] if len(self.streams) == 1 else self.cube.columns(value)
+
+    def halves(self, value, label, left):
         bit = self.cube.bits[label]
         axis = sum(other < label for other in left)
-        return add_low(pick(value, axis, bit.place), bit.swap(pick(value, axis, 1 - bit.place)))
+        return pick(value, axis, bit.place), pick(value, axis, 1 - bit.place)
+
+    def send(self):
+        self.own, self.sent, self.labels = [], [], []
+        far = self.cube.far
+        if self.stage == len(self.streams[0]):
+            self.parts = [jnp.concatenate(self.parts, axis=-1)]
+        for index, part in enumerate(self.parts):
+            order = self.streams[index] + far
+            left = order[self.stage :] if self.stage >= len(self.streams[0]) else (
+                far + self.streams[index][self.stage :]
+            )
+            own, sent = self.halves(part, order[self.stage], left)
+            self.own.append(own)
+            self.sent.append(sent)
+            self.labels.append(order[self.stage])
+        self.stage += 1
+
+    def meet(self):
+        bits = self.cube.bits
+        self.parts = [
+            add_low(own, bits[label].swap(sent))
+            for own, sent, label in zip(self.own, self.sent, self.labels)
+        ]
 
     def finish(self):
-        bit = self.cube.bits[self.cube.core]
-        sums = [add_low(own, bit.swap(sent)) for own, sent in zip(self.own, self.sent)]
-        parts = self.cube.columns(jnp.stack(sums, axis=-3))
-        for stage in range(len(self.cube.streams[0])):
-            for index, stream in enumerate(self.cube.streams):
-                left = self.cube.far + stream[stage:]
-                parts[index] = self.meet(parts[index], stream[stage], left)
-        value = jnp.concatenate(parts, axis=-1)
-        for position, label in enumerate(self.cube.far):
-            value = self.meet(value, label, self.cube.far[position:])
-        return [jnp.transpose(value[index].astype(jnp.float32)) for index in range(len(sums))]
+        while self.stage < len(self.streams[0]) + len(self.cube.far):
+            self.send()
+            self.meet()
+        (value,) = self.parts
+        return [jnp.transpose(value[index].astype(jnp.float32)) for index in range(value.shape[0])]
 
 
 def scatter_call(terms, shards):
@@ -376,6 +401,10 @@
 
 def tie(values):
     return lax.optimization_barrier(values)
+
+
+def after(earlier, value):
+    return tie((earlier, value))[1]
 
 
 def weight_term(left, right):
@@ -400,21 +429,21 @@
     glu = Gather((first_weight, second_weight, down_weight))
     last = len(glu.cube.streams[0])
     heads.begin()
-    heads.parts, glu.value = tie((heads.parts, glu.value))
+    glu.value = after(heads.parts, glu.value)
+    heads.advance(last - 1)
     glu.begin()
-    heads.advance(last - 1)
-    heads.parts, glu.parts = tie((heads.parts, glu.parts))
+    glu.parts = after(heads.parts, glu.parts)
     heads.advance(1)
     glu.advance(last - 2)
-    heads.parts, glu.parts = tie((heads.parts, glu.parts))
+    glu.parts = after(heads.parts, glu.parts)
+    query_t, key_t, value_t, gate_t, out_t = heads.finish(shards)
     glu.advance(1)
-    query_t, key_t, value_t, gate_t, out_t = heads.finish(shards)
     inputs_f = inputs.astype(jnp.float32)
     length = inputs.shape[0]
     mask = (lax.iota(jnp.int32, length) < lengths[0]).astype(jnp.float32)[:, None]
     tables = make_tables(length)
     normed = simple_norm(inputs_f).astype(jnp.bfloat16)
-    query_t, glu.parts = tie((query_t, glu.parts))
+    glu.parts = after(query_t, glu.parts)
     glu.advance(1)
     query_pre = back_dot(normed, query_t)
     key_pre = back_dot(normed, key_t)
@@ -430,27 +459,32 @@
     first = back_dot(normed_two, first_t).astype(jnp.bfloat16)
     second = back_dot(normed_two, second_t).astype(jnp.bfloat16)
     product_low = (first.astype(jnp.float32) * second * mask).astype(jnp.bfloat16)
-    product_grad = forward_dot(cotangent, down_t)
+    down = Scatter([weight_term(cotangent, product_low)], single=True)
+    product_grad = forward_dot(after(down.sent, cotangent), down_t)
     first_low = (product_grad * second * mask).astype(jnp.bfloat16)
     second_low = (product_grad * first * mask).astype(jnp.bfloat16)
+    down.to_core()
+    down.send()
+    first_low, second_low, down.sent = tie((first_low, second_low, down.sent))
     stacked, widths = scatter_call(
-        [
-            weight_term(first_low, normed_two),
-            weight_term(second_low, normed_two),
-            weight_term(cotangent, product_low),
-        ],
-        shards,
+        [weight_term(first_low, normed_two), weight_term(second_low, normed_two)], shards
     )
     first_low, second_low, product_low, stacked = tie(
         (first_low, second_low, product_low, stacked)
     )
-    first_sum, second_sum, down_sum = scatter_sums(stacked, widths)
+    first_sum, second_sum = scatter_sums(stacked, widths)
     normed_two_grad = forward_dot(first_low, first_t) + forward_dot(second_low, second_t)
+    down.meet()
+    down.send()
+    normed_two_grad, down.sent = tie((normed_two_grad, down.sent))
     mixed_grad = cotangent.astype(jnp.float32) + norm_back(mixed, normed_two_grad)
     mixed_low = mixed_grad.astype(jnp.bfloat16)
     gated_grad = forward_dot(mixed_low, out_t)
     gate_low = (gated_grad * attended_norm * mask).astype(jnp.bfloat16)
     attended_low = norm_back(attended, gated_grad * gate_pre * mask).astype(jnp.bfloat16)
+    down.meet()
+    down.send()
+    attended_low, down.sent = tie((attended_low, down.sent))
     query_low, key_low, value_low = lightning_backward(
         lengths, query_pre, key_pre, value_pre, attended_low, tables
     )
@@ -463,8 +497,11 @@
             weight_term(value_low, normed),
         ]
     )
-    query_low, key_low, value_low, gate_low, product_low, attention.sent = tie(
-        (query_low, key_low, value_low, gate_low, product_low, attention.sent)
+    down.meet()
+    attention.to_core()
+    attention.send()
+    query_low, key_low, value_low, gate_low, product_low, attention.sent, down.parts = tie(
+        (query_low, key_low, value_low, gate_low, product_low, attention.sent, down.parts)
     )
     result = mixed + back_dot(product_low, down_t)
     normed_grad = (
@@ -474,6 +511,8 @@
         + forward_dot(gate_low, gate_t)
     )
     input_grad = mixed_grad + norm_back(inputs_f, normed_grad)
+    attention.meet()
+    (down_sum,) = down.finish()
     out_sum, gate_sum, query_sum, key_sum, value_sum = attention.finish()
     return (
         result.astype(jnp.bfloat16),

time: 529 us -> 509 us (0.962)
  waiting for transfers between devices: 153 us -> 113 us
  other arithmetic: 56.3 us -> 72.6 us
  local copies, waits for them, and re-layouts: 81.4 us -> 73.3 us
  starting transfers between devices: 36.2 us -> 41.9 us
    ppermute x41 -> x46, waiting for transfers between devices: 135 us -> 113 us  [swap(): return lax.ppermute(value, self.name, pairs)]
    reduce_scatter x1, waiting for transfers between devices: 18.2 us -> 0.01 us  [scatter_sums(): summed = lax.psum_scatter(stacked, AXES, scatter_dimension=0, tiled=True)]
    unnamed x184 -> x201, local copies, waits for them, and re-layouts: 53.3 us -> 41.3 us
    concatenate x2, other arithmetic: 0.36 us -> 9.14 us  [the longest x1 9.06 us: scatter_call(): return (jnp.concatenate(pieces, axis=1).reshape(-1, D), widths)]
    dot_general x8, matrix products: 49.1 us -> 56.5 us  [forward_dot(): return jnp.dot(left, right, preferred_element_type=jnp.float32)]
    convert_element_type x10 -> x14, other arithmetic: 3.77 us -> 9.59 us  [add_low(): return total.astype(jnp.bfloat16)]
    ppermute x41 -> x46, starting transfers between devices: 36.1 us -> 41.9 us  [swap(): return lax.ppermute(value, self.name, pairs)]
    select_n x46 -> x49, other arithmetic: 26.8 us -> 27.7 us  [paired(): return jnp.where(self.place == 0, low, high)]
  transfers between devices with their start and end apart: 42 -> 47, of which waited for: 22 -> 17; matrix products, arithmetic and copies ran while one was open for 33% -> 45% of each run, Pallas kernels for 6% -> 7%
where the time goes in v7:
time: 509 us; the launch traced here: 502 us
  matrix products  150 us (29%)
  waiting for transfers between devices  113 us (22%)
  local copies, waits for them, and re-layouts  73.3 us (14%)
  other arithmetic  72.6 us (14%)
  starting transfers between devices  41.9 us (8%)
  Pallas kernels  33 us (6%)
  between operations  17.3 us (3%)
    ppermute x46, waiting for transfers between devices, swap(): return lax.ppermute(value, self.name, pairs)  113 us
    dot_general x8, matrix products, back_dot(): lax.dot_general(left, right, (((1,), (1,)), ((), ())), preferred_element_...  57.2 us
    dot_general x8, matrix products, forward_dot(): return jnp.dot(left, right, preferred_element_type=jnp.float32)  56.5 us
    ppermute x46, starting transfers between devices, swap(): return lax.ppermute(value, self.name, pairs)  41.9 us
    unnamed x201, local copies, waits for them, and re-layouts  41.3 us
    dot_general x8, matrix products, weight_dot(): lax.dot_general(left, right, (((0,), (0,)), ((), ())), preferred_element_...  36.5 us
    select_n x49, other arithmetic, paired(): return jnp.where(self.place == 0, low, high)  27.7 us
    pallas_call x1, Pallas kernels, lightning_backward(): pl.pallas_call(backward_kernel, grid=(HEADS,), in_specs=scalar_specs() +...  19.7 us
  transfers between devices with their start and end apart: 47, of which 17 were waited for; matrix products, arithmetic and copies ran while one was open for 45% of the time, Pallas kernels for 7%

profile of v7, /device:TPU:0, one launch (start us, length us, event | category | flops | bytes accessed | tf_op | source)
XLA Modules:
  0.0 501.6 jit_solution(4542093965062329833)
XLA Ops:
  24.0 6.3 %collective-permute-done = bf16[160,1024]{1,0:T(8,128)(2,1)S(1)} collective-permute-done((bf16[160,1024]{1,0:T(8,128)(2,1)S(1)}, bf16[160,1024]{1,0:T(8,128)(2,1)S(1)}, u32[]{:S(2)}, u32[]{:S(2)}) %collective-permute-start) | collective-permute-done | bytes 327712 | tf_op jit(solution)/shard_map/ppermute | solution.py:230
  47.8 14.0 %collective-permute-done.13 = bf16[272,1024]{1,0:T(8,128)(2,1)S(1)} collective-permute-done((bf16[272,1024]{1,0:T(8,128)(2,1)S(1)}, bf16[272,1024]{1,0:T(8,128)(2,1)S(1)}, u32[]{:S(2)}, u32[]{:S(2)}) %collective-permute-start.13) | collective-permute-done | bytes 557088 | tf_op jit(solution)/shard_map/ppermute | solution.py:230
  79.8 13.8 %collective-permute-done.15 = bf16[2,272,384]{2,1,0:T(8,128)(2,1)S(1)} collective-permute-done((bf16[2,272,384]{2,1,0:T(8,128)(2,1)S(1)}, bf16[2,272,384]{2,1,0:T(8,128)(2,1)S(1)}, u32[]{:S(2)}, u32[]{:S(2)}) %collective-permute-start.15) | collective-permute-done | bytes 417824 | tf_op jit(solution)/shard_map/ppermute | solution.py:230
  128.9 19.4 %collective-permute-done.22 = bf16[2,2,2,272,256]{4,3,1,2,0:T(8,128)(2,1)S(1)} collective-permute-done((bf16[2,2,2,272,256]{4,3,1,2,0:T(8,128)(2,1)S(1)}, bf16[2,2,2,272,256]{4,3,1,2,0:T(8,128)(2,1)S(1)}, u32[]{:S(2)}, u32[]{:S(2)}) %collective-permute-start.22) | collective-permute-done | bytes 1114144 | tf_op jit(solution)/shard_map/ppermute | solution.py:230
  165.5 4.9 fusion.62.query_ref
  170.4 13.3 %lightning_forward.1 = f32[1024,1024]{1,0:T(8,128)} custom-call(s32[1]{0:T(128)} %copy.177.count_ref, f32[8]{0:T(128)} %exponential_multiply_fusion.slope_ref, f32[1024,1024]{1,0:T(8,128)} %fusion.62.query_ref, f32[1024,1024]{1,0:T(8,128)} %fusion.45.key_ref, f32[1024,1024]{1,0:T(8,128)} %fusion.43.value_ref, f32[1024,128]{1,0:T(8,128)} %get-tuple-element.205.cosine_ref, ...), custom_call_target="tpu_custom_call" | custom-call | tf_op jit(solution)/shard_map/lightning_forward/pallas_call | solution.py:175
  194.8 5.4 %multiply_convert_fusion.2 = (bf16[1024,1024]{1,0:T(8,128)(2,1)}, f32[1024,1024]{1,0:T(8,128)}) fusion(f32[1024,1024]{1,0:T(8,128)S(1)} %copy-done, f32[1024]{0:T(1024)S(1)} %fusion.67, f32[1024]{0:T(1024)S(1)} %fusion.69, bf16[1024,256]{1,0:T(8,128)(2,1)S(1)} %bitcast.477, bf16[1024,384]{1,0:T(8,128)(2,1)S(1)} %bitcast.462, ...), kind=kOutput, calls=%fused_computation.41 | convolution fusion | flops 2161115136 | bytes 14692352 | tf_op jit(solution)/shard_map/dot_general | solution.py:34
  214.9 8.8 %convolution_convert_fusion.4 = bf16[1024,2816]{1,0:T(8,128)(2,1)} fusion(bf16[1024,1024]{0,1:T(8,128)(2,1)S(1)} %multiply_convert_fusion.1, bf16[2816,256]{1,0:T(8,128)(2,1)S(1)} %bitcast.497, bf16[2816,384]{1,0:T(8,128)(2,1)S(1)} %bitcast.475, bf16[2816,384]{1,0:T(8,128)(2,1)S(1)} %bitcast.471), kind=kOutput, calls=%fused_computation.26 | convolution fusion | flops 5925765120 | bytes 13631488 | tf_op jit(solution)/shard_map/dot_general | solution.py:34
  223.8 14.0 %fusion.3 = (bf16[1024,2816]{1,0:T(8,128)(2,1)}, bf16[1024,2816]{1,0:T(8,128)(2,1)}) fusion(bf16[1024,2816]{1,0:T(8,128)(2,1)} %convolution_convert_fusion.4, f32[1024]{0:T(1024)S(1)} %fusion.67, bf16[1024,1024]{0,1:T(8,128)(2,1)} %copy-done.39, bf16[2816,256]{1,0:T(8,128)(2,1)} %bitcast.499, bf16[2816,384]{1,0:T(8,128)(2,1)} %bitcast.473, ...), kind=kOutput, calls=%fused_computation.7 | convolution fusion | flops 5940183040 | bytes 25169920 | tf_op jit(solution)/shard_map/dot_general | solution.py:34
  237.8 9.5 %convolution_convert_fusion.2 = bf16[2816,1024]{0,1:T(8,128)(2,1)S(1)} fusion(bf16[1024,2816]{1,0:T(8,128)(2,1)} %get-tuple-element.76, bf16[1024,1024]{1,0:T(8,128)(2,1)S(1)} %copy-done.36), kind=kOutput, calls=%fused_computation.24 | convolution fusion | flops 5908463616 | bytes 13631488 | tf_op jit(solution)/shard_map/dot_general | solution.py:40
  257.1 12.7 %fusion.1 = (bf16[1024,2816]{1,0:T(8,128)(2,1)}, bf16[1024,2816]{1,0:T(8,128)(2,1)}) fusion(bf16[1024,2816]{1,0:T(8,128)(2,1)} %convolution_convert_fusion.4, f32[1024]{0:T(1024)S(1)} %fusion.67, bf16[1024,2816]{1,0:T(8,128)(2,1)} %get-tuple-element.211, bf16[1024,1024]{1,0:T(8,128)(2,1)S(1)} %copy-done.37, ...), kind=kOutput, calls=%fused_computation.5 | convolution fusion | flops 5928648704 | bytes 30937088 | tf_op jit(solution)/shard_map/dot_general | solution.py:30
  274.6 6.8 %convolution_convert_fusion.1 = bf16[2816,1024]{1,0:T(8,128)(2,1)S(1)} fusion(bf16[1024,2816]{1,0:T(8,128)(2,1)S(1)} %copy-done.88, bf16[1024,1024]{0,1:T(8,128)(2,1)S(1)} %copy-done.40), kind=kOutput, calls=%fused_computation.23 | convolution fusion | flops 5908463616 | bytes 13631488 | tf_op jit(solution)/shard_map/dot_general | solution.py:40
  281.5 6.6 %convolution_convert_fusion = bf16[2816,1024]{1,0:T(8,128)(2,1)S(1)} fusion(bf16[1024,2816]{1,0:T(8,128)(2,1)S(1)} %bitcast.540, bf16[1024,1024]{0,1:T(8,128)(2,1)S(1)} %copy-done.40), kind=kOutput, calls=%fused_computation.22 | convolution fusion | flops 5908463616 | bytes 13631488 | tf_op jit(solution)/shard_map/dot_general | solution.py:40
  288.2 9.1 %maximum_maximum_fusion = bf16[32,192,1024]{2,1,0:T(8,128)(2,1)} fusion(bf16[32,88,1024]{2,1,0:T(8,128)(2,1)S(1)} %bitcast.447, bf16[32,88,1024]{2,1,0:T(8,128)(2,1)S(1)} %bitcast.446, bf16[192]{0:T(256)(128)(2,1)S(1)} %copy-done.83), kind=kLoop, calls=%fused_computation.3 | loop fusion | flops 37748736 | bytes 24117632 | tf_op jit(solution)/shard_map/concatenate | solution.py:384
  297.2 12.1 %fusion.14 = f32[1024,1024]{0,1:T(8,128)} fusion(bf16[1024,2816]{1,0:T(8,128)(2,1)} %get-tuple-element.66, bf16[2816,256]{1,0:T(8,128)(2,1)S(1)} %bitcast.500, bf16[2816,384]{1,0:T(8,128)(2,1)} %bitcast.474, bf16[2816,384]{1,0:T(8,128)(2,1)} %bitcast.470), kind=kOutput, calls=%fused_computation.51 | convolution fusion | flops 5922881536 | bytes 15728640 | tf_op jit(solution)/shard_map/dot_general | solution.py:30
  310.7 12.7 %fusion.23 = f32[1024,1024]{0,1:T(8,128)S(1)} fusion(f32[1024,1024]{0,1:T(8,128)} %fusion.14, bf16[1024,2816]{1,0:T(8,128)(2,1)} %get-tuple-element.65, bf16[2816,256]{1,0:T(8,128)(2,1)S(1)} %bitcast.498, bf16[2816,384]{1,0:T(8,128)(2,1)} %bitcast.476, bf16[2816,384]{1,0:T(8,128)(2,1)} %bitcast.472), kind=kOutput, calls=%fused_computation.81 | convolution fusion | flops 5923930112 | bytes 19922944 | tf_op jit(solution)/shard_map/dot_general | solution.py:30
  350.2 19.7 %lightning_backward.1 = (bf16[1024,1024]{1,0:T(8,128)(2,1)}, bf16[1024,1024]{1,0:T(8,128)(2,1)}, bf16[1024,1024]{1,0:T(8,128)(2,1)}) custom-call(s32[1]{0:T(128)} %copy.177.count_ref, f32[8]{0:T(128)} %exponential_multiply_fusion.slope_ref, f32[1024,1024]{1,0:T(8,128)} %fusion.62.query_ref, f32[1024,1024]{1,0:T(8,128)} %fusion.45.key_ref, ...), custom_call_target="tpu_custom_call" | custom-call | tf_op jit(solution)/shard_map/lightning_backward/pallas_call | solution.py:188
  407.7 6.5 %fusion.12 = (f32[1024]{0:T(1024)S(1)}, f32[1024,1024]{0,1:T(8,128)S(1)}) fusion(bf16[1024,1024]{0,1:T(8,128)(2,1)S(1)} %copy-done.5, bf16[1024,1024]{1,0:T(8,128)(2,1)S(1)} %copy-done.11, bf16[1024,256]{1,0:T(8,128)(2,1)} %bitcast.478, bf16[1024,384]{1,0:T(8,128)(2,1)} %bitcast.461, bf16[1024,384]{1,0:T(8,128)(2,1)} %bitcast.459, ...), kind=kOutput, calls=%fused_computation.32 | convolution fusion | flops 2160065536 | bytes 23072768 | tf_op jit(solution)/shard_map/dot_general | solution.py:30
  414.2 11.2 %add_convert_fusion = bf16[1024,1024]{0,1:T(8,128)(2,1)} fusion(f32[1024,1024]{0,1:T(8,128)S(1)} %copy-done.8, bf16[1024,2816]{1,0:T(8,128)(2,1)} %get-tuple-element.76, bf16[1024,2816]{1,0:T(8,128)(2,1)} %copy-done.70), kind=kOutput, calls=%fused_computation.34 | convolution fusion | flops 5907677184 | bytes 17825792 | tf_op jit(solution)/shard_map/dot_general | solution.py:34
  428.8 5.5 %copy.112 = f32[1024,1024]{1,0:T(8,128)} copy(f32[1024,1024]{0,1:T(8,128)} %fusion.9) | data formatting | bytes 8388608
  449.2 6.8 %collective-permute-done.36 = bf16[2,2,5,32,384]{4,3,2,0,1:T(8,128)(2,1)S(1)} collective-permute-done((bf16[2,2,5,32,384]{4,3,2,0,1:T(8,128)(2,1)S(1)}, bf16[2,2,5,32,384]{4,3,2,0,1:T(8,128)(2,1)S(1)}, u32[]{:S(2)}, u32[]{:S(2)}) %collective-permute-start.36) | collective-permute-done | bytes 491552 | tf_op jit(solution)/shard_map/ppermute | solution.py:230
  457.4 4.9 collective-permute-done.39
  467.6 5.3 %collective-permute-done.40 = bf16[2,5,32,384]{3,2,1,0:T(8,128)(2,1)S(1)} collective-permute-done((bf16[2,5,32,384]{3,2,1,0:T(8,128)(2,1)S(1)}, bf16[2,5,32,384]{3,2,1,0:T(8,128)(2,1)S(1)}, u32[]{:S(2)}, u32[]{:S(2)}) %collective-permute-start.40) | collective-permute-done | bytes 245792 | tf_op jit(solution)/shard_map/ppermute | solution.py:230
  476.1 15.3 %collective-permute-done.44 = bf16[5,32,1024]{2,1,0:T(8,128)(2,1)S(1)} collective-permute-done((bf16[5,32,1024]{2,1,0:T(8,128)(2,1)S(1)}, bf16[5,32,1024]{2,1,0:T(8,128)(2,1)S(1)}, u32[]{:S(2)}, u32[]{:S(2)}) %collective-permute-start.44) | collective-permute-done | bytes 327712 | tf_op jit(solution)/shard_map/ppermute | solution.py:230
  (478 shorter events, 239.6 us)
Async XLA Ops:
  7.2 485.1 %reduce-scatter.2.cloned.1.call-start = ((), (), s32[]{:S(2)}) async-start(), calls=%async_computation.1 | async-start | bytes 12976128 | tf_op jit(solution)/shard_map/reduce_scatter | solution.py:388
  34.4 27.4 %collective-permute-start.13 = (bf16[272,1024]{1,0:T(8,128)(2,1)S(1)}, bf16[272,1024]{1,0:T(8,128)(2,1)S(1)}, u32[]{:S(2)}, u32[]{:S(2)}) collective-permute-start(bf16[272,1024]{1,0:T(8,128)(2,1)S(1)} %fusion.66), channel_id=1, source_target_pairs={{0,4},{1,5},{2,6},{3,7},{4,0},{5,1},{6,2},{7,3},{8,12},{9,13},{10,... | collective-permute-start | bytes 1671176 | tf_op jit(solution)/shard_map/ppermute | solution.py:230
  44.2 21.4 %collective-permute-start.6 = (bf16[2,2,160,384]{3,2,1,0:T(8,128)(2,1)S(1)}, bf16[2,2,160,384]{3,2,1,0:T(8,128)(2,1)S(1)}, u32[]{:S(2)}, u32[]{:S(2)}) collective-permute-start(bf16[2,2,160,384]{3,2,1,0:T(8,128)(2,1)S(1)} %maximum_select_fusion.49), channel_id=1, source_target_pairs={{0,2},{1,3},{2,0},{3,1},{4,6},{5,7},{6,4},{7,5},{8,10},{9,11},{10,... | collective-permute-start | bytes 1474568 | tf_op jit(solution)/shard_map/ppermute | solution.py:230
  47.3 32.3 %collective-permute-start.11 = (bf16[2,2,2,160,256]{4,3,1,2,0:T(8,128)(2,1)S(1)}, bf16[2,2,2,160,256]{4,3,1,2,0:T(8,128)(2,1)S(1)}, u32[]{:S(2)}, u32[]{:S(2)}) collective-permute-start(bf16[2,2,2,160,256]{4,3,1,2,0:T(8,128)(2,1)S(1)} %maximum_select_fusion.37), channel_id=1, source_target_pairs={{0,2},{1,3},{2,0},{3,1},{4,6},{5,7},{6,4},{7,5},{8,10},{9,11},{10,... | collective-permute-start | bytes 1966088 | tf_op jit(solution)/shard_map/ppermute | solution.py:230
  62.4 33.5 %collective-permute-start.3 = (bf16[2,2,2,160,384]{4,3,0,1,2:T(8,128)(2,1)S(1)}, bf16[2,2,2,160,384]{4,3,0,1,2:T(8,128)(2,1)S(1)}, u32[]{:S(2)}, u32[]{:S(2)}) collective-permute-start(bf16[2,2,2,160,384]{4,3,0,1,2:T(8,128)(2,1)S(1)} %maximum_select_fusion.15), channel_id=1, source_target_pairs={{0,16},{8,24},{16,0},{24,8},{1,17},{9,25},{17,1},{25,9},{2,18},{10... | collective-permute-start | bytes 2949128 | tf_op jit(solution)/shard_map/ppermute | solution.py:230
  67.7 25.9 %collective-permute-start.15 = (bf16[2,272,384]{2,1,0:T(8,128)(2,1)S(1)}, bf16[2,272,384]{2,1,0:T(8,128)(2,1)S(1)}, u32[]{:S(2)}, u32[]{:S(2)}) collective-permute-start(bf16[2,272,384]{2,1,0:T(8,128)(2,1)S(1)} %get-tuple-element.50), channel_id=1, source_target_pairs={{0,16},{8,24},{16,0},{24,8},{1,17},{9,25},{17,1},{25,9},{2,18},{10... | collective-permute-start | bytes 1253384 | tf_op jit(solution)/shard_map/ppermute | solution.py:230
  70.6 24.2 %collective-permute-start.14 = (bf16[2,272,384]{2,1,0:T(8,128)(2,1)S(1)}, bf16[2,272,384]{2,1,0:T(8,128)(2,1)S(1)}, u32[]{:S(2)}, u32[]{:S(2)}) collective-permute-start(bf16[2,272,384]{2,1,0:T(8,128)(2,1)S(1)} %get-tuple-element.49), channel_id=1, source_target_pairs={{0,2},{1,3},{2,0},{3,1},{4,6},{5,7},{6,4},{7,5},{8,10},{9,11},{10,... | collective-permute-start | bytes 1253384 | tf_op jit(solution)/shard_map/ppermute | solution.py:230
  74.9 22.8 %collective-permute-start.7 = (bf16[2,2,2,160,384]{4,3,1,0,2:T(8,128)(2,1)S(1)}, bf16[2,2,2,160,384]{4,3,1,0,2:T(8,128)(2,1)S(1)}, u32[]{:S(2)}, u32[]{:S(2)}) collective-permute-start(bf16[2,2,2,160,384]{4,3,1,0,2:T(8,128)(2,1)S(1)} %maximum_select_fusion.17), channel_id=1, source_target_pairs={{0,1},{1,0},{2,3},{3,2},{4,5},{5,4},{6,7},{7,6},{8,9},{9,8},{10,11... | collective-permute-start | bytes 2949128 | tf_op jit(solution)/shard_map/ppermute | solution.py:230
  100.0 21.4 %collective-permute-start.17 = (bf16[2,2,272,384]{3,2,1,0:T(8,128)(2,1)}, bf16[2,2,272,384]{3,2,1,0:T(8,128)(2,1)}, u32[]{:S(2)}, u32[]{:S(2)}) collective-permute-start(bf16[2,2,272,384]{3,2,1,0:T(8,128)(2,1)} %maximum_select_fusion.18), channel_id=1, source_target_pairs={{0,1},{1,0},{2,3},{3,2},{4,5},{5,4},{6,7},{7,6},{8,9},{9,8},{10,11... | collective-permute-start | bytes 2506760 | tf_op jit(solution)/shard_map/ppermute | solution.py:230
  108.7 41.3 %collective-permute-start.8 = (bf16[2,2,2,2,160,384]{5,4,1,0,2,3:T(8,128)(2,1)}, bf16[2,2,2,2,160,384]{5,4,1,0,2,3:T(8,128)(2,1)S(1)}, u32[]{:S(2)}, u32[]{:S(2)}) collective-permute-start(bf16[2,2,2,2,160,384]{5,4,1,0,2,3:T(8,128)(2,1)} %maximum_select_fusion.6), channel_id=1, source_target_pairs={{0,8},{8,0},{16,24},{24,16},{1,9},{9,1},{17,25},{25,17},{2,10},{10... | collective-permute-start | bytes 5898248 | tf_op jit(solution)/shard_map/ppermute | solution.py:230
  112.0 38.7 %collective-permute-start.4 = (bf16[2,2,2,2,160,384]{5,4,3,2,1,0:T(8,128)(2,1)S(1)}, bf16[2,2,2,2,160,384]{5,4,3,2,1,0:T(8,128)(2,1)S(1)}, u32[]{:S(2)}, u32[]{:S(2)}) collective-permute-start(bf16[2,2,2,2,160,384]{5,4,3,2,1,0:T(8,128)(2,1)S(1)} %copy-done.15), channel_id=1, source_target_pairs={{0,8},{8,0},{16,24},{24,16},{1,9},{9,1},{17,25},{25,17},{2,10},{10... | collective-permute-start | bytes 5898248 | tf_op jit(solution)/shard_map/ppermute | solution.py:230
  124.9 23.3 %collective-permute-start.22 = (bf16[2,2,2,272,256]{4,3,1,2,0:T(8,128)(2,1)S(1)}, bf16[2,2,2,272,256]{4,3,1,2,0:T(8,128)(2,1)S(1)}, u32[]{:S(2)}, u32[]{:S(2)}) collective-permute-start(bf16[2,2,2,272,256]{4,3,1,2,0:T(8,128)(2,1)S(1)} %maximum_select_fusion.13), channel_id=1, source_target_pairs={{0,2},{1,3},{2,0},{3,1},{4,6},{5,7},{6,4},{7,5},{8,10},{9,11},{10,... | collective-permute-start | bytes 3342344 | tf_op jit(solution)/shard_map/ppermute | solution.py:230
  127.8 55.8 %collective-permute-start.21 = (bf16[2,2,2,272,384]{4,3,1,0,2:T(8,128)(2,1)}, bf16[2,2,2,272,384]{4,3,1,0,2:T(8,128)(2,1)}, u32[]{:S(2)}, u32[]{:S(2)}) collective-permute-start(bf16[2,2,2,272,384]{4,3,1,0,2:T(8,128)(2,1)} %maximum_select_fusion.8), channel_id=1, source_target_pairs={{0,1},{1,0},{2,3},{3,2},{4,5},{5,4},{6,7},{7,6},{8,9},{9,8},{10,11... | collective-permute-start | bytes 5013512 | tf_op jit(solution)/shard_map/ppermute | solution.py:230
  128.3 59.7 %collective-permute-start.20 = (bf16[2,2,2,272,384]{4,3,2,1,0:T(8,128)(2,1)}, bf16[2,2,2,272,384]{4,3,2,1,0:T(8,128)(2,1)}, u32[]{:S(2)}, u32[]{:S(2)}) collective-permute-start(bf16[2,2,2,272,384]{4,3,2,1,0:T(8,128)(2,1)} %maximum_select_fusion.7), channel_id=1, source_target_pairs={{0,16},{8,24},{16,0},{24,8},{1,17},{9,25},{17,1},{25,9},{2,18},{10... | collective-permute-start | bytes 5013512 | tf_op jit(solution)/shard_map/ppermute | solution.py:230
  249.7 20.1 %collective-permute-start.26 = (bf16[2,2,2,2,32,2816]{5,4,1,2,3,0:T(8,128)(2,1)}, bf16[2,2,2,2,32,2816]{5,4,1,2,3,0:T(8,128)(2,1)S(1)}, u32[]{:S(2)}, u32[]{:S(2)}) collective-permute-start(bf16[2,2,2,2,32,2816]{5,4,1,2,3,0:T(8,128)(2,1)} %bitcast.437), channel_id=1, source_target_pairs={{0,8},{8,0},{16,24},{24,16},{1,9},{9,1},{17,25},{25,17},{2,10},{10... | collective-permute-start | bytes 8650760 | tf_op jit(solution)/shard_map/ppermute | solution.py:230
  271.9 51.5 %collective-permute-start.27 = (bf16[2,2,2,1,32,2816]{5,4,0,1,3,2:T(8,128)(2,1)}, bf16[2,2,2,1,32,2816]{5,4,0,1,3,2:T(8,128)(2,1)}, u32[]{:S(2)}, u32[]{:S(2)}) collective-permute-start(bf16[2,2,2,1,32,2816]{5,4,0,1,3,2:T(8,128)(2,1)} %dynamic-slice_bitcast_fusion), channel_id=1, source_target_pairs={{0,16},{8,24},{16,0},{24,8},{1,17},{9,25},{17,1},{25,9},{2,18},{10... | collective-permute-start | bytes 4325384 | tf_op jit(solution)/shard_map/ppermute | solution.py:230
  325.9 22.0 %collective-permute-start.28 = (bf16[2,2,1,32,2816]{4,3,0,2,1:T(8,128)(2,1)S(1)}, bf16[2,2,1,32,2816]{4,3,0,2,1:T(8,128)(2,1)S(1)}, u32[]{:S(2)}, u32[]{:S(2)}) collective-permute-start(bf16[2,2,1,32,2816]{4,3,0,2,1:T(8,128)(2,1)S(1)} %dynamic-slice_bitcast_fusion.3), channel_id=1, source_target_pairs={{0,1},{1,0},{2,3},{3,2},{4,5},{5,4},{6,7},{7,6},{8,9},{9,8},{10,11... | collective-permute-start | bytes 2162696 | tf_op jit(solution)/shard_map/ppermute | solution.py:230
  340.0 42.3 %collective-permute-start.29 = (bf16[2,2,2,2,32,1024]{5,4,1,3,0,2:T(8,128)(2,1)}, bf16[2,2,2,2,32,1024]{5,4,1,3,0,2:T(8,128)(2,1)}, u32[]{:S(2)}, u32[]{:S(2)}) collective-permute-start(bf16[2,2,2,2,32,1024]{5,4,1,3,0,2:T(8,128)(2,1)} %bitcast.442), channel_id=1, source_target_pairs={{0,8},{8,0},{16,24},{24,16},{1,9},{9,1},{17,25},{25,17},{2,10},{10... | collective-permute-start | bytes 3145736 | tf_op jit(solution)/shard_map/ppermute | solution.py:230
  347.4 36.7 %collective-permute-start.30 = (bf16[2,2,2,2,32,1024]{5,4,1,3,0,2:T(8,128)(2,1)}, bf16[2,2,2,2,32,1024]{5,4,1,3,0,2:T(8,128)(2,1)}, u32[]{:S(2)}, u32[]{:S(2)}) collective-permute-start(bf16[2,2,2,2,32,1024]{5,4,1,3,0,2:T(8,128)(2,1)} %bitcast.441), channel_id=1, source_target_pairs={{0,8},{8,0},{16,24},{24,16},{1,9},{9,1},{17,25},{25,17},{2,10},{10... | collective-permute-start | bytes 3145736 | tf_op jit(solution)/shard_map/ppermute | solution.py:230
  349.0 36.9 %collective-permute-start.34 = (bf16[2,1,32,2816]{3,2,1,0:T(8,128)(2,1)S(1)}, bf16[2,1,32,2816]{3,2,1,0:T(8,128)(2,1)}, u32[]{:S(2)}, u32[]{:S(2)}) collective-permute-start(bf16[2,1,32,2816]{3,2,1,0:T(8,128)(2,1)S(1)} %dynamic-slice_bitcast_fusion.7), channel_id=1, source_target_pairs={{0,2},{1,3},{2,0},{3,1},{4,6},{5,7},{6,4},{7,5},{8,10},{9,11},{10,... | collective-permute-start | bytes 1081352 | tf_op jit(solution)/shard_map/ppermute | solution.py:230
  393.1 81.4 %collective-permute-start.45 = (bf16[1,32,2816]{2,1,0:T(8,128)(2,1)}, bf16[1,32,2816]{2,1,0:T(8,128)(2,1)}, u32[]{:S(2)}, u32[]{:S(2)}) collective-permute-start(bf16[1,32,2816]{2,1,0:T(8,128)(2,1)} %dynamic-slice_bitcast_fusion.12), channel_id=1, source_target_pairs={{0,4},{1,5},{2,6},{3,7},{4,0},{5,1},{6,2},{7,3},{8,12},{9,13},{10,... | collective-permute-start | bytes 540680 | tf_op jit(solution)/shard_map/ppermute | solution.py:230
  395.3 45.0 %collective-permute-start.35 = (bf16[2,2,2,5,32,384]{5,4,3,0,2,1:T(8,128)(2,1)}, bf16[2,2,2,5,32,384]{5,4,3,0,2,1:T(8,128)(2,1)}, u32[]{:S(2)}, u32[]{:S(2)}) collective-permute-start(bf16[2,2,2,5,32,384]{5,4,3,0,2,1:T(8,128)(2,1)} %dynamic-slice_bitcast_fusion.2), channel_id=1, source_target_pairs={{0,16},{8,24},{16,0},{24,8},{1,17},{9,25},{17,1},{25,9},{2,18},{10... | collective-permute-start | bytes 2949128 | tf_op jit(solution)/shard_map/ppermute | solution.py:230
  395.3 47.7 %collective-permute-start.38 = (bf16[2,2,2,5,32,384]{5,4,3,1,0,2:T(8,128)(2,1)}, bf16[2,2,2,5,32,384]{5,4,3,1,0,2:T(8,128)(2,1)}, u32[]{:S(2)}, u32[]{:S(2)}) collective-permute-start(bf16[2,2,2,5,32,384]{5,4,3,1,0,2:T(8,128)(2,1)} %dynamic-slice_bitcast_fusion.1), channel_id=1, source_target_pairs={{0,1},{1,0},{2,3},{3,2},{4,5},{5,4},{6,7},{7,6},{8,9},{9,8},{10,11... | collective-permute-start | bytes 2949128 | tf_op jit(solution)/shard_map/ppermute | solution.py:230
  396.6 40.3 %collective-permute-start.41 = (bf16[2,2,2,5,32,256]{5,4,3,1,2,0:T(8,128)(2,1)}, bf16[2,2,2,5,32,256]{5,4,3,1,2,0:T(8,128)(2,1)}, u32[]{:S(2)}, u32[]{:S(2)}) collective-permute-start(bf16[2,2,2,5,32,256]{5,4,3,1,2,0:T(8,128)(2,1)} %dynamic-slice_bitcast_fusion.4), channel_id=1, source_target_pairs={{0,2},{1,3},{2,0},{3,1},{4,6},{5,7},{6,4},{7,5},{8,10},{9,11},{10,... | collective-permute-start | bytes 1966088 | tf_op jit(solution)/shard_map/ppermute | solution.py:230
  (114 other events, 1275.5 us)
Sparse Core Ops, SparseCore 0:
  309.5 178.4 reduce-scatter.1
